TPU v7x, 512 devices: a whole 4x4x16 slice. The times are simulated.
512 devices in a mesh: dp: 4 (over x), cand: 32 (over z, core), tensor: 4 (over y).
Axes of the slice: x: 4, y: 4, z: 16, core: 2. Of those that a mesh axis runs over, the one named last changes fastest.
Arguments:
- context: bfloat16 [8, 4096, 3584], P('dp', 'cand', 'tensor'), may hold values from -12 to 12
- residual: bfloat16 [8, 4096, 3584], P('dp', ('cand', 'tensor')), may hold values from -36 to 36
- out_weight: bfloat16 [3584, 3584], P('cand', 'tensor'), may hold values from -0.09375 to 0.09375
- adapter_down: bfloat16 [3584, 16], P('tensor'), may hold values from -0.09375 to 0.09375
- adapter_up_weight: bfloat16 [16, 3584], replicated, may hold values from -1.5 to 1.5
- norm_gain: float32 [3584], replicated, may hold values from 0.5 to 1.5
- score_weight: float32 [3584], replicated, may hold values from -0.09375 to 0.09375
- teacher: bfloat16 [8, 4096, 4096], P('dp', 'cand', 'tensor'), may hold values from 0.019897461 to 0.9765625
- pair_mask: int32 [8, 4096, 4096], P('dp', 'cand', 'tensor'), may hold values from 0 to 1, as said below
- loss_scale: float32 [8], P('dp'), may hold values from 65536 to 262144
Outputs:
- context_grad: bfloat16 [8, 4096, 3584], P('dp', 'cand', 'tensor')
- residual_gradient: bfloat16 [8, 4096, 3584], P('dp', ('cand', 'tensor'))
- down_grad: float32 [3584, 16], P('tensor')
- up_weight_gradient: float32 [16, 3584], P(None, 'tensor')
- pair_loss: float32 [8], P('dp')
Inputs may be any that keep to these rules, and one draw needn't show every extreme that they name: pair_mask holds 0 or 1; with P = 32, every pair (i, j) whose group j // P lies 4096 / (2P) groups after i // P, counted round over the 4096 / P groups, is valid.
All inputs are finite; a program needn't handle non-finite values.
Results may differ from a plain program's by a relative error of at most 0.02.
Values may be sent and summed in bfloat16 or wider, within the bound.
No kernel may reach another device: no remote copies, remote signals or barrier semaphores. Data moves between devices by JAX's collectives and lax.ppermute only.
A program may use at most 64 MiB of HBM per device.

v0:
```python
import jax
import jax.numpy as jnp
from jax import lax
from jax.sharding import PartitionSpec as P

ADAPTER_SCALE = 0.5
epsilon = 1e-06


def rounded(term):
    return lax.optimization_barrier(term.astype(jnp.bfloat16)).astype(jnp.float32)


def pair_terms(all_scores, own_scores, teacher, valid_pairs, row_start, col_start):
    column_scores = lax.dynamic_slice_in_dim(all_scores, col_start, teacher.shape[2], 1)
    margin = own_scores[:, :, None] - column_scores[:, None, :]
    target = teacher.astype(jnp.float32)
    total = jnp.sum(valid_pairs * (jax.nn.softplus(margin) - target * margin), axis=(1, 2))
    slope = valid_pairs * (jax.nn.sigmoid(margin) - target)
    blank = jnp.zeros(all_scores.shape, jnp.float32)
    row_part = lax.dynamic_update_slice_in_dim(blank, jnp.sum(slope, axis=2), row_start, 1)
    column_part = lax.dynamic_update_slice_in_dim(blank, jnp.sum(slope, axis=1), col_start, 1)
    return (total, row_part - column_part)


def on_device(
    context,
    residual,
    out_weight,
    adapter_down,
    adapter_up_weight,
    norm_gain,
    score_weight,
    teacher,
    pair_mask,
    loss_scale,
):
    cand_rows = context.shape[1]
    tensor_count = lax.axis_size("tensor")
    share = cand_rows // tensor_count
    tensor_index = lax.axis_index("tensor")
    group_index = lax.axis_index("cand")
    valid_pairs = pair_mask.astype(jnp.float32)
    mask_count = jnp.sum(valid_pairs, axis=(1, 2))
    count = lax.psum(mask_count, ("cand", "tensor"))
    low_terms = rounded(
        jnp.einsum("qch,hr->qcr", context, adapter_down, preferred_element_type=jnp.float32)
    )
    full_weight = lax.all_gather(out_weight, "cand", axis=0, tiled=True)
    head_terms = jnp.einsum("qch,dh->qcd", context, full_weight, preferred_element_type=jnp.float32)
    head_terms = rounded(head_terms)
    summed_output, low_sum = (
        lax.psum_scatter(
            head_terms.astype(jnp.bfloat16), "tensor", scatter_dimension=1, tiled=True
        ).astype(jnp.float32),
        lax.psum_scatter(
            low_terms.astype(jnp.bfloat16), "tensor", scatter_dimension=1, tiled=True
        ).astype(jnp.float32),
    )
    adapter_input_rows = low_sum.astype(jnp.bfloat16)
    lifted_rows = jnp.einsum(
        "qcr,rd->qcd", adapter_input_rows, adapter_up_weight, preferred_element_type=jnp.float32
    )
    hidden_state = (
        residual.astype(jnp.float32) + summed_output + ADAPTER_SCALE * lifted_rows
    ).astype(jnp.bfloat16)
    hidden_wide = hidden_state.astype(jnp.float32)
    inv_rms = lax.rsqrt(jnp.mean(hidden_wide * hidden_wide, axis=2, keepdims=True) + epsilon)
    scores = jnp.sum(hidden_wide * inv_rms * norm_gain * score_weight, axis=2)
    all_scores = lax.all_gather(scores, ("cand", "tensor"), axis=1, tiled=True)
    own_start = group_index * cand_rows + tensor_index * share
    row_start = group_index * cand_rows
    col_start = tensor_index * teacher.shape[2]
    own_scores = lax.dynamic_slice_in_dim(all_scores, row_start, cand_rows, 1)
    total, score_vector = pair_terms(
        all_scores, own_scores, teacher, valid_pairs, row_start, col_start
    )
    summed_grad, loss_sum = lax.psum((score_vector, total), ("cand", "tensor"))
    pair_loss = loss_sum / count
    factor = loss_scale / count
    score_grad = lax.dynamic_slice_in_dim(summed_grad, own_start, share, 1) * factor[:, None]
    back_step = score_grad[:, :, None] * norm_gain * score_weight
    grad_hidden = inv_rms * back_step - hidden_wide * inv_rms**3 * jnp.mean(
        hidden_wide * back_step, axis=2, keepdims=True
    )
    grad_rows = grad_hidden.astype(jnp.bfloat16)
    adapter_rows = (
        ADAPTER_SCALE
        * jnp.einsum(
            "qcd,rd->qcr", grad_rows, adapter_up_weight, preferred_element_type=jnp.float32
        )
    ).astype(jnp.bfloat16)
    full_grads, full_adapter = (
        lax.all_gather(grad_rows, "tensor", axis=1, tiled=True),
        lax.all_gather(adapter_rows, "tensor", axis=1, tiled=True),
    )
    up_partial_gradient = ADAPTER_SCALE * jnp.einsum(
        "qcr,qcd->rd", adapter_input_rows, grad_rows, preferred_element_type=jnp.float32
    )
    up_share = lax.psum_scatter(
        up_partial_gradient.astype(jnp.bfloat16), "tensor", scatter_dimension=1, tiled=True
    ).astype(jnp.float32)
    adapter_back = jnp.einsum(
        "qcr,hr->qch", full_adapter, adapter_down, preferred_element_type=jnp.float32
    )
    context_wide = (
        jnp.einsum("qcd,dh->qch", full_grads, full_weight, preferred_element_type=jnp.float32)
        + adapter_back
    )
    context_grad = context_wide.astype(jnp.bfloat16)
    down_local = jnp.einsum(
        "qch,qcr->hr", context, full_adapter, preferred_element_type=jnp.float32
    )
    down_grad, up_weight_gradient = lax.psum((down_local, up_share), ("dp", "cand"))
    return (context_grad, grad_rows, down_grad, up_weight_gradient, pair_loss)


def solution(mesh):
    in_specs = (
        P("dp", "cand", "tensor"),
        P("dp", ("cand", "tensor"), None),
        P("cand", "tensor"),
        P("tensor", None),
        P(),
        P(),
        P(),
        P("dp", "cand", "tensor"),
        P("dp", "cand", "tensor"),
        P("dp"),
    )
    out_specs = (
        P("dp", "cand", "tensor"),
        P("dp", ("cand", "tensor"), None),
        P("tensor", None),
        P(None, "tensor"),
        P("dp"),
    )
    return jax.shard_map(
        on_device, mesh=mesh, in_specs=in_specs, out_specs=out_specs, check_vma=False
    )
```

profile of v0, /device:TPU:1, one launch (start us, length us, event | category | flops | bytes accessed | tf_op | source)
XLA Modules:
  0.0 1306.9 jit_solution(4041656282521602248)
XLA Ops:
  8.0 0.0 copy-start
  8.0 0.0 all-gather.4.cloned.1.call-start
  8.1 0.7 all-gather.4.cloned.1.call-update
  8.7 0.0 reduce-scatter.10.cloned.1.call-start
  8.8 0.2 copy-done
  9.0 0.9 convolution_convert_fusion
  10.0 0.2 copy.20
  10.2 0.7 reshape.41
  10.9 0.0 reduce-scatter.10.cloned.1.call-update
  10.9 0.0 copy-start.4
  10.9 0.0 copy-start.5
  10.9 0.0 copy-start.6
  10.9 0.0 copy-start.7
  10.9 0.0 copy-start.2
  11.0 0.0 copy-start.3
  11.0 0.0 reduce-scatter.8.cloned.1.call-start
  11.0 83.0 %all-gather.4.cloned.1.call-done = bf16[3584,896]{1,0:T(8,128)(2,1)} async-done(((bf16[112,896]{1,0:T(8,128)(2,1)}), bf16[3584,896]{1,0:T(8,128)(2,1)}) %all-gather.4.cloned.1.call-update) | async-done | bytes 6422544 | tf_op jit(solution)/shard_map/all_gather | solution.py:49
  94.0 6.2 fusion.4
  100.1 0.0 reduce-scatter.8.cloned.1.call-update
  100.2 0.0 reduce-scatter.12.cloned.1.call-start
  100.2 0.0 reduce-scatter.10.cloned.1.call-done
  100.3 0.8 reshape.42
  101.0 0.7 copy.21
  101.7 30.3 %reduce-scatter.8.cloned.1.call-done = bf16[2,32,3584]{2,1,0:T(8,128)(2,1)} async-done(((bf16[2,128,3584]{2,1,0:T(8,128)(2,1)}), bf16[2,32,3584]{2,1,0:T(8,128)(2,1)}) %reduce-scatter.8.cloned.1.call-update) | async-done | bytes 458768 | tf_op jit(solution)/shard_map/reduce_scatter | solution.py:53
  132.0 0.0 copy-done.4
  132.0 0.0 copy-done.5
  132.0 1.5 multiply_reduce_fusion.2
  133.5 0.0 copy-start.9
  133.5 0.0 copy-done.6
  133.5 0.0 copy-done.7
  133.5 0.3 multiply_reduce_fusion.1
  133.8 139.8 %all-gather = f32[128,32,2]{1,2,0:T(2,128)S(1)} all-gather(f32[1,32,2]{1,2,0:T(2,128)S(1)} %bitcast.57), channel_id=1, replica_groups=mesh['dp'=4,'cand'=32,'tensor'=4] {'cand','tensor'}, dimensions={0}, use_global_device_ids=true | all-gather | bytes 33024 | tf_op jit(solution)/shard_map/all_gather | solution.py:70
  273.6 0.1 reshape.35
  273.7 0.0 copy-done.2
  273.7 0.0 copy-done.3
  273.7 1.2 fusion.24
  275.0 0.2 fusion.31
  275.2 491.3 %all-reduce = (f32[2,4096]{1,0:T(2,128)S(1)}, f32[2]{0:T(128)S(1)}, f32[2]{0:T(128)S(1)}) all-reduce(f32[2,4096]{1,0:T(2,128)S(1)} %sub.29, f32[2]{0:T(128)S(1)} %get-tuple-element.6, f32[2]{0:T(128)S(1)} %get-tuple-element.5), channel_id=1, replica_groups=mesh['dp'=4,'cand'=32,'tensor'=4] {'cand','tensor'}, use_global_device_ids=true, to_apply=%region_6.7 | all-reduce | flops 8196 | bytes 65568 | tf_op jit(solution)/shard_map/psum | solution.py:78
  766.5 1.2 fusion.32
  767.7 0.1 fusion.30
  767.8 0.3 multiply_reduce_fusion
  768.1 0.3 subtract_convert_fusion
  768.4 0.0 copy-start.1
  768.4 0.0 copy-done.9
  768.4 0.2 fusion.11
  768.6 1.3 copy.22
  769.9 0.0 reduce-scatter.12.cloned.1.call-update
  769.9 0.0 all-gather.6.cloned.1.call-start
  770.0 0.0 copy-done.1
  770.0 0.7 all-gather.6.cloned.1.call-update
  770.7 1.4 fusion.13
  772.1 0.1 copy.17
  772.2 9.0 all_gather.15
  781.2 0.1 copy.18
  781.3 0.2 convolution_bitcast_fusion.1
  781.5 18.8 %reduce-scatter.12.cloned.1.call-done = bf16[896,16]{1,0:T(8,128)(2,1)} async-done(((bf16[3584,16]{1,0:T(8,128)(2,1)}), bf16[896,16]{1,0:T(8,128)(2,1)}) %reduce-scatter.12.cloned.1.call-update) | async-done | bytes 28688
  800.2 1.0 copy.23
  801.3 491.4 %all-reduce.3 = (f32[896,16]{0,1:T(8,128)}, f32[16,896]{1,0:T(8,128)}) all-reduce(f32[896,16]{0,1:T(8,128)S(1)} %convolution_bitcast_fusion.1, bf16[16,896]{1,0:T(8,128)(2,1)S(1)} %copy.23), channel_id=1, replica_groups=mesh['dp'=4,'cand'=32,'tensor'=4] {'dp','cand'}, use_global_device_ids=true, to_apply=%region_10.11 | all-reduce | flops 28672 | bytes 200704 | tf_op jit(solution)/shard_map/psum | solution.py:114
  1292.7 0.0 copy-start.8
  1292.7 0.0 all-gather.6.cloned.1.call-done
  1292.7 5.5 fusion
  1298.2 0.0 copy-done.8
  1298.2 1.1 fusion.12
  (10 shorter events, 0.1 us)
Async XLA Ops:
  8.0 1.0 copy-start
  8.0 86.0 %all-gather.4.cloned.1.call-start = ((), (), s32[]{:S(2)}) async-start(), calls=%async_computation.3 | async-start | bytes 6623232 | tf_op jit(solution)/shard_map/all_gather | solution.py:49
  8.7 91.5 %reduce-scatter.10.cloned.1.call-start = ((), (), s32[]{:S(2)}) async-start(), calls=%async_computation.6 | async-start | bytes 40960
  10.9 121.1 %copy-start.4 = (bf16[2,32,3584]{2,1,0:T(8,128)(2,1)S(1)}, bf16[2,32,3584]{2,1,0:T(8,128)(2,1)}, u32[]{:S(2)}) copy-start(bf16[2,32,3584]{2,1,0:T(8,128)(2,1)} %param.11) | copy-start | bytes 1376260
  10.9 121.1 %copy-start.5 = (bf16[16,3584]{1,0:T(8,128)(2,1)S(1)}, bf16[16,3584]{1,0:T(8,128)(2,1)}, u32[]{:S(2)}) copy-start(bf16[16,3584]{1,0:T(8,128)(2,1)} %param.14) | copy-start | bytes 344068
  10.9 122.6 %copy-start.6 = (f32[3584]{0:T(1024)S(1)}, f32[3584]{0:T(1024)}, u32[]{:S(2)}) copy-start(f32[3584]{0:T(1024)} %param.16) | copy-start | bytes 43012
  10.9 122.6 %copy-start.7 = (f32[3584]{0:T(1024)S(1)}, f32[3584]{0:T(1024)}, u32[]{:S(2)}) copy-start(f32[3584]{0:T(1024)} %param.15) | copy-start | bytes 43012
  10.9 262.8 %copy-start.2 = (s32[2,128,1024]{2,1,0:T(8,128)S(1)}, s32[2,128,1024]{2,1,0:T(8,128)}, u32[]{:S(2)}) copy-start(s32[2,128,1024]{2,1,0:T(8,128)} %param.18) | copy-start | bytes 3145732
  11.0 262.8 %copy-start.3 = (bf16[2,128,1024]{2,1,0:T(8,128)(2,1)S(1)}, bf16[2,128,1024]{2,1,0:T(8,128)(2,1)}, u32[]{:S(2)}) copy-start(bf16[2,128,1024]{2,1,0:T(8,128)(2,1)} %param.17) | copy-start | bytes 1572868
  11.0 121.0 %reduce-scatter.8.cloned.1.call-start = ((), (), s32[]{:S(2)}) async-start(), calls=%async_computation.4 | async-start | bytes 2293760 | tf_op jit(solution)/shard_map/reduce_scatter | solution.py:53
  100.2 700.1 %reduce-scatter.12.cloned.1.call-start = ((), (), s32[]{:S(2)}) async-start(), calls=%async_computation.7 | async-start | bytes 1146880
  133.5 634.9 %copy-start.9 = (bf16[2,32,16]{1,2,0:T(8,128)(2,1)S(1)}, bf16[2,32,16]{1,2,0:T(8,128)(2,1)}, u32[]{:S(2)}) copy-start(bf16[2,32,16]{1,2,0:T(8,128)(2,1)} %copy.21) | copy-start | bytes 6148
  768.4 1.7 copy-start.1
  769.9 522.8 %all-gather.6.cloned.1.call-start = ((), (), s32[]{:S(2)}) async-start(), calls=%async_computation.5 | async-start | bytes 2293760 | tf_op jit(solution)/shard_map/all_gather | solution.py:94
  1292.7 5.5 copy-start.8
Sparse Core Ops, SparseCore 0:
  11.2 82.7 all-gather.3
Sparse Core Ops, SparseCore 1:
  12.6 31.5 reduce-scatter.9
  100.3 31.7 reduce-scatter.7
  770.0 30.2 reduce-scatter.11
  803.1 37.2 all-gather.5
where the time goes:
time: 1310 us
  blocking collectives  1130 us (86%)
  waiting for transfers between devices  133 us (10%)
  matrix products  16.9 us (1%)
  between operations  15.9 us (1%)
    psum x1, blocking collectives, on_device(): lax.psum((down_local, up_share), ('dp', 'cand'))  491 us
    psum x1, blocking collectives, on_device(): summed_grad, loss_sum = lax.psum((score_vector, total), ('cand', 'tensor'))  491 us
    all_gather x1, blocking collectives, on_device(): all_scores = lax.all_gather(scores, ('cand', 'tensor'), axis=1, tiled=True)  140 us
    all_gather x1, waiting for transfers between devices, on_device(): full_weight = lax.all_gather(out_weight, 'cand', axis=0, tiled=True)  83 us
    reduce_scatter x1, waiting for transfers between devices, on_device(): lax.psum_scatter(head_terms.astype(jnp.bfloat16), 'tensor', scatter_dimen...  30.3 us
  transfers between devices with their start and end apart: 5, of which 3 were waited for; matrix products, arithmetic and copies ran while one was open for 1% of the time, Pallas kernels for 0%

commit v1 on v0

v1 whole, which is shorter than its diff:
```python
import jax
import jax.numpy as jnp
from jax import lax
from jax.sharding import PartitionSpec as P

ADAPTER_SCALE = 0.5
epsilon = 1e-06
F32 = jnp.float32
BF16 = jnp.bfloat16


def on_device(
    context,
    residual,
    out_weight,
    adapter_down,
    adapter_up_weight,
    norm_gain,
    score_weight,
    teacher,
    pair_mask,
    loss_scale,
):
    queries, cand_rows, _ = context.shape
    width = residual.shape[2]
    cols = teacher.shape[2]
    tensor_count = lax.axis_size("tensor")
    cand_count = lax.axis_size("cand")
    share = cand_rows // tensor_count
    near = cols // cand_rows
    tensor_index = lax.axis_index("tensor")
    dp_index = lax.axis_index("dp")

    full_weight = lax.all_gather(out_weight, "cand", axis=0, tiled=True)

    low_terms = jnp.einsum(
        "qch,hr->qcr", context, adapter_down, preferred_element_type=F32
    ).astype(BF16)
    low_all = lax.all_gather(low_terms, "tensor", axis=0)
    adapter_in = jnp.sum(low_all.astype(F32), axis=0).astype(BF16)
    adapter_own = lax.dynamic_slice_in_dim(adapter_in, tensor_index * share, share, 1)
    lifted = jnp.einsum("qcr,rd->qcd", adapter_own, adapter_up_weight, preferred_element_type=F32)
    base = residual.astype(F32) + ADAPTER_SCALE * lifted

    valid = pair_mask.astype(F32)
    target = teacher.astype(F32)
    mask_count = jnp.sum(valid, axis=(1, 2))
    row_known = jnp.sum(valid * target, axis=2)
    col_known = jnp.sum(valid * (1.0 - target), axis=1)
    groups = [[a * near + b for b in range(near)] for a in range(cand_count // near)]
    swap = [
        ((a * near + b) * tensor_count + t, (t * near + b) * tensor_count + a)
        for a in range(cand_count // near)
        for b in range(near)
        for t in range(tensor_count)
    ]
    blocks = jnp.swapaxes(
        pair_mask.astype(BF16).reshape(queries, cand_rows, near, cand_rows), 1, 2
    )
    blocks = jnp.swapaxes(blocks, 2, 3)
    blocks = jnp.swapaxes(blocks, 0, 1)
    blocks = lax.all_to_all(
        blocks, "cand", 0, 0, axis_index_groups=groups, tiled=True
    )
    blocks = lax.ppermute(blocks, ("cand", "tensor"), swap)
    other_valid = jnp.moveaxis(blocks, 0, 2).reshape(queries, cand_rows, cols)
    col_known = jnp.swapaxes(col_known.reshape(queries, near, cand_rows), 0, 1)
    col_known = lax.all_to_all(
        col_known, "cand", 0, 0, axis_index_groups=groups, tiled=True
    )
    col_known = lax.ppermute(jnp.sum(col_known, axis=0), ("cand", "tensor"), swap)
    both = valid + other_valid.astype(F32)
    known = row_known + col_known

    full_weight, adapter_in, base, both, known, mask_count = lax.optimization_barrier(
        (full_weight, adapter_in, base, both, known, mask_count)
    )

    by_owner = jnp.swapaxes(
        context.reshape(queries, tensor_count, share, context.shape[2]), 0, 1
    )
    head_terms = jnp.einsum(
        "tqch,dh->tqcd", by_owner, full_weight, preferred_element_type=F32
    ).astype(BF16)
    head_terms = lax.all_to_all(head_terms, "tensor", 0, 0, tiled=True)
    hidden = (base + jnp.sum(head_terms.astype(F32), axis=0)).astype(BF16).astype(F32)
    inv_rms = lax.rsqrt(jnp.mean(hidden * hidden, axis=2) + epsilon)
    gain = norm_gain * score_weight
    dot = jnp.sum(hidden * gain, axis=2)
    scores = dot * inv_rms
    slant = inv_rms * inv_rms * dot / width
    unit = inv_rms[:, :, None] * (gain - hidden * slant[:, :, None])

    unit_sent, unit, scores = lax.optimization_barrier((unit.astype(BF16), unit, scores))
    unit_all = lax.all_gather(unit_sent, "tensor", axis=1, tiled=True)
    message = jnp.concatenate([scores, mask_count[:, None]], axis=1)
    message = lax.all_gather(message, "tensor", axis=0)
    own_scores = jnp.swapaxes(message[:, :, :share], 0, 1).reshape(queries, cand_rows)
    message = jnp.concatenate([own_scores, jnp.sum(message[:, :, share], axis=0)[:, None]], axis=1)
    message = lax.all_gather(message, "cand", axis=0)
    count = jnp.sum(message[:, :, cand_rows], axis=0)
    col_scores = lax.dynamic_slice_in_dim(message, tensor_index * near, near, 0)
    col_scores = jnp.swapaxes(col_scores[:, :, :cand_rows], 0, 1).reshape(queries, cols)

    margin = own_scores[:, :, None] - col_scores[:, None, :]
    raw = jnp.sum(both * jax.nn.sigmoid(margin), axis=2) - known
    total = jnp.sum(valid * (jax.nn.softplus(margin) - target * margin), axis=(1, 2))
    sums = lax.psum(jnp.concatenate([raw, total[:, None]], axis=1), "tensor")
    score_grad = sums[:, :cand_rows] * (loss_scale / count)[:, None]

    own_grad = lax.dynamic_slice_in_dim(score_grad, tensor_index * share, share, 1)
    grad_rows = (own_grad[:, :, None] * unit).astype(BF16)

    adapter_unit = ADAPTER_SCALE * jnp.einsum(
        "qcd,rd->qcr", unit_all, adapter_up_weight, preferred_element_type=F32
    )
    context_unit = jnp.einsum(
        "qcd,dh->qch", unit_all, full_weight, preferred_element_type=F32
    ) + jnp.einsum("qcr,hr->qch", adapter_unit.astype(BF16), adapter_down, preferred_element_type=F32)
    context_grad = (score_grad[:, :, None] * context_unit).astype(BF16)
    adapter_back = (score_grad[:, :, None] * adapter_unit).astype(BF16)
    down_local = jnp.einsum("qcr,qch->rh", adapter_back, context, preferred_element_type=F32)
    block = lax.dynamic_slice_in_dim(
        unit_all, tensor_index * context.shape[2], context.shape[2], 2
    )
    block = (score_grad[:, :, None] * block.astype(F32)).astype(BF16)
    up_local = ADAPTER_SCALE * jnp.einsum(
        "qcr,qcd->rd", adapter_in, block, preferred_element_type=F32
    )

    slots = jnp.zeros((128,), F32)
    slots = lax.dynamic_update_slice_in_dim(slots, sums[:, cand_rows], dp_index * queries, 0)
    flat = jnp.concatenate([down_local, up_local], axis=0)
    columns = flat.shape[1]
    flat = jnp.concatenate([flat, jnp.broadcast_to(slots, (flat.shape[0], 128))], axis=1)
    pieces = lax.all_to_all(flat, "cand", 0, 0, tiled=True)
    piece = jnp.sum(pieces.reshape(cand_count, -1, flat.shape[1]), axis=0)
    piece = lax.psum(piece, "dp")
    flat = lax.all_gather(piece[:, :columns], "cand", axis=0, tiled=True)
    rank = adapter_down.shape[1]
    down_grad = flat[:rank].T
    up_weight_gradient = flat[rank:]
    loss_sum = lax.dynamic_slice_in_dim(piece[0, columns:], dp_index * queries, queries, 0)
    pair_loss = loss_sum / count
    return (context_grad, grad_rows, down_grad, up_weight_gradient, pair_loss)


def solution(mesh):
    in_specs = (
        P("dp", "cand", "tensor"),
        P("dp", ("cand", "tensor"), None),
        P("cand", "tensor"),
        P("tensor", None),
        P(),
        P(),
        P(),
        P("dp", "cand", "tensor"),
        P("dp", "cand", "tensor"),
        P("dp"),
    )
    out_specs = (
        P("dp", "cand", "tensor"),
        P("dp", ("cand", "tensor"), None),
        P("tensor", None),
        P(None, "tensor"),
        P("dp"),
    )
    return jax.shard_map(
        on_device, mesh=mesh, in_specs=in_specs, out_specs=out_specs, check_vma=False
    )
```

time: 1310 us -> 318 us (0.24)
  blocking collectives: 1130 us -> 204 us
  waiting for transfers between devices: 133 us -> 44.7 us
  starting transfers between devices: 0.21 us -> 22.4 us
    psum x2, blocking collectives: 983 us -> 15 us  [the longest x1 8.39 us: on_device(): piece = lax.psum(piece, 'dp')]
    all_gather x1, waiting for transfers between devices: 83 us -> 11.5 us  [on_device(): full_weight = lax.all_gather(out_weight, 'cand', axis=0, tiled=True)]
    all_to_all x0 -> x3, waiting for transfers between devices: none -> 32.5 us  [the longest x1 22.3 us: on_device(): head_terms = lax.all_to_all(head_terms, 'tensor', 0, 0, tiled=True)]
    reduce_scatter x1 -> x0, waiting for transfers between devices: 30.3 us -> none  [on_device(): lax.psum_scatter(head_terms.astype(jnp.bfloat16), 'tensor', scatter_dimen...]
    all_to_all x0 -> x1, blocking collectives: none -> 23.6 us  [on_device(): lax.all_to_all(blocks, 'cand', 0, 0, axis_index_groups=groups, tiled=True)]
    all_to_all x0 -> x3, starting transfers between devices: none -> 20 us  [the longest x1 9 us: on_device(): pieces = lax.all_to_all(flat, 'cand', 0, 0, tiled=True)]
    unnamed x7 -> x2, waiting for transfers between devices: 20.2 us -> 0.7 us
    all_gather x2 -> x4, blocking collectives: 149 us -> 166 us  [the longest x1 94.4 us: on_device(): low_all = lax.all_gather(low_terms, 'tensor', axis=0)]
  transfers between devices with their start and end apart: 5 -> 7, of which waited for: 3 -> 3; matrix products, arithmetic and copies ran while one was open for 1% -> 6% of each run, Pallas kernels for 0% -> 0%
where the time goes in v1:
time: 318 us; the launch traced here: 317 us
  blocking collectives  204 us (64%)
  waiting for transfers between devices  44.7 us (14%)
  starting transfers between devices  22.4 us (7%)
  matrix products  16.3 us (5%)
  between operations  14.2 us (4%)
  other arithmetic  9.15 us (3%)
  local copies, waits for them, and re-layouts  6.21 us (2%)
    all_gather x1, blocking collectives, on_device(): low_all = lax.all_gather(low_terms, 'tensor', axis=0)  94.4 us
    all_gather x1, blocking collectives, on_device(): message = lax.all_gather(message, 'cand', axis=0)  34.2 us
    all_gather x1, blocking collectives, on_device(): flat = lax.all_gather(piece[:, :columns], 'cand', axis=0, tiled=True)  30.8 us
    all_to_all x1, blocking collectives, on_device(): lax.all_to_all(blocks, 'cand', 0, 0, axis_index_groups=groups, tiled=True)  23.6 us
    all_to_all x1, waiting for transfers between devices, on_device(): head_terms = lax.all_to_all(head_terms, 'tensor', 0, 0, tiled=True)  22.3 us
    all_gather x1, waiting for transfers between devices, on_device(): full_weight = lax.all_gather(out_weight, 'cand', axis=0, tiled=True)  11.5 us
    all_to_all x1, waiting for transfers between devices, on_device(): pieces = lax.all_to_all(flat, 'cand', 0, 0, tiled=True)  10.2 us
    all_to_all x1, starting transfers between devices, on_device(): pieces = lax.all_to_all(flat, 'cand', 0, 0, tiled=True)  9 us
  transfers between devices with their start and end apart: 7, of which 3 were waited for; matrix products, arithmetic and copies ran while one was open for 6% of the time, Pallas kernels for 0%

profile of v1, /device:TPU:1, one launch (start us, length us, event | category | flops | bytes accessed | tf_op | source)
XLA Modules:
  0.0 317.1 jit_solution(14492580790109656171)
XLA Ops:
  7.2 0.0 copy-start
  7.2 0.0 all-gather.9.cloned.1.call-start
  7.2 0.7 all-gather.9.cloned.1.call-update
  7.9 1.5 copy.36
  9.5 0.1 convert_element_type.65
  9.6 0.0 copy-start.6
  9.6 0.3 copy.38
  9.8 23.6 %all_to_all.24 = bf16[8,2,128,128]{2,3,1,0:T(8,128)(2,1)S(1)} all-to-all(bf16[8,2,128,128]{2,3,1,0:T(8,128)(2,1)S(1)} %copy.38), channel_id=1, replica_groups={{0,4,8,12,16,20,24,28},{32,36,40,44,48,52,56,60},{64,68,72,76,80,84,88,..., dimensions={0} | all-to-all | bytes 1048576 | tf_op jit(solution)/shard_map/all_to_all | solution.py:62
  33.5 0.9 copy.39
  34.3 1.7 collective-permute-start
  36.0 0.3 copy.40
  36.3 0.0 copy-start.4
  36.3 0.0 copy-start.8
  36.3 0.0 copy-start.7
  36.3 0.0 collective-permute-done
  36.3 2.0 fusion.23
  38.3 4.3 %all-to-all-start.1 = ((f32[8,2,128]{2,1,0:T(2,128)}), f32[8,2,128]{2,1,0:T(2,128)S(1)}, u32[]{:S(2)}, u32[]{:S(2)}) async-start(f32[8,2,128]{2,1,0:T(2,128)} %bitcast.8), calls=%async_computation.1 | async-start | bytes 16384 | tf_op jit(solution)/shard_map/all_to_all | solution.py:68
  42.6 0.0 copy-done.8
  42.6 0.2 convolution_convert_fusion
  42.8 94.4 %all-gather = bf16[8,128,16]{1,2,0:T(8,128)(2,1)S(1)} all-gather(bf16[2,128,16]{1,2,0:T(8,128)(2,1)S(1)} %convolution_convert_fusion), channel_id=2, replica_groups=mesh['dp'=4,'cand'=32,'tensor'=4] {'tensor'}, dimensions={0}, use_global_device_ids=true | all-gather | bytes 40960 | tf_op jit(solution)/shard_map/all_gather | solution.py:39
  137.2 0.0 all-to-all-done.1
  137.3 0.7 collective-permute-start.1
  137.9 0.0 copy-done
  137.9 1.3 fusion.10
  139.2 0.0 collective-permute-done.1
  139.2 11.5 %all-gather.9.cloned.1.call-done = bf16[3584,896]{1,0:T(8,128)(2,1)} async-done(((bf16[112,896]{1,0:T(8,128)(2,1)}), bf16[3584,896]{1,0:T(8,128)(2,1)}) %all-gather.9.cloned.1.call-update) | async-done | bytes 6422544 | tf_op jit(solution)/shard_map/all_gather | solution.py:34
  150.8 6.2 %fusion.7 = bf16[4,2,32,3584]{3,2,1,0:T(8,128)(2,1)} fusion(bf16[3584,896]{1,0:T(8,128)(2,1)} %all-gather.9.cloned.1.call-done, bf16[2,4,32,896]{3,2,1,0:T(8,128)(2,1)S(1)} %bitcast.85), kind=kOutput, calls=%fused_computation.5 | convolution fusion | flops 1645084672 | bytes 8716288 | tf_op jit(solution)/shard_map/tqch,dh->tqcd/dot_general | solution.py:82
  156.9 6.8 %all-to-all-start.2 = ((bf16[4,2,32,3584]{3,2,1,0:T(8,128)(2,1)}), bf16[4,2,32,3584]{3,2,1,0:T(8,128)(2,1)S(1)}, u32[]{:S(2)}, u32[]{:S(2)}) async-start(bf16[4,2,32,3584]{3,2,1,0:T(8,128)(2,1)} %fusion.7), calls=%async_computation.2 | async-start | bytes 3670016 | tf_op jit(solution)/shard_map/all_to_all | solution.py:85
  163.7 0.7 mul.141
  164.4 22.3 %all-to-all-done.2 = bf16[4,2,32,3584]{3,2,1,0:T(8,128)(2,1)S(1)} async-done(((bf16[4,2,32,3584]{3,2,1,0:T(8,128)(2,1)}), bf16[4,2,32,3584]{3,2,1,0:T(8,128)(2,1)S(1)}, u32[]{:S(2)}, u32[]{:S(2)}) %all-to-all-start.2) | async-done | bytes 1835040 | tf_op jit(solution)/shard_map/all_to_all | solution.py:85
  186.7 0.3 convert_reduce_fusion
  187.0 0.9 copy-done.2
  187.9 0.3 fusion.36
  188.2 1.3 fusion.39
  189.5 0.0 all-gather.11.cloned.1.call-update
  189.5 0.1 copy.43
  189.6 0.1 maximum_bitcast_fusion.2
  189.7 6.1 %all-gather.3 = f32[4,2,33]{2,1,0:T(2,128)S(1)} all-gather(f32[1,2,33]{2,1,0:T(2,128)S(1)} %maximum_bitcast_fusion.2), channel_id=3, replica_groups=mesh['dp'=4,'cand'=32,'tensor'=4] {'tensor'}, dimensions={0}, use_global_device_ids=true | all-gather | bytes 1320 | tf_op jit(solution)/shard_map/all_gather | solution.py:97
  195.8 0.1 sub.37
  195.9 0.2 slice_reduce_fusion.1
  196.0 0.1 copy.45
  196.2 34.2 %all-gather.4 = f32[32,2,129]{2,1,0:T(2,128)S(1)} all-gather(f32[1,2,129]{2,1,0:T(2,128)S(1)} %maximum_bitcast_fusion.1), channel_id=4, replica_groups=mesh['dp'=4,'cand'=32,'tensor'=4] {'cand'}, dimensions={0}, use_global_device_ids=true | all-gather | bytes 34056 | tf_op jit(solution)/shard_map/all_gather | solution.py:100
  230.4 1.1 fusion.35
  231.5 0.1 copy.47
  231.6 0.1 slice_reduce_fusion
  231.8 6.6 %psum.14 = f32[2,129]{1,0:T(2,128)S(1)} all-reduce(f32[2,129]{1,0:T(2,128)S(1)} %pad_maximum_fusion), channel_id=1, replica_groups=mesh['dp'=4,'cand'=32,'tensor'=4] {'tensor'}, use_global_device_ids=true, to_apply=%region_11.12 | all-reduce | flops 258 | bytes 2064 | tf_op jit(solution)/shard_map/psum | solution.py:108
  238.4 0.1 slice_reduce_fusion.2
  238.5 0.2 dynamic_update_slice.3
  238.7 0.1 broadcast_multiply_fusion
  238.8 0.1 constant_dynamic-slice_fusion.1
  238.9 2.1 multiply_convert_fusion.1
  241.0 2.2 fusion.44
  243.2 0.4 fusion.48
  243.6 0.2 convolution_bitcast_fusion.1
  243.7 0.3 fusion.20
  244.1 0.8 copy.48
  244.8 9.0 %all-to-all-start.3 = ((f32[32,1,1024]{2,1,0:T(1,128)}), f32[32,1,1024]{2,1,0:T(1,128)S(1)}, u32[]{:S(2)}, u32[]{:S(2)}) async-start(f32[32,1,1024]{2,1,0:T(1,128)} %copy.48), calls=%async_computation.3 | async-start | bytes 262144 | tf_op jit(solution)/shard_map/all_to_all | solution.py:136
  253.8 5.7 %fusion.17 = bf16[2,128,896]{2,1,0:T(8,128)(2,1)} fusion(f32[2,128,896]{2,1,0:T(8,128)S(1)} %fusion.48, bf16[2,128,3584]{2,1,0:T(8,128)(2,1)S(1)} %copy-done.3, bf16[3584,896]{1,0:T(8,128)(2,1)} %all-gather.9.cloned.1.call-done, f32[2,128]{1,0:T(2,128)S(1)} %get-tuple-element.31), kind=kOutput, calls=%fused_computation.22 | convolution fusion | flops 1644855296 | bytes 9634816 | tf_op jit(solution)/shard_map/qcd,dh->qch/dot_general | solution.py:117
  259.5 10.2 %all-to-all-done.3 = f32[32,1,1024]{2,1,0:T(1,128)S(1)} async-done(((f32[32,1,1024]{2,1,0:T(1,128)}), f32[32,1,1024]{2,1,0:T(1,128)S(1)}, u32[]{:S(2)}, u32[]{:S(2)}) %all-to-all-start.3) | async-done | bytes 131104 | tf_op jit(solution)/shard_map/all_to_all | solution.py:136
  269.7 0.1 reduce_sum.134
  269.8 8.4 %psum.15 = f32[1,1024]{1,0:T(1,128)S(1)} all-reduce(f32[1,1024]{1,0:T(1,128)S(1)} %bitcast.87), channel_id=1, replica_groups=mesh['dp'=4,'cand'=32,'tensor'=4] {'dp'}, use_global_device_ids=true, to_apply=%region_14.15 | all-reduce | flops 1024 | bytes 8192 | tf_op jit(solution)/shard_map/psum | solution.py:138
  278.2 0.6 fusion.57
  278.8 30.8 %all-gather.5 = f32[32,1,896]{2,1,0:T(1,128)S(1)} all-gather(f32[1,1,896]{2,1,0:T(1,128)S(1)} %slice_bitcast_fusion.1), channel_id=1, replica_groups=mesh['dp'=4,'cand'=32,'tensor'=4] {'cand'}, dimensions={0}, use_global_device_ids=true | all-gather | bytes 118272 | tf_op jit(solution)/shard_map/all_gather | solution.py:139
  309.6 0.6 copy_bitcast_fusion
  (33 shorter events, 0.2 us)
Async XLA Ops:
  7.2 130.8 %copy-start = (bf16[16,3584]{1,0:T(8,128)(2,1)S(1)}, bf16[16,3584]{1,0:T(8,128)(2,1)}, u32[]{:S(2)}) copy-start(bf16[16,3584]{1,0:T(8,128)(2,1)} %param.14) | copy-start | bytes 344068
  7.2 143.6 %all-gather.9.cloned.1.call-start = ((), (), s32[]{:S(2)}) async-start(), calls=%async_computation.4 | async-start | bytes 6623232 | tf_op jit(solution)/shard_map/all_gather | solution.py:34
  9.6 26.5 %copy-start.6 = (bf16[2,128,1024]{2,1,0:T(8,128)(2,1)S(1)}, bf16[2,128,1024]{2,1,0:T(8,128)(2,1)}, u32[]{:S(2)}) copy-start(bf16[2,128,1024]{2,1,0:T(8,128)(2,1)} %param.17) | copy-start | bytes 1572868
  34.3 2.0 collective-permute-start
  36.3 6.3 %copy-start.4 = (bf16[2,128,896]{2,1,0:T(8,128)(2,1)S(1)}, bf16[2,128,896]{2,1,0:T(8,128)(2,1)}, u32[]{:S(2)}) copy-start(bf16[2,128,896]{2,1,0:T(8,128)(2,1)} %param.10) | copy-start | bytes 1376260
  36.3 6.3 %copy-start.8 = (bf16[896,16]{0,1:T(8,128)(2,1)S(1)}, bf16[896,16]{0,1:T(8,128)(2,1)}, u32[]{:S(2)}) copy-start(bf16[896,16]{0,1:T(8,128)(2,1)} %param.13) | copy-start | bytes 86020
  36.3 101.6 %copy-start.7 = (bf16[2,32,3584]{2,1,0:T(8,128)(2,1)S(1)}, bf16[2,32,3584]{2,1,0:T(8,128)(2,1)}, u32[]{:S(2)}) copy-start(bf16[2,32,3584]{2,1,0:T(8,128)(2,1)} %param.11) | copy-start | bytes 1376260
  38.3 98.9 %all-to-all-start.1 = ((f32[8,2,128]{2,1,0:T(2,128)}), f32[8,2,128]{2,1,0:T(2,128)S(1)}, u32[]{:S(2)}, u32[]{:S(2)}) async-start(f32[8,2,128]{2,1,0:T(2,128)} %bitcast.8), calls=%async_computation.1 | async-start | bytes 16384 | tf_op jit(solution)/shard_map/all_to_all | solution.py:68
  137.3 2.0 collective-permute-start.1
  156.9 29.8 %all-to-all-start.2 = ((bf16[4,2,32,3584]{3,2,1,0:T(8,128)(2,1)}), bf16[4,2,32,3584]{3,2,1,0:T(8,128)(2,1)S(1)}, u32[]{:S(2)}, u32[]{:S(2)}) async-start(bf16[4,2,32,3584]{3,2,1,0:T(8,128)(2,1)} %fusion.7), calls=%async_computation.2 | async-start | bytes 3670016 | tf_op jit(solution)/shard_map/all_to_all | solution.py:85
  163.7 77.3 %all-gather.11.cloned.1.call-start = ((), (), s32[]{:S(2)}) async-start(), calls=%async_computation.5 | async-start | bytes 2293760 | tf_op jit(solution)/shard_map/all_gather | solution.py:95
  186.7 1.2 copy-start.2
  187.9 42.5 %copy-start.1 = (f32[2,128,1024]{1,2,0:T(8,128)S(1)}, f32[2,128,1024]{1,2,0:T(8,128)}, u32[]{:S(2)}) copy-start(f32[2,128,1024]{1,2,0:T(8,128)} %get-tuple-element.14) | copy-start | bytes 3145732
  189.5 42.3 %copy-start.10 = (f32[2]{0:T(128)S(1)}, f32[2]{0:T(128)}, u32[]{:S(2)}) copy-start(f32[2]{0:T(128)} %param.19) | copy-start | bytes 28
  231.5 11.7 %copy-start.9 = (bf16[896,16]{0,1:T(8,128)(2,1)S(1)}, bf16[896,16]{0,1:T(8,128)(2,1)}, u32[]{:S(2)}) copy-start(bf16[896,16]{0,1:T(8,128)(2,1)} %param.13) | copy-start | bytes 86020
  238.9 4.7 %copy-start.5 = (bf16[2,128,896]{2,1,0:T(8,128)(2,1)S(1)}, bf16[2,128,896]{2,1,0:T(8,128)(2,1)}, u32[]{:S(2)}) copy-start(bf16[2,128,896]{2,1,0:T(8,128)(2,1)} %param.10) | copy-start | bytes 1376260
  241.0 2.7 copy-start.3
  244.8 24.9 %all-to-all-start.3 = ((f32[32,1,1024]{2,1,0:T(1,128)}), f32[32,1,1024]{2,1,0:T(1,128)S(1)}, u32[]{:S(2)}, u32[]{:S(2)}) async-start(f32[32,1,1024]{2,1,0:T(1,128)} %copy.48), calls=%async_computation.3 | async-start | bytes 262144 | tf_op jit(solution)/shard_map/all_to_all | solution.py:136
Sparse Core Ops, SparseCore 0:
  10.1 140.5 all-gather.8
  189.6 34.0 all-gather.10

commit v2 on v1

--- a/solution.py
+++ b/solution.py
@@ -7,6 +7,11 @@
 epsilon = 1e-06
 F32 = jnp.float32
 BF16 = jnp.bfloat16
+
+
+def gather_copies(x, axis):
+    copies = jnp.broadcast_to(x[None], (lax.axis_size(axis),) + x.shape)
+    return lax.all_to_all(copies, axis, 0, 0, tiled=True)
 
 
 def on_device(
@@ -45,35 +50,9 @@
     valid = pair_mask.astype(F32)
     target = teacher.astype(F32)
     mask_count = jnp.sum(valid, axis=(1, 2))
-    row_known = jnp.sum(valid * target, axis=2)
-    col_known = jnp.sum(valid * (1.0 - target), axis=1)
-    groups = [[a * near + b for b in range(near)] for a in range(cand_count // near)]
-    swap = [
-        ((a * near + b) * tensor_count + t, (t * near + b) * tensor_count + a)
-        for a in range(cand_count // near)
-        for b in range(near)
-        for t in range(tensor_count)
-    ]
-    blocks = jnp.swapaxes(
-        pair_mask.astype(BF16).reshape(queries, cand_rows, near, cand_rows), 1, 2
-    )
-    blocks = jnp.swapaxes(blocks, 2, 3)
-    blocks = jnp.swapaxes(blocks, 0, 1)
-    blocks = lax.all_to_all(
-        blocks, "cand", 0, 0, axis_index_groups=groups, tiled=True
-    )
-    blocks = lax.ppermute(blocks, ("cand", "tensor"), swap)
-    other_valid = jnp.moveaxis(blocks, 0, 2).reshape(queries, cand_rows, cols)
-    col_known = jnp.swapaxes(col_known.reshape(queries, near, cand_rows), 0, 1)
-    col_known = lax.all_to_all(
-        col_known, "cand", 0, 0, axis_index_groups=groups, tiled=True
-    )
-    col_known = lax.ppermute(jnp.sum(col_known, axis=0), ("cand", "tensor"), swap)
-    both = valid + other_valid.astype(F32)
-    known = row_known + col_known
 
-    full_weight, adapter_in, base, both, known, mask_count = lax.optimization_barrier(
-        (full_weight, adapter_in, base, both, known, mask_count)
+    full_weight, adapter_in, base, mask_count = lax.optimization_barrier(
+        (full_weight, adapter_in, base, mask_count)
     )
 
     by_owner = jnp.swapaxes(
@@ -96,15 +75,24 @@
     message = jnp.concatenate([scores, mask_count[:, None]], axis=1)
     message = lax.all_gather(message, "tensor", axis=0)
     own_scores = jnp.swapaxes(message[:, :, :share], 0, 1).reshape(queries, cand_rows)
-    message = jnp.concatenate([own_scores, jnp.sum(message[:, :, share], axis=0)[:, None]], axis=1)
-    message = lax.all_gather(message, "cand", axis=0)
+    message = jnp.concatenate(
+        [own_scores, jnp.broadcast_to(jnp.sum(message[:, :, share], axis=0)[:, None], (queries, 128))],
+        axis=1,
+    )
+    message = gather_copies(message, "cand")
     count = jnp.sum(message[:, :, cand_rows], axis=0)
     col_scores = lax.dynamic_slice_in_dim(message, tensor_index * near, near, 0)
     col_scores = jnp.swapaxes(col_scores[:, :, :cand_rows], 0, 1).reshape(queries, cols)
 
     margin = own_scores[:, :, None] - col_scores[:, None, :]
-    raw = jnp.sum(both * jax.nn.sigmoid(margin), axis=2) - known
+    slope = valid * (jax.nn.sigmoid(margin) - target)
     total = jnp.sum(valid * (jax.nn.softplus(margin) - target * margin), axis=(1, 2))
+    columns = jnp.swapaxes(jnp.sum(slope, axis=1).reshape(queries, near, cand_rows), 0, 1)
+    columns = lax.dynamic_update_slice_in_dim(
+        jnp.zeros((cand_count, queries, cand_rows), F32), columns, tensor_index * near, 0
+    )
+    columns = lax.all_to_all(columns, "cand", 0, 0, tiled=True)
+    raw = jnp.sum(slope, axis=2) - jnp.sum(columns, axis=0)
     sums = lax.psum(jnp.concatenate([raw, total[:, None]], axis=1), "tensor")
     score_grad = sums[:, :cand_rows] * (loss_scale / count)[:, None]
 
@@ -131,16 +119,16 @@
     slots = jnp.zeros((128,), F32)
     slots = lax.dynamic_update_slice_in_dim(slots, sums[:, cand_rows], dp_index * queries, 0)
     flat = jnp.concatenate([down_local, up_local], axis=0)
-    columns = flat.shape[1]
+    wide = flat.shape[1]
     flat = jnp.concatenate([flat, jnp.broadcast_to(slots, (flat.shape[0], 128))], axis=1)
     pieces = lax.all_to_all(flat, "cand", 0, 0, tiled=True)
     piece = jnp.sum(pieces.reshape(cand_count, -1, flat.shape[1]), axis=0)
     piece = lax.psum(piece, "dp")
-    flat = lax.all_gather(piece[:, :columns], "cand", axis=0, tiled=True)
+    flat = gather_copies(piece[:, :wide], "cand").reshape(flat.shape[0], wide)
     rank = adapter_down.shape[1]
     down_grad = flat[:rank].T
     up_weight_gradient = flat[rank:]
-    loss_sum = lax.dynamic_slice_in_dim(piece[0, columns:], dp_index * queries, queries, 0)
+    loss_sum = lax.dynamic_slice_in_dim(piece[0, wide:], dp_index * queries, queries, 0)
     pair_loss = loss_sum / count
     return (context_grad, grad_rows, down_grad, up_weight_gradient, pair_loss)
 

time: 318 us -> 254 us (0.80)
  blocking collectives: 204 us -> 31.7 us
  waiting for transfers between devices: 44.7 us -> 146 us
  starting transfers between devices: 22.4 us -> 33.5 us
    all_gather x1, blocking collectives: 94.4 us -> 10.4 us  [on_device(): low_all = lax.all_gather(low_terms, 'tensor', axis=0)]
    all_gather x2 -> x0, blocking collectives: 65 us -> none  [the longest x1 34.2 us: on_device(): message = lax.all_gather(message, 'cand', axis=0)]
    all_gather x1, waiting for transfers between devices: 11.5 us -> 71.6 us  [on_device(): full_weight = lax.all_gather(out_weight, 'cand', axis=0, tiled=True)]
    all_to_all x1 -> x3, waiting for transfers between devices: 0.01 us -> 39 us  [the longest x2 27 us: gather_copies(): return lax.all_to_all(copies, axis, 0, 0, tiled=True)]
    all_to_all x1 -> x0, blocking collectives: 23.6 us -> none  [on_device(): lax.all_to_all(blocks, 'cand', 0, 0, axis_index_groups=groups, tiled=True)]
    all_to_all x1 -> x3, starting transfers between devices: 4.28 us -> 23 us  [the longest x2 17.9 us: gather_copies(): return lax.all_to_all(copies, axis, 0, 0, tiled=True)]
  transfers between devices with their start and end apart: 7 -> 7, of which waited for: 3 -> 6; matrix products, arithmetic and copies ran while one was open for 6% -> 6% of each run, Pallas kernels for 0% -> 0%
where the time goes in v2:
time: 254 us; the launch traced here: 253 us
  waiting for transfers between devices  146 us (57%)
  starting transfers between devices  33.5 us (13%)
  blocking collectives  31.7 us (12%)
  matrix products  16.4 us (6%)
  between operations  14.2 us (6%)
  other arithmetic  6.54 us (3%)
  local copies, waits for them, and re-layouts  4.9 us (2%)
    all_gather x1, waiting for transfers between devices, on_device(): full_weight = lax.all_gather(out_weight, 'cand', axis=0, tiled=True)  71.6 us
    all_to_all x2, waiting for transfers between devices, gather_copies(): return lax.all_to_all(copies, axis, 0, 0, tiled=True)  27 us
    all_to_all x1, waiting for transfers between devices, on_device(): head_terms = lax.all_to_all(head_terms, 'tensor', 0, 0, tiled=True)  23 us
    all_to_all x2, starting transfers between devices, gather_copies(): return lax.all_to_all(copies, axis, 0, 0, tiled=True)  17.9 us
    all_to_all x1, waiting for transfers between devices, on_device(): columns = lax.all_to_all(columns, 'cand', 0, 0, tiled=True)  12 us
    all_to_all x1, waiting for transfers between devices, on_device(): pieces = lax.all_to_all(flat, 'cand', 0, 0, tiled=True)  11.3 us
    all_gather x1, blocking collectives, on_device(): low_all = lax.all_gather(low_terms, 'tensor', axis=0)  10.4 us
    psum x1, blocking collectives, on_device(): piece = lax.psum(piece, 'dp')  8.41 us
  transfers between devices with their start and end apart: 7, of which 6 were waited for; matrix products, arithmetic and copies ran while one was open for 6% of the time, Pallas kernels for 0%

profile of v2, /device:TPU:1, one launch (start us, length us, event | category | flops | bytes accessed | tf_op | source)
XLA Modules:
  0.0 252.9 jit_solution(18331303863001939634)
XLA Ops:
  7.2 0.0 copy-start
  7.2 0.0 copy-start.3
  7.2 0.0 copy-start.5
  7.2 0.0 all-gather.6.cloned.1.call-start
  7.2 0.7 all-gather.6.cloned.1.call-update
  7.9 1.2 convolution_convert_fusion
  9.1 10.4 %all-gather = bf16[8,128,16]{1,2,0:T(8,128)(2,1)S(1)} all-gather(bf16[2,128,16]{1,2,0:T(8,128)(2,1)S(1)} %convolution_convert_fusion), channel_id=2, replica_groups=mesh['dp'=4,'cand'=32,'tensor'=4] {'tensor'}, dimensions={0}, use_global_device_ids=true | all-gather | bytes 40960 | tf_op jit(solution)/shard_map/all_gather | solution.py:44
  19.6 1.5 convert_reduce_fusion.1
  21.0 0.0 copy-done
  21.0 0.0 copy-done.5
  21.0 0.4 fusion.10
  21.4 71.6 %all-gather.6.cloned.1.call-done = bf16[3584,896]{1,0:T(8,128)(2,1)} async-done(((bf16[112,896]{1,0:T(8,128)(2,1)}), bf16[3584,896]{1,0:T(8,128)(2,1)}) %all-gather.6.cloned.1.call-update) | async-done | bytes 6422544 | tf_op jit(solution)/shard_map/all_gather | solution.py:39
  93.1 0.0 copy-done.3
  93.1 6.2 %fusion.7 = bf16[4,2,32,3584]{3,2,1,0:T(8,128)(2,1)} fusion(bf16[3584,896]{1,0:T(8,128)(2,1)} %all-gather.6.cloned.1.call-done, bf16[2,4,32,896]{3,2,1,0:T(8,128)(2,1)S(1)} %bitcast.67), kind=kOutput, calls=%fused_computation.5 | convolution fusion | flops 1645084672 | bytes 8716288 | tf_op jit(solution)/shard_map/tqch,dh->tqcd/dot_general | solution.py:61
  99.2 4.1 %all-to-all-start = ((bf16[4,2,32,3584]{3,2,1,0:T(8,128)(2,1)}), bf16[4,2,32,3584]{3,2,1,0:T(8,128)(2,1)S(1)}, u32[]{:S(2)}, u32[]{:S(2)}) async-start(bf16[4,2,32,3584]{3,2,1,0:T(8,128)(2,1)} %fusion.7), calls=%async_computation | async-start | bytes 3670016 | tf_op jit(solution)/shard_map/all_to_all | solution.py:64
  103.4 0.0 all-gather.8.cloned.1.call-start
  103.4 0.0 copy-done.7
  103.4 0.0 copy-done.8
  103.4 0.1 copy.42
  103.5 23.0 %all-to-all-done = bf16[4,2,32,3584]{3,2,1,0:T(8,128)(2,1)S(1)} async-done(((bf16[4,2,32,3584]{3,2,1,0:T(8,128)(2,1)}), bf16[4,2,32,3584]{3,2,1,0:T(8,128)(2,1)S(1)}, u32[]{:S(2)}, u32[]{:S(2)}) %all-to-all-start) | async-done | bytes 1835040 | tf_op jit(solution)/shard_map/all_to_all | solution.py:64
  126.4 0.3 convert_reduce_fusion
  126.7 0.3 fusion.25
  127.0 1.0 fusion.28
  128.0 0.1 maximum_bitcast_fusion.1
  128.1 6.1 %all-gather.2 = f32[4,2,33]{2,1,0:T(2,128)S(1)} all-gather(f32[1,2,33]{2,1,0:T(2,128)S(1)} %maximum_bitcast_fusion.1), channel_id=3, replica_groups=mesh['dp'=4,'cand'=32,'tensor'=4] {'tensor'}, dimensions={0}, use_global_device_ids=true | all-gather | bytes 1320 | tf_op jit(solution)/shard_map/all_gather | solution.py:76
  134.2 0.2 slice_reduce_fusion.1
  134.4 0.1 sub.36
  134.5 0.0 all-gather.8.cloned.1.call-update
  134.5 0.1 broadcast_in_dim.19
  134.6 0.7 broadcast_in_dim.20
  135.2 11.0 %all-to-all-start.1 = ((f32[32,2,256]{2,1,0:T(2,128)}), f32[32,2,256]{2,1,0:T(2,128)S(1)}, u32[]{:S(2)}, u32[]{:S(2)}) async-start(f32[32,2,256]{2,1,0:T(2,128)} %broadcast_in_dim.20), calls=%async_computation.1 | async-start | bytes 131072 | tf_op jit(solution)/shard_map/all_to_all | solution.py:14
  146.3 13.1 %all-to-all-done.1 = f32[32,2,256]{2,1,0:T(2,128)S(1)} async-done(((f32[32,2,256]{2,1,0:T(2,128)}), f32[32,2,256]{2,1,0:T(2,128)S(1)}, u32[]{:S(2)}, u32[]{:S(2)}) %all-to-all-start.1) | async-done | bytes 65568 | tf_op jit(solution)/shard_map/all_to_all | solution.py:14
  159.4 0.0 copy-start.9
  159.4 1.2 fusion.14
  160.6 0.2 fusion.48
  160.8 0.6 broadcast_in_dim.21
  161.4 0.6 bitcast_dynamic-update-slice_fusion
  162.0 5.1 %all-to-all-start.2 = ((f32[32,2,128]{2,1,0:T(2,128)}), f32[32,2,128]{2,1,0:T(2,128)S(1)}, u32[]{:S(2)}, u32[]{:S(2)}) async-start(f32[32,2,128]{2,1,0:T(2,128)} %bitcast_dynamic-update-slice_fusion), calls=%async_computation.2 | async-start | bytes 65536 | tf_op jit(solution)/shard_map/all_to_all | solution.py:94
  167.1 0.1 copy.45
  167.2 0.1 slice_reduce_fusion
  167.3 0.0 copy-done.9
  167.3 12.0 %all-to-all-done.2 = f32[32,2,128]{2,1,0:T(2,128)S(1)} async-done(((f32[32,2,128]{2,1,0:T(2,128)}), f32[32,2,128]{2,1,0:T(2,128)S(1)}, u32[]{:S(2)}, u32[]{:S(2)}) %all-to-all-start.2) | async-done | bytes 32800 | tf_op jit(solution)/shard_map/all_to_all | solution.py:94
  179.4 6.8 %psum.14 = f32[2,129]{1,0:T(2,128)S(1)} all-reduce(f32[2,129]{1,0:T(2,128)S(1)} %pad_maximum_fusion.1), channel_id=1, replica_groups=mesh['dp'=4,'cand'=32,'tensor'=4] {'tensor'}, use_global_device_ids=true, to_apply=%region_10.11 | all-reduce | flops 258 | bytes 2064 | tf_op jit(solution)/shard_map/psum | solution.py:96
  186.2 0.1 slice_reduce_fusion.3
  186.3 0.2 dynamic_update_slice.7
  186.6 0.1 broadcast_multiply_fusion
  186.6 0.1 constant_dynamic-slice_fusion.1
  186.7 0.9 multiply_convert_fusion.1
  187.6 2.2 fusion.33
  189.8 0.2 convolution_bitcast_fusion.1
  190.0 0.3 fusion.13
  190.3 0.8 copy.46
  191.1 6.4 %all-to-all-start.3 = ((f32[32,1,1024]{2,1,0:T(1,128)}), f32[32,1,1024]{2,1,0:T(1,128)S(1)}, u32[]{:S(2)}, u32[]{:S(2)}) async-start(f32[32,1,1024]{2,1,0:T(1,128)} %copy.46), calls=%async_computation.3 | async-start | bytes 262144 | tf_op jit(solution)/shard_map/all_to_all | solution.py:124
  197.5 0.0 copy-start.6
  197.5 4.9 %fusion.2 = f32[2,128,896]{2,1,0:T(8,128)S(1)} fusion(bf16[2,128,3584]{2,1,0:T(8,128)(2,1)S(1)} %copy-done.2, bf16[3584,896]{1,0:T(8,128)(2,1)} %all-gather.6.cloned.1.call-done), kind=kOutput, calls=%fused_computation.2 | convolution fusion | flops 1644167168 | bytes 9175040 | tf_op jit(solution)/shard_map/qcd,dh->qch/dot_general | solution.py:105
  202.4 11.3 %all-to-all-done.3 = f32[32,1,1024]{2,1,0:T(1,128)S(1)} async-done(((f32[32,1,1024]{2,1,0:T(1,128)}), f32[32,1,1024]{2,1,0:T(1,128)S(1)}, u32[]{:S(2)}, u32[]{:S(2)}) %all-to-all-start.3) | async-done | bytes 131104 | tf_op jit(solution)/shard_map/all_to_all | solution.py:124
  213.6 0.1 reduce_sum.124
  213.7 8.4 %psum.15 = f32[1,1024]{1,0:T(1,128)S(1)} all-reduce(f32[1,1024]{1,0:T(1,128)S(1)} %bitcast.69), channel_id=1, replica_groups=mesh['dp'=4,'cand'=32,'tensor'=4] {'dp'}, use_global_device_ids=true, to_apply=%region_13.14 | all-reduce | flops 1024 | bytes 8192 | tf_op jit(solution)/shard_map/psum | solution.py:126
  222.2 0.7 broadcast_in_dim.52
  222.9 6.9 %all-to-all-start.4 = ((f32[32,1,896]{2,1,0:T(1,128)}), f32[32,1,896]{2,1,0:T(1,128)S(1)}, u32[]{:S(2)}, u32[]{:S(2)}) async-start(f32[32,1,896]{2,1,0:T(1,128)} %broadcast_in_dim.52), calls=%async_computation.4 | async-start | bytes 229376 | tf_op jit(solution)/shard_map/all_to_all | solution.py:14
  229.8 1.1 fusion.12
  230.9 0.6 fusion.45
  231.4 13.9 %all-to-all-done.4 = f32[32,1,896]{2,1,0:T(1,128)S(1)} async-done(((f32[32,1,896]{2,1,0:T(1,128)}), f32[32,1,896]{2,1,0:T(1,128)S(1)}, u32[]{:S(2)}, u32[]{:S(2)}) %all-to-all-start.4) | async-done | bytes 114720 | tf_op jit(solution)/shard_map/all_to_all | solution.py:14
  245.4 0.6 copy_bitcast_fusion
  (27 shorter events, 0.2 us)
Async XLA Ops:
  7.2 13.9 %copy-start = (bf16[16,3584]{1,0:T(8,128)(2,1)S(1)}, bf16[16,3584]{1,0:T(8,128)(2,1)}, u32[]{:S(2)}) copy-start(bf16[16,3584]{1,0:T(8,128)(2,1)} %param.14) | copy-start | bytes 344068
  7.2 85.9 %copy-start.3 = (bf16[2,128,896]{2,1,0:T(8,128)(2,1)S(1)}, bf16[2,128,896]{2,1,0:T(8,128)(2,1)}, u32[]{:S(2)}) copy-start(bf16[2,128,896]{2,1,0:T(8,128)(2,1)} %param.10) | copy-start | bytes 1376260
  7.2 13.9 %copy-start.5 = (bf16[2,32,3584]{2,1,0:T(8,128)(2,1)S(1)}, bf16[2,32,3584]{2,1,0:T(8,128)(2,1)}, u32[]{:S(2)}) copy-start(bf16[2,32,3584]{2,1,0:T(8,128)(2,1)} %param.11) | copy-start | bytes 1376260
  7.2 85.9 %all-gather.6.cloned.1.call-start = ((), (), s32[]{:S(2)}) async-start(), calls=%async_computation.5 | async-start | bytes 6623232 | tf_op jit(solution)/shard_map/all_gather | solution.py:39
  99.2 4.1 %copy-start.7 = (f32[3584]{0:T(1024)S(1)}, f32[3584]{0:T(1024)}, u32[]{:S(2)}) copy-start(f32[3584]{0:T(1024)} %param.15) | copy-start | bytes 43012
  99.2 4.1 %copy-start.8 = (f32[3584]{0:T(1024)S(1)}, f32[3584]{0:T(1024)}, u32[]{:S(2)}) copy-start(f32[3584]{0:T(1024)} %param.16) | copy-start | bytes 43012
  99.2 27.2 %all-to-all-start = ((bf16[4,2,32,3584]{3,2,1,0:T(8,128)(2,1)}), bf16[4,2,32,3584]{3,2,1,0:T(8,128)(2,1)S(1)}, u32[]{:S(2)}, u32[]{:S(2)}) async-start(bf16[4,2,32,3584]{3,2,1,0:T(8,128)(2,1)} %fusion.7), calls=%async_computation | async-start | bytes 3670016 | tf_op jit(solution)/shard_map/all_to_all | solution.py:64
  103.4 84.2 %all-gather.8.cloned.1.call-start = ((), (), s32[]{:S(2)}) async-start(), calls=%async_computation.6 | async-start | bytes 2293760 | tf_op jit(solution)/shard_map/all_gather | solution.py:74
  127.0 32.3 %copy-start.1 = (s32[2,128,1024]{2,1,0:T(8,128)S(1)}, s32[2,128,1024]{2,1,0:T(8,128)}, u32[]{:S(2)}) copy-start(s32[2,128,1024]{2,1,0:T(8,128)} %param.18) | copy-start | bytes 3145732
  127.0 32.3 %copy-start.4 = (bf16[2,128,1024]{2,1,0:T(8,128)(2,1)S(1)}, bf16[2,128,1024]{2,1,0:T(8,128)(2,1)}, u32[]{:S(2)}) copy-start(bf16[2,128,1024]{2,1,0:T(8,128)(2,1)} %param.17) | copy-start | bytes 1572868
  135.2 24.1 %all-to-all-start.1 = ((f32[32,2,256]{2,1,0:T(2,128)}), f32[32,2,256]{2,1,0:T(2,128)S(1)}, u32[]{:S(2)}, u32[]{:S(2)}) async-start(f32[32,2,256]{2,1,0:T(2,128)} %broadcast_in_dim.20), calls=%async_computation.1 | async-start | bytes 131072 | tf_op jit(solution)/shard_map/all_to_all | solution.py:14
  159.4 7.9 %copy-start.9 = (f32[2]{0:T(128)S(1)}, f32[2]{0:T(128)}, u32[]{:S(2)}) copy-start(f32[2]{0:T(128)} %param.19) | copy-start | bytes 28
  162.0 17.4 %all-to-all-start.2 = ((f32[32,2,128]{2,1,0:T(2,128)}), f32[32,2,128]{2,1,0:T(2,128)S(1)}, u32[]{:S(2)}, u32[]{:S(2)}) async-start(f32[32,2,128]{2,1,0:T(2,128)} %bitcast_dynamic-update-slice_fusion), calls=%async_computation.2 | async-start | bytes 65536 | tf_op jit(solution)/shard_map/all_to_all | solution.py:94
  187.6 2.4 copy-start.2
  191.1 22.5 %all-to-all-start.3 = ((f32[32,1,1024]{2,1,0:T(1,128)}), f32[32,1,1024]{2,1,0:T(1,128)S(1)}, u32[]{:S(2)}, u32[]{:S(2)}) async-start(f32[32,1,1024]{2,1,0:T(1,128)} %copy.46), calls=%async_computation.3 | async-start | bytes 262144 | tf_op jit(solution)/shard_map/all_to_all | solution.py:124
  197.5 32.3 %copy-start.6 = (bf16[896,16]{0,1:T(8,128)(2,1)S(1)}, bf16[896,16]{0,1:T(8,128)(2,1)}, u32[]{:S(2)}) copy-start(bf16[896,16]{0,1:T(8,128)(2,1)} %param.13) | copy-start | bytes 86020
  222.9 22.5 %all-to-all-start.4 = ((f32[32,1,896]{2,1,0:T(1,128)}), f32[32,1,896]{2,1,0:T(1,128)S(1)}, u32[]{:S(2)}, u32[]{:S(2)}) async-start(f32[32,1,896]{2,1,0:T(1,128)} %broadcast_in_dim.52), calls=%async_computation.4 | async-start | bytes 229376 | tf_op jit(solution)/shard_map/all_to_all | solution.py:14
Sparse Core Ops, SparseCore 0:
  10.2 82.8 all-gather.5
  134.6 33.5 all-gather.7

commit v3 on v2

--- a/solution.py
+++ b/solution.py
@@ -35,6 +35,8 @@
     near = cols // cand_rows
     tensor_index = lax.axis_index("tensor")
     dp_index = lax.axis_index("dp")
+    cand_index = lax.axis_index("cand")
+    dp_count = lax.axis_size("dp")
 
     full_weight = lax.all_gather(out_weight, "cand", axis=0, tiled=True)
 
@@ -50,19 +52,28 @@
     valid = pair_mask.astype(F32)
     target = teacher.astype(F32)
     mask_count = jnp.sum(valid, axis=(1, 2))
+    mask_rows = pair_mask.astype(BF16).reshape(queries, tensor_count, share, cols)
+    mask_rows = lax.all_to_all(jnp.swapaxes(mask_rows, 0, 1), "tensor", 0, 0, tiled=True)
+    mask_rows = mask_rows.reshape(tensor_count, queries, share, near, cand_rows)
+    mask_rows = jnp.moveaxis(mask_rows, 3, 1).reshape(cand_count, queries, share, cand_rows)
+    known = jnp.swapaxes(jnp.sum(valid * target, axis=1).reshape(queries, near, cand_rows), 0, 1)
+    known = lax.dynamic_update_slice_in_dim(
+        jnp.zeros((cand_count, queries, cand_rows), F32), known, tensor_index * near, 0
+    )
+    known = jnp.sum(lax.all_to_all(known, "cand", 0, 0, tiled=True), axis=0)
 
-    full_weight, adapter_in, base, mask_count = lax.optimization_barrier(
-        (full_weight, adapter_in, base, mask_count)
+    full_weight, adapter_in, base, mask_count, mask_rows, known = lax.optimization_barrier(
+        (full_weight, adapter_in, base, mask_count, mask_rows, known)
     )
 
-    by_owner = jnp.swapaxes(
-        context.reshape(queries, tensor_count, share, context.shape[2]), 0, 1
-    )
     head_terms = jnp.einsum(
-        "tqch,dh->tqcd", by_owner, full_weight, preferred_element_type=F32
+        "qch,dh->qcd", context, full_weight, preferred_element_type=F32
     ).astype(BF16)
-    head_terms = lax.all_to_all(head_terms, "tensor", 0, 0, tiled=True)
-    hidden = (base + jnp.sum(head_terms.astype(F32), axis=0)).astype(BF16).astype(F32)
+    head_terms, mask_rows = lax.optimization_barrier((head_terms, mask_rows))
+    head_sum = lax.psum_scatter(head_terms, "tensor", scatter_dimension=1, tiled=True)
+    turned = lax.all_to_all(mask_rows, "cand", 0, 0, tiled=True)
+    head_sum, turned = lax.optimization_barrier((head_sum, turned))
+    hidden = (base + head_sum.astype(F32)).astype(BF16).astype(F32)
     inv_rms = lax.rsqrt(jnp.mean(hidden * hidden, axis=2) + epsilon)
     gain = norm_gain * score_weight
     dot = jnp.sum(hidden * gain, axis=2)
@@ -72,27 +83,24 @@
 
     unit_sent, unit, scores = lax.optimization_barrier((unit.astype(BF16), unit, scores))
     unit_all = lax.all_gather(unit_sent, "tensor", axis=1, tiled=True)
-    message = jnp.concatenate([scores, mask_count[:, None]], axis=1)
-    message = lax.all_gather(message, "tensor", axis=0)
-    own_scores = jnp.swapaxes(message[:, :, :share], 0, 1).reshape(queries, cand_rows)
     message = jnp.concatenate(
-        [own_scores, jnp.broadcast_to(jnp.sum(message[:, :, share], axis=0)[:, None], (queries, 128))],
-        axis=1,
+        [scores, jnp.broadcast_to(mask_count[:, None], (queries, 128 - share))], axis=1
     )
-    message = gather_copies(message, "cand")
-    count = jnp.sum(message[:, :, cand_rows], axis=0)
-    col_scores = lax.dynamic_slice_in_dim(message, tensor_index * near, near, 0)
-    col_scores = jnp.swapaxes(col_scores[:, :, :cand_rows], 0, 1).reshape(queries, cols)
+    message = gather_copies(message, ("cand", "tensor"))
+    count = jnp.sum(message[:, :, share], axis=0)
+    message = message[:, :, :share].reshape(cand_count, tensor_count, queries, share)
+    all_scores = jnp.moveaxis(message, 2, 0).reshape(queries, cand_count * cand_rows)
+    own_scores = lax.dynamic_slice_in_dim(all_scores, cand_index * cand_rows, cand_rows, 1)
+    col_scores = lax.dynamic_slice_in_dim(all_scores, tensor_index * cols, cols, 1)
+    turned_scores = lax.dynamic_index_in_dim(message, tensor_index, 1, keepdims=False)
 
     margin = own_scores[:, :, None] - col_scores[:, None, :]
     slope = valid * (jax.nn.sigmoid(margin) - target)
     total = jnp.sum(valid * (jax.nn.softplus(margin) - target * margin), axis=(1, 2))
-    columns = jnp.swapaxes(jnp.sum(slope, axis=1).reshape(queries, near, cand_rows), 0, 1)
-    columns = lax.dynamic_update_slice_in_dim(
-        jnp.zeros((cand_count, queries, cand_rows), F32), columns, tensor_index * near, 0
-    )
-    columns = lax.all_to_all(columns, "cand", 0, 0, tiled=True)
-    raw = jnp.sum(slope, axis=2) - jnp.sum(columns, axis=0)
+    turned_margin = turned_scores[:, :, :, None] - own_scores[None, :, None, :]
+    turned_sum = jnp.sum(turned.astype(F32) * jax.nn.sigmoid(turned_margin), axis=(0, 2))
+    raw = jnp.sum(slope, axis=2) - (turned_sum - known)
+    raw, unit_all = lax.optimization_barrier((raw, unit_all))
     sums = lax.psum(jnp.concatenate([raw, total[:, None]], axis=1), "tensor")
     score_grad = sums[:, :cand_rows] * (loss_scale / count)[:, None]
 
@@ -116,20 +124,25 @@
         "qcr,qcd->rd", adapter_in, block, preferred_element_type=F32
     )
 
-    slots = jnp.zeros((128,), F32)
-    slots = lax.dynamic_update_slice_in_dim(slots, sums[:, cand_rows], dp_index * queries, 0)
+    rank = adapter_down.shape[1]
     flat = jnp.concatenate([down_local, up_local], axis=0)
-    wide = flat.shape[1]
-    flat = jnp.concatenate([flat, jnp.broadcast_to(slots, (flat.shape[0], 128))], axis=1)
-    pieces = lax.all_to_all(flat, "cand", 0, 0, tiled=True)
-    piece = jnp.sum(pieces.reshape(cand_count, -1, flat.shape[1]), axis=0)
-    piece = lax.psum(piece, "dp")
-    flat = gather_copies(piece[:, :wide], "cand").reshape(flat.shape[0], wide)
-    rank = adapter_down.shape[1]
+    slots = jnp.zeros((1, 128), F32)
+    slots = lax.dynamic_update_slice_in_dim(slots, sums[None, :, cand_rows], dp_index * queries, 1)
+    tiles = flat.shape[1] // 128
+    devices = dp_count * cand_count
+    rows = (tiles + 1) * 2 * rank
+    rows += -rows % devices
+    pad = jnp.zeros((rows - 2 * rank * tiles - 1, 128), F32)
+    flat = jnp.swapaxes(flat.reshape(2 * rank, tiles, 128), 0, 1).reshape(-1, 128)
+    flat = jnp.concatenate([flat, slots, pad])
+    pieces = lax.all_to_all(flat.reshape(devices, -1, 128), ("dp", "cand"), 0, 0, tiled=True)
+    flat = gather_copies(jnp.sum(pieces, axis=0), ("dp", "cand")).reshape(rows, 128)
+    loss_sum = lax.dynamic_slice_in_dim(flat[2 * rank * tiles], dp_index * queries, queries, 0)
+    pair_loss = loss_sum / count
+    flat = flat[: 2 * rank * tiles].reshape(tiles, 2 * rank, 128)
+    flat = jnp.swapaxes(flat, 0, 1).reshape(2 * rank, 128 * tiles)
     down_grad = flat[:rank].T
     up_weight_gradient = flat[rank:]
-    loss_sum = lax.dynamic_slice_in_dim(piece[0, wide:], dp_index * queries, queries, 0)
-    pair_loss = loss_sum / count
     return (context_grad, grad_rows, down_grad, up_weight_gradient, pair_loss)
 
 

time: 254 us -> 253 us (level)
  starting transfers between devices: 33.5 us -> 59.2 us
  waiting for transfers between devices: 146 us -> 123 us
  blocking collectives: 31.7 us -> 18.4 us
  other arithmetic: 6.54 us -> 11.2 us
  local copies, waits for them, and re-layouts: 4.9 us -> 8.62 us
    all_gather x1, waiting for transfers between devices: 71.6 us -> 32.8 us  [on_device(): full_weight = lax.all_gather(out_weight, 'cand', axis=0, tiled=True)]
    all_to_all x3 -> x4, starting transfers between devices: 15.6 us -> 45.1 us  [the longest x1 16.7 us: on_device(): known = jnp.sum(lax.all_to_all(known, 'cand', 0, 0, tiled=True), axis=0)]
    all_to_all x3 -> x4, waiting for transfers between devices: 46.2 us -> 61 us  [the longest x1 33.4 us: on_device(): turned = lax.all_to_all(mask_rows, 'cand', 0, 0, tiled=True)]
    psum x1 -> x0, blocking collectives: 8.41 us -> none  [on_device(): piece = lax.psum(piece, 'dp')]
    all_gather x1 -> x0, blocking collectives: 6.1 us -> none  [on_device(): message = lax.all_gather(message, 'tensor', axis=0)]
    all_to_all x2, starting transfers between devices: 17.9 us -> 14 us  [gather_copies(): return lax.all_to_all(copies, axis, 0, 0, tiled=True)]
    reduce_sum x7 -> x6, other arithmetic: 2.36 us -> 5.81 us  [the longest x1 2.2 us: on_device(): jnp.sum(valid * target, axis=1).reshape(queries, near, cand_rows)]
  transfers between devices with their start and end apart: 7 -> 9, of which waited for: 6 -> 6; matrix products, arithmetic and copies ran while one was open for 6% -> 8% of each run, Pallas kernels for 0% -> 0%
where the time goes in v3:
time: 253 us; the launch traced here: 252 us
  waiting for transfers between devices  123 us (49%)
  starting transfers between devices  59.2 us (23%)
  blocking collectives  18.4 us (7%)
  matrix products  17.5 us (7%)
  between operations  14.1 us (6%)
  other arithmetic  11.2 us (4%)
  local copies, waits for them, and re-layouts  8.62 us (3%)
    all_to_all x1, waiting for transfers between devices, on_device(): turned = lax.all_to_all(mask_rows, 'cand', 0, 0, tiled=True)  33.4 us
    all_gather x1, waiting for transfers between devices, on_device(): full_weight = lax.all_gather(out_weight, 'cand', axis=0, tiled=True)  32.8 us
    all_to_all x2, waiting for transfers between devices, gather_copies(): return lax.all_to_all(copies, axis, 0, 0, tiled=True)  28.6 us
    all_to_all x1, starting transfers between devices, on_device(): known = jnp.sum(lax.all_to_all(known, 'cand', 0, 0, tiled=True), axis=0)  16.7 us
    all_to_all x1, waiting for transfers between devices, on_device(): lax.all_to_all(flat.reshape(devices, -1, 128), ('dp', 'cand'), 0, 0, tile...  16.5 us
    all_to_all x1, starting transfers between devices, on_device(): lax.all_to_all(flat.reshape(devices, -1, 128), ('dp', 'cand'), 0, 0, tile...  16.3 us
    all_to_all x2, starting transfers between devices, gather_copies(): return lax.all_to_all(copies, axis, 0, 0, tiled=True)  14 us
    all_gather x1, blocking collectives, on_device(): low_all = lax.all_gather(low_terms, 'tensor', axis=0)  12.3 us
  transfers between devices with their start and end apart: 9, of which 6 were waited for; matrix products, arithmetic and copies ran while one was open for 8% of the time, Pallas kernels for 0%

profile of v3, /device:TPU:1, one launch (start us, length us, event | category | flops | bytes accessed | tf_op | source)
XLA Modules:
  0.0 252.2 jit_solution(5291334645356774703)
XLA Ops:
  7.2 0.0 copy-start
  7.2 0.0 all-gather.4.cloned.1.call-start
  7.2 0.7 all-gather.4.cloned.1.call-update
  7.9 2.2 fusion.14
  10.1 0.6 broadcast_in_dim.14
  10.8 0.6 bitcast_dynamic-update-slice_fusion
  11.4 16.7 %all-to-all-start.1 = ((f32[32,2,128]{2,1,0:T(2,128)}), f32[32,2,128]{2,1,0:T(2,128)S(1)}, u32[]{:S(2)}, u32[]{:S(2)}) async-start(f32[32,2,128]{2,1,0:T(2,128)} %bitcast_dynamic-update-slice_fusion), calls=%async_computation.1 | async-start | bytes 65536 | tf_op jit(solution)/shard_map/all_to_all | solution.py:63
  28.1 0.0 copy-start.4
  28.1 0.0 copy-start.5
  28.2 0.1 convert_element_type.59
  28.2 0.9 copy.83
  29.1 11.1 %all-to-all-done.1 = f32[32,2,128]{2,1,0:T(2,128)S(1)} async-done(((f32[32,2,128]{2,1,0:T(2,128)}), f32[32,2,128]{2,1,0:T(2,128)S(1)}, u32[]{:S(2)}, u32[]{:S(2)}) %all-to-all-start.1) | async-done | bytes 32800 | tf_op jit(solution)/shard_map/all_to_all | solution.py:63
  40.2 4.2 %all-to-all-start = ((bf16[4,2,32,1024]{3,2,1,0:T(8,128)(2,1)}), bf16[4,2,32,1024]{3,2,1,0:T(8,128)(2,1)S(1)}, u32[]{:S(2)}, u32[]{:S(2)}) async-start(bf16[4,2,32,1024]{3,2,1,0:T(8,128)(2,1)} %bitcast.76), calls=%async_computation | async-start | bytes 1048576 | tf_op jit(solution)/shard_map/all_to_all | solution.py:56
  44.4 0.2 convolution_convert_fusion
  44.6 12.3 %all-gather = bf16[8,128,16]{1,2,0:T(8,128)(2,1)S(1)} all-gather(bf16[2,128,16]{1,2,0:T(8,128)(2,1)S(1)} %convolution_convert_fusion), channel_id=2, replica_groups=mesh['dp'=4,'cand'=32,'tensor'=4] {'tensor'}, dimensions={0}, use_global_device_ids=true | all-gather | bytes 40960 | tf_op jit(solution)/shard_map/all_gather | solution.py:46
  56.9 0.6 reduce_sum.102
  57.5 1.1 fusion.10
  58.6 0.6 reduce_sum.105
  59.2 0.1 copy.79
  59.3 1.0 copy.65
  60.2 32.8 %all-gather.4.cloned.1.call-done = bf16[3584,896]{1,0:T(8,128)(2,1)} async-done(((bf16[112,896]{1,0:T(8,128)(2,1)}), bf16[3584,896]{1,0:T(8,128)(2,1)}) %all-gather.4.cloned.1.call-update) | async-done | bytes 6422544 | tf_op jit(solution)/shard_map/all_gather | solution.py:41
  93.0 6.2 %fusion.7 = bf16[2,128,3584]{2,1,0:T(8,128)(2,1)} fusion(bf16[2,128,896]{2,1,0:T(8,128)(2,1)S(1)} %copy-done, bf16[3584,896]{1,0:T(8,128)(2,1)} %all-gather.4.cloned.1.call-done), kind=kOutput, calls=%fused_computation.5 | convolution fusion | flops 1645084672 | bytes 8716288 | tf_op jit(solution)/shard_map/qch,dh->qcd/dot_general | solution.py:69
  99.2 0.0 reduce-scatter.2.cloned.1.call-update
  99.2 7.9 %all-to-all-start.2 = ((bf16[32,2,32,128]{3,2,1,0:T(8,128)(2,1)}), bf16[32,2,32,128]{3,2,1,0:T(8,128)(2,1)S(1)}, u32[]{:S(2)}, u32[]{:S(2)}) async-start(bf16[32,2,32,128]{3,2,1,0:T(8,128)(2,1)} %bitcast.6), calls=%async_computation.3 | async-start | bytes 1048576 | tf_op jit(solution)/shard_map/all_to_all | solution.py:74
  107.2 0.0 all-gather.6.cloned.1.call-start
  107.3 33.4 %all-to-all-done.2 = bf16[32,2,32,128]{3,2,1,0:T(8,128)(2,1)S(1)} async-done(((bf16[32,2,32,128]{3,2,1,0:T(8,128)(2,1)}), bf16[32,2,32,128]{3,2,1,0:T(8,128)(2,1)S(1)}, u32[]{:S(2)}, u32[]{:S(2)}) %all-to-all-start.2) | async-done | bytes 524320 | tf_op jit(solution)/shard_map/all_to_all | solution.py:74
  140.7 1.3 fusion.27
  142.0 1.0 fusion.30
  143.0 0.0 all-gather.6.cloned.1.call-update
  143.0 0.1 broadcast_in_dim.15
  143.1 0.1 pad_maximum_fusion.2
  143.2 0.7 broadcast_in_dim.16
  143.9 6.9 %all-to-all-start.3 = ((f32[128,2,128]{2,1,0:T(2,128)}), f32[128,2,128]{2,1,0:T(2,128)}, u32[]{:S(2)}, u32[]{:S(2)}) async-start(f32[128,2,128]{2,1,0:T(2,128)} %broadcast_in_dim.16), calls=%async_computation.4 | async-start | bytes 262144 | tf_op jit(solution)/shard_map/all_to_all | solution.py:14
  150.8 0.1 pad.2.clone
  150.9 17.7 %all-to-all-done.3 = f32[128,2,128]{2,1,0:T(2,128)} async-done(((f32[128,2,128]{2,1,0:T(2,128)}), f32[128,2,128]{2,1,0:T(2,128)}, u32[]{:S(2)}, u32[]{:S(2)}) %all-to-all-start.3) | async-done | bytes 131104 | tf_op jit(solution)/shard_map/all_to_all | solution.py:14
  168.5 0.9 copy.76
  169.4 0.6 copy-done.3
  170.2 1.0 reshape.78
  171.3 0.0 copy-start.8
  171.3 1.3 fusion.26
  172.5 0.1 copy.70
  172.6 1.2 slice_reduce_fusion
  173.9 0.4 multiply_reduce_fusion
  174.3 0.0 all-gather.6.cloned.1.call-done
  174.3 6.1 %psum.7 = f32[2,129]{1,0:T(2,128)S(1)} all-reduce(f32[2,129]{1,0:T(2,128)S(1)} %pad_maximum_fusion.1), channel_id=1, replica_groups=mesh['dp'=4,'cand'=32,'tensor'=4] {'tensor'}, use_global_device_ids=true, to_apply=%region_10.11 | all-reduce | flops 258 | bytes 2064 | tf_op jit(solution)/shard_map/psum | solution.py:104
  180.5 0.1 slice_reduce_fusion.1
  180.6 0.1 broadcast_multiply_fusion
  180.6 0.1 constant_dynamic-slice_fusion.1
  180.7 2.1 fusion.33
  182.8 1.3 fusion.13
  184.1 0.2 convolution_bitcast_fusion.1
  184.4 0.1 dynamic_update_slice.7
  184.5 0.8 maximum_maximum_fusion
  185.3 16.3 %all-to-all-start.4 = ((f32[128,2,128]{2,1,0:T(2,128)}), f32[128,2,128]{2,1,0:T(2,128)S(1)}, u32[]{:S(2)}, u32[]{:S(2)}) async-start(f32[128,2,128]{2,1,0:T(2,128)} %bitcast.19), calls=%async_computation.5 | async-start | bytes 262144 | tf_op jit(solution)/shard_map/all_to_all | solution.py:138
  201.6 0.9 multiply_convert_fusion.1
  202.5 16.5 %all-to-all-done.4 = f32[128,2,128]{2,1,0:T(2,128)S(1)} async-done(((f32[128,2,128]{2,1,0:T(2,128)}), f32[128,2,128]{2,1,0:T(2,128)S(1)}, u32[]{:S(2)}, u32[]{:S(2)}) %all-to-all-start.4) | async-done | bytes 131104 | tf_op jit(solution)/shard_map/all_to_all | solution.py:138
  219.0 0.1 reduce_sum.112
  219.1 0.7 broadcast_in_dim.20
  219.8 7.1 %all-to-all-start.5 = ((f32[128,2,128]{2,1,0:T(2,128)}), f32[128,2,128]{2,1,0:T(2,128)S(1)}, u32[]{:S(2)}, u32[]{:S(2)}) async-start(f32[128,2,128]{2,1,0:T(2,128)} %broadcast_in_dim.20), calls=%async_computation.6 | async-start | bytes 262144 | tf_op jit(solution)/shard_map/all_to_all | solution.py:14
  226.9 5.5 %fusion = f32[2,128,896]{2,1,0:T(8,128)S(1)} fusion(bf16[2,128,3584]{2,1,0:T(8,128)(2,1)} %all-gather.6.cloned.1.call-done, bf16[3584,896]{1,0:T(8,128)(2,1)} %all-gather.4.cloned.1.call-done), kind=kOutput, calls=%fused_computation | convolution fusion | flops 1644167168 | bytes 9175040 | tf_op jit(solution)/shard_map/qcd,dh->qch/dot_general | solution.py:113
  232.4 1.1 fusion.12
  233.5 10.9 %all-to-all-done.5 = f32[128,2,128]{2,1,0:T(2,128)S(1)} async-done(((f32[128,2,128]{2,1,0:T(2,128)}), f32[128,2,128]{2,1,0:T(2,128)S(1)}, u32[]{:S(2)}, u32[]{:S(2)}) %all-to-all-start.5) | async-done | bytes 131104 | tf_op jit(solution)/shard_map/all_to_all | solution.py:14
  244.4 0.6 fusion.45
  245.0 0.6 copy_bitcast_fusion.1
  (43 shorter events, 0.3 us)
Async XLA Ops:
  7.2 37.3 %copy-start = (bf16[2,128,896]{2,1,0:T(8,128)(2,1)S(1)}, bf16[2,128,896]{2,1,0:T(8,128)(2,1)}, u32[]{:S(2)}) copy-start(bf16[2,128,896]{2,1,0:T(8,128)(2,1)} %param.10) | copy-start | bytes 1376260
  7.2 20.9 %copy-start.1 = (s32[2,128,1024]{2,1,0:T(8,128)S(1)}, s32[2,128,1024]{2,1,0:T(8,128)}, u32[]{:S(2)}) copy-start(s32[2,128,1024]{2,1,0:T(8,128)} %param.18) | copy-start | bytes 3145732
  7.2 85.8 %all-gather.4.cloned.1.call-start = ((), (), s32[]{:S(2)}) async-start(), calls=%async_computation.7 | async-start | bytes 6623232 | tf_op jit(solution)/shard_map/all_gather | solution.py:41
  11.4 28.9 %all-to-all-start.1 = ((f32[32,2,128]{2,1,0:T(2,128)}), f32[32,2,128]{2,1,0:T(2,128)S(1)}, u32[]{:S(2)}, u32[]{:S(2)}) async-start(f32[32,2,128]{2,1,0:T(2,128)} %bitcast_dynamic-update-slice_fusion), calls=%async_computation.1 | async-start | bytes 65536 | tf_op jit(solution)/shard_map/all_to_all | solution.py:63
  28.1 16.3 %copy-start.6 = (bf16[896,16]{0,1:T(8,128)(2,1)S(1)}, bf16[896,16]{0,1:T(8,128)(2,1)}, u32[]{:S(2)}) copy-start(bf16[896,16]{0,1:T(8,128)(2,1)} %param.13) | copy-start | bytes 86020
  28.1 29.4 %copy-start.4 = (bf16[2,32,3584]{2,1,0:T(8,128)(2,1)S(1)}, bf16[2,32,3584]{2,1,0:T(8,128)(2,1)}, u32[]{:S(2)}) copy-start(bf16[2,32,3584]{2,1,0:T(8,128)(2,1)} %param.11) | copy-start | bytes 1376260
  28.1 29.3 %copy-start.5 = (bf16[16,3584]{1,0:T(8,128)(2,1)S(1)}, bf16[16,3584]{1,0:T(8,128)(2,1)}, u32[]{:S(2)}) copy-start(bf16[16,3584]{1,0:T(8,128)(2,1)} %param.14) | copy-start | bytes 344068
  40.2 18.9 %all-to-all-start = ((bf16[4,2,32,1024]{3,2,1,0:T(8,128)(2,1)}), bf16[4,2,32,1024]{3,2,1,0:T(8,128)(2,1)S(1)}, u32[]{:S(2)}, u32[]{:S(2)}) async-start(bf16[4,2,32,1024]{3,2,1,0:T(8,128)(2,1)} %bitcast.76), calls=%async_computation | async-start | bytes 1048576 | tf_op jit(solution)/shard_map/all_to_all | solution.py:56
  44.4 96.3 %reduce-scatter.2.cloned.1.call-start = ((), (), s32[]{:S(2)}) async-start(), calls=%async_computation.8 | async-start | bytes 2293760 | tf_op jit(solution)/shard_map/reduce_scatter | solution.py:73
  99.2 8.0 %copy-start.9 = (f32[3584]{0:T(1024)S(1)}, f32[3584]{0:T(1024)}, u32[]{:S(2)}) copy-start(f32[3584]{0:T(1024)} %param.15) | copy-start | bytes 43012
  99.2 8.0 %copy-start.10 = (f32[3584]{0:T(1024)S(1)}, f32[3584]{0:T(1024)}, u32[]{:S(2)}) copy-start(f32[3584]{0:T(1024)} %param.16) | copy-start | bytes 43012
  99.2 41.5 %all-to-all-start.2 = ((bf16[32,2,32,128]{3,2,1,0:T(8,128)(2,1)}), bf16[32,2,32,128]{3,2,1,0:T(8,128)(2,1)S(1)}, u32[]{:S(2)}, u32[]{:S(2)}) async-start(bf16[32,2,32,128]{3,2,1,0:T(8,128)(2,1)} %bitcast.6), calls=%async_computation.3 | async-start | bytes 1048576 | tf_op jit(solution)/shard_map/all_to_all | solution.py:74
  107.2 67.1 %all-gather.6.cloned.1.call-start = ((), (), s32[]{:S(2)}) async-start(), calls=%async_computation.9 | async-start | bytes 2293760 | tf_op jit(solution)/shard_map/all_gather | solution.py:85
  107.2 35.8 %copy-start.12 = (f32[2]{0:T(128)S(1)}, f32[2]{0:T(128)}, u32[]{:S(2)}) copy-start(f32[2]{0:T(128)} %get-tuple-element.27) | copy-start | bytes 28
  142.0 29.3 %copy-start.2 = (bf16[2,128,1024]{2,1,0:T(8,128)(2,1)S(1)}, bf16[2,128,1024]{2,1,0:T(8,128)(2,1)}, u32[]{:S(2)}) copy-start(bf16[2,128,1024]{2,1,0:T(8,128)(2,1)} %param.17) | copy-start | bytes 1572868
  143.0 30.9 %copy-start.13 = (f32[2]{0:T(128)S(1)}, f32[2]{0:T(128)}, u32[]{:S(2)}) copy-start(f32[2]{0:T(128)} %param.19) | copy-start | bytes 28
  143.0 31.3 %copy-start.11 = (f32[2,128]{1,0:T(2,128)S(1)}, f32[2,128]{1,0:T(2,128)}, u32[]{:S(2)}) copy-start(f32[2,128]{1,0:T(2,128)} %reduce_sum.105) | copy-start | bytes 3076
  143.9 24.7 %all-to-all-start.3 = ((f32[128,2,128]{2,1,0:T(2,128)}), f32[128,2,128]{2,1,0:T(2,128)}, u32[]{:S(2)}, u32[]{:S(2)}) async-start(f32[128,2,128]{2,1,0:T(2,128)} %broadcast_in_dim.16), calls=%async_computation.4 | async-start | bytes 262144 | tf_op jit(solution)/shard_map/all_to_all | solution.py:14
  169.4 0.7 copy-start.3
  171.3 11.5 %copy-start.8 = (bf16[2,128,16]{1,2,0:T(8,128)(2,1)S(1)}, bf16[2,128,16]{1,2,0:T(8,128)(2,1)}, u32[]{:S(2)}) copy-start(bf16[2,128,16]{1,2,0:T(8,128)(2,1)} %reduce_sum.102) | copy-start | bytes 24580
  185.3 33.7 %all-to-all-start.4 = ((f32[128,2,128]{2,1,0:T(2,128)}), f32[128,2,128]{2,1,0:T(2,128)S(1)}, u32[]{:S(2)}, u32[]{:S(2)}) async-start(f32[128,2,128]{2,1,0:T(2,128)} %bitcast.19), calls=%async_computation.5 | async-start | bytes 262144 | tf_op jit(solution)/shard_map/all_to_all | solution.py:138
  219.8 24.6 %all-to-all-start.5 = ((f32[128,2,128]{2,1,0:T(2,128)}), f32[128,2,128]{2,1,0:T(2,128)S(1)}, u32[]{:S(2)}, u32[]{:S(2)}) async-start(f32[128,2,128]{2,1,0:T(2,128)} %broadcast_in_dim.20), calls=%async_computation.6 | async-start | bytes 262144 | tf_op jit(solution)/shard_map/all_to_all | solution.py:14
  226.9 5.5 %copy-start.7 = (bf16[896,16]{0,1:T(8,128)(2,1)S(1)}, bf16[896,16]{0,1:T(8,128)(2,1)}, u32[]{:S(2)}) copy-start(bf16[896,16]{0,1:T(8,128)(2,1)} %param.13) | copy-start | bytes 86020
Sparse Core Ops, SparseCore 0:
  10.1 82.8 all-gather.3
  99.3 31.6 reduce-scatter.1
  143.1 28.8 all-gather.5

commit v4 on v2

--- a/solution.py
+++ b/solution.py
@@ -35,6 +35,7 @@
     near = cols // cand_rows
     tensor_index = lax.axis_index("tensor")
     dp_index = lax.axis_index("dp")
+    cand_index = lax.axis_index("cand")
 
     full_weight = lax.all_gather(out_weight, "cand", axis=0, tiled=True)
 
@@ -47,12 +48,17 @@
     lifted = jnp.einsum("qcr,rd->qcd", adapter_own, adapter_up_weight, preferred_element_type=F32)
     base = residual.astype(F32) + ADAPTER_SCALE * lifted
 
-    valid = pair_mask.astype(F32)
-    target = teacher.astype(F32)
-    mask_count = jnp.sum(valid, axis=(1, 2))
+    mask_count = jnp.sum(pair_mask.astype(F32), axis=(1, 2))
+    pairs = gather_copies(jnp.stack([pair_mask.astype(BF16), teacher]), "tensor")
+    valid = pairs[:, 0]
+    known = valid.astype(F32) * pairs[:, 1].astype(F32)
+    row_known = jnp.sum(known, axis=(0, 3))
+    col_known = jnp.sum(known, axis=2)
 
-    full_weight, adapter_in, base, mask_count = lax.optimization_barrier(
-        (full_weight, adapter_in, base, mask_count)
+    full_weight, adapter_in, base, mask_count, valid, row_known, col_known = (
+        lax.optimization_barrier(
+            (full_weight, adapter_in, base, mask_count, valid, row_known, col_known)
+        )
     )
 
     by_owner = jnp.swapaxes(
@@ -72,39 +78,48 @@
 
     unit_sent, unit, scores = lax.optimization_barrier((unit.astype(BF16), unit, scores))
     unit_all = lax.all_gather(unit_sent, "tensor", axis=1, tiled=True)
-    message = jnp.concatenate([scores, mask_count[:, None]], axis=1)
-    message = lax.all_gather(message, "tensor", axis=0)
-    own_scores = jnp.swapaxes(message[:, :, :share], 0, 1).reshape(queries, cand_rows)
     message = jnp.concatenate(
-        [own_scores, jnp.broadcast_to(jnp.sum(message[:, :, share], axis=0)[:, None], (queries, 128))],
-        axis=1,
+        [scores, jnp.broadcast_to(mask_count[:, None], (queries, 128 - share))], axis=1
     )
-    message = gather_copies(message, "cand")
-    count = jnp.sum(message[:, :, cand_rows], axis=0)
-    col_scores = lax.dynamic_slice_in_dim(message, tensor_index * near, near, 0)
-    col_scores = jnp.swapaxes(col_scores[:, :, :cand_rows], 0, 1).reshape(queries, cols)
+    message = gather_copies(message, ("cand", "tensor"))
+    count = jnp.sum(message[:, :, share], axis=0)
+    message = message[:, :, :share].reshape(cand_count, tensor_count, queries, share)
+    own_scores = lax.dynamic_index_in_dim(message, cand_index, 0, keepdims=False)
+    own_scores = jnp.swapaxes(own_scores, 0, 1).reshape(queries, cand_rows)
+    message = message.reshape(tensor_count, near, tensor_count, queries, share)
+    col_scores = jnp.moveaxis(message, 3, 1).reshape(tensor_count, queries, cols)
 
-    margin = own_scores[:, :, None] - col_scores[:, None, :]
-    slope = valid * (jax.nn.sigmoid(margin) - target)
-    total = jnp.sum(valid * (jax.nn.softplus(margin) - target * margin), axis=(1, 2))
-    columns = jnp.swapaxes(jnp.sum(slope, axis=1).reshape(queries, near, cand_rows), 0, 1)
-    columns = lax.dynamic_update_slice_in_dim(
-        jnp.zeros((cand_count, queries, cand_rows), F32), columns, tensor_index * near, 0
+    margin = own_scores[None, :, :, None] - col_scores[:, :, None, :]
+    chance = valid.astype(F32) * jax.nn.sigmoid(margin)
+    row_sum = jnp.sum(chance, axis=(0, 3)) - row_known
+    columns = jnp.sum(chance, axis=2) - col_known
+    columns = columns.reshape(tensor_count, queries, near, cand_rows)
+    columns = jnp.swapaxes(columns, 1, 2).reshape(cand_count, queries, cand_rows)
+    columns, row_sum, own_late, col_late = lax.optimization_barrier(
+        (columns, row_sum, own_scores, col_scores)
     )
     columns = lax.all_to_all(columns, "cand", 0, 0, tiled=True)
-    raw = jnp.sum(slope, axis=2) - jnp.sum(columns, axis=0)
-    sums = lax.psum(jnp.concatenate([raw, total[:, None]], axis=1), "tensor")
-    score_grad = sums[:, :cand_rows] * (loss_scale / count)[:, None]
 
-    own_grad = lax.dynamic_slice_in_dim(score_grad, tensor_index * share, share, 1)
-    grad_rows = (own_grad[:, :, None] * unit).astype(BF16)
-
+    margin = own_late[None, :, :, None] - col_late[:, :, None, :]
+    total = (
+        jnp.sum(valid.astype(F32) * jax.nn.softplus(margin), axis=(0, 2, 3))
+        - jnp.sum(own_late * row_known, axis=1)
+        + jnp.sum(col_late * col_known, axis=(0, 2))
+    )
     adapter_unit = ADAPTER_SCALE * jnp.einsum(
         "qcd,rd->qcr", unit_all, adapter_up_weight, preferred_element_type=F32
     )
     context_unit = jnp.einsum(
         "qcd,dh->qch", unit_all, full_weight, preferred_element_type=F32
     ) + jnp.einsum("qcr,hr->qch", adapter_unit.astype(BF16), adapter_down, preferred_element_type=F32)
+    columns, total, adapter_unit, context_unit, count = lax.optimization_barrier(
+        (columns, total, adapter_unit, context_unit, count)
+    )
+    score_grad = (row_sum - jnp.sum(columns, axis=0)) * (loss_scale / count)[:, None]
+
+    own_grad = lax.dynamic_slice_in_dim(score_grad, tensor_index * share, share, 1)
+    grad_rows = (own_grad[:, :, None] * unit).astype(BF16)
+
     context_grad = (score_grad[:, :, None] * context_unit).astype(BF16)
     adapter_back = (score_grad[:, :, None] * adapter_unit).astype(BF16)
     down_local = jnp.einsum("qcr,qch->rh", adapter_back, context, preferred_element_type=F32)
@@ -117,7 +132,7 @@
     )
 
     slots = jnp.zeros((128,), F32)
-    slots = lax.dynamic_update_slice_in_dim(slots, sums[:, cand_rows], dp_index * queries, 0)
+    slots = lax.dynamic_update_slice_in_dim(slots, total, dp_index * queries, 0)
     flat = jnp.concatenate([down_local, up_local], axis=0)
     wide = flat.shape[1]
     flat = jnp.concatenate([flat, jnp.broadcast_to(slots, (flat.shape[0], 128))], axis=1)

time: 254 us -> 247 us (0.972)
  waiting for transfers between devices: 146 us -> 93.7 us
  blocking collectives: 31.7 us -> 56.2 us
  other arithmetic: 6.54 us -> 17.1 us
  starting transfers between devices: 33.5 us -> 41.4 us
  local copies, waits for them, and re-layouts: 4.9 us -> 8.81 us
    all_gather x1, waiting for transfers between devices: 71.6 us -> 21 us  [on_device(): full_weight = lax.all_gather(out_weight, 'cand', axis=0, tiled=True)]
    all_gather x1, blocking collectives: 10.4 us -> 47.8 us  [on_device(): low_all = lax.all_gather(low_terms, 'tensor', axis=0)]
    all_to_all x1, waiting for transfers between devices: 12 us -> 1.42 us  [on_device(): columns = lax.all_to_all(columns, 'cand', 0, 0, tiled=True)]
    reduce_sum x5 -> x8, other arithmetic: 2 us -> 8.78 us  [the longest x1 3.25 us: on_device(): col_known = jnp.sum(known, axis=2)]
    psum x1 -> x0, blocking collectives: 6.78 us -> none  [on_device(): sums = lax.psum(jnp.concatenate([raw, total[:, None]], axis=1), 'tensor')]
    all_gather x1 -> x0, blocking collectives: 6.1 us -> none  [on_device(): message = lax.all_gather(message, 'tensor', axis=0)]
    all_to_all x2 -> x3, waiting for transfers between devices: 27 us -> 32.3 us  [gather_copies(): return lax.all_to_all(copies, axis, 0, 0, tiled=True)]
    all_to_all x2 -> x3, starting transfers between devices: 17.9 us -> 22.8 us  [gather_copies(): return lax.all_to_all(copies, axis, 0, 0, tiled=True)]
  transfers between devices with their start and end apart: 7 -> 8, of which waited for: 6 -> 6; matrix products, arithmetic and copies ran while one was open for 6% -> 11% of each run, Pallas kernels for 0% -> 0%
where the time goes in v4:
time: 247 us; the launch traced here: 246 us
  waiting for transfers between devices  93.7 us (38%)
  blocking collectives  56.2 us (23%)
  starting transfers between devices  41.4 us (17%)
  other arithmetic  17.1 us (7%)
  matrix products  14.8 us (6%)
  between operations  14.3 us (6%)
  local copies, waits for them, and re-layouts  8.81 us (4%)
    all_gather x1, blocking collectives, on_device(): low_all = lax.all_gather(low_terms, 'tensor', axis=0)  47.8 us
    all_to_all x3, waiting for transfers between devices, gather_copies(): return lax.all_to_all(copies, axis, 0, 0, tiled=True)  32.3 us
    all_to_all x1, waiting for transfers between devices, on_device(): head_terms = lax.all_to_all(head_terms, 'tensor', 0, 0, tiled=True)  23.4 us
    all_to_all x3, starting transfers between devices, gather_copies(): return lax.all_to_all(copies, axis, 0, 0, tiled=True)  22.8 us
    all_gather x1, waiting for transfers between devices, on_device(): full_weight = lax.all_gather(out_weight, 'cand', axis=0, tiled=True)  21 us
    all_to_all x1, waiting for transfers between devices, on_device(): pieces = lax.all_to_all(flat, 'cand', 0, 0, tiled=True)  15 us
    all_to_all x1, starting transfers between devices, on_device(): pieces = lax.all_to_all(flat, 'cand', 0, 0, tiled=True)  10.2 us
    psum x1, blocking collectives, on_device(): piece = lax.psum(piece, 'dp')  8.41 us
  transfers between devices with their start and end apart: 8, of which 6 were waited for; matrix products, arithmetic and copies ran while one was open for 11% of the time, Pallas kernels for 0%

profile of v4, /device:TPU:1, one launch (start us, length us, event | category | flops | bytes accessed | tf_op | source)
XLA Modules:
  0.0 246.3 jit_solution(14012891154526012248)
XLA Ops:
  7.2 0.0 copy-start
  7.2 0.0 all-gather.4.cloned.1.call-start
  7.2 0.7 all-gather.4.cloned.1.call-update
  7.9 1.3 convert_bitcast_fusion
  9.2 1.1 pad_maximum_fusion
  10.4 2.6 %broadcast_in_dim.14 = bf16[4,2,2,128,1024]{4,3,2,1,0:T(8,128)(2,1)} broadcast(bf16[2,2,128,1024]{3,2,1,0:T(8,128)(2,1)S(1)} %pad_maximum_fusion), dimensions={1,2,3,4} | broadcast | bytes 5242880 | tf_op jit(solution)/shard_map/broadcast_in_dim | solution.py:13
  13.0 5.2 %all-to-all-start = ((bf16[4,2,2,128,1024]{4,3,2,1,0:T(8,128)(2,1)}), bf16[4,2,2,128,1024]{4,3,2,1,0:T(8,128)(2,1)}, u32[]{:S(2)}, u32[]{:S(2)}) async-start(bf16[4,2,2,128,1024]{4,3,2,1,0:T(8,128)(2,1)} %broadcast_in_dim.14), calls=%async_computation | async-start | bytes 8388608 | tf_op jit(solution)/shard_map/all_to_all | solution.py:14
  18.2 0.0 copy-done.3
  18.2 0.0 copy-done.6
  18.2 0.2 convolution_convert_fusion
  18.4 47.8 %all-gather = bf16[8,128,16]{1,2,0:T(8,128)(2,1)S(1)} all-gather(bf16[2,128,16]{1,2,0:T(8,128)(2,1)S(1)} %convolution_convert_fusion), channel_id=2, replica_groups=mesh['dp'=4,'cand'=32,'tensor'=4] {'tensor'}, dimensions={0}, use_global_device_ids=true | all-gather | bytes 40960 | tf_op jit(solution)/shard_map/all_gather | solution.py:45
  66.2 0.0 copy-done.1
  66.2 0.2 convert_reduce_fusion.1
  66.4 0.4 fusion.10
  66.8 0.0 all-to-all-done
  66.8 3.3 %fusion.16 = (f32[4,2,1024]{2,1,0:T(2,128)S(1)}, f32[2,128]{1,0:T(2,128)S(1)}) fusion(bf16[4,2,2,128,1024]{4,3,2,1,0:T(8,128)(2,1)} %all-to-all-done), kind=kLoop, calls=%fused_computation.19 | loop fusion | flops 5234432 | bytes 4228096 | tf_op jit(solution)/shard_map/reduce_sum | solution.py:56
  70.0 1.9 slice_bitcast_fusion.1
  72.0 21.0 %all-gather.4.cloned.1.call-done = bf16[3584,896]{1,0:T(8,128)(2,1)} async-done(((bf16[112,896]{1,0:T(8,128)(2,1)}), bf16[3584,896]{1,0:T(8,128)(2,1)}) %all-gather.4.cloned.1.call-update) | async-done | bytes 6422544 | tf_op jit(solution)/shard_map/all_gather | solution.py:40
  93.0 6.3 %fusion.7 = bf16[4,2,32,3584]{3,2,1,0:T(8,128)(2,1)} fusion(bf16[3584,896]{1,0:T(8,128)(2,1)} %all-gather.4.cloned.1.call-done, bf16[2,4,32,896]{3,2,1,0:T(8,128)(2,1)} %bitcast.87), kind=kOutput, calls=%fused_computation.10 | convolution fusion | flops 1645084672 | bytes 8716288 | tf_op jit(solution)/shard_map/tqch,dh->tqcd/dot_general | solution.py:67
  99.3 4.4 %all-to-all-start.1 = ((bf16[4,2,32,3584]{3,2,1,0:T(8,128)(2,1)}), bf16[4,2,32,3584]{3,2,1,0:T(8,128)(2,1)}, u32[]{:S(2)}, u32[]{:S(2)}) async-start(bf16[4,2,32,3584]{3,2,1,0:T(8,128)(2,1)} %fusion.7), calls=%async_computation.1 | async-start | bytes 3670016 | tf_op jit(solution)/shard_map/all_to_all | solution.py:70
  103.7 0.0 all-gather.6.cloned.1.call-start
  103.7 0.0 copy-done.7
  103.7 0.0 copy-done.8
  103.8 23.4 %all-to-all-done.1 = bf16[4,2,32,3584]{3,2,1,0:T(8,128)(2,1)} async-done(((bf16[4,2,32,3584]{3,2,1,0:T(8,128)(2,1)}), bf16[4,2,32,3584]{3,2,1,0:T(8,128)(2,1)}, u32[]{:S(2)}, u32[]{:S(2)}) %all-to-all-start.1) | async-done | bytes 1835040 | tf_op jit(solution)/shard_map/all_to_all | solution.py:70
  127.1 1.9 convert_reduce_fusion
  129.0 0.3 fusion.21
  129.3 1.0 fusion.24
  130.3 0.0 all-gather.6.cloned.1.call-update
  130.3 0.1 broadcast_in_dim.15
  130.4 0.1 pad_maximum_fusion.1
  130.5 0.7 broadcast_in_dim.16
  131.2 10.5 %all-to-all-start.2 = ((f32[128,2,128]{2,1,0:T(2,128)}), f32[128,2,128]{2,1,0:T(2,128)S(1)}, u32[]{:S(2)}, u32[]{:S(2)}) async-start(f32[128,2,128]{2,1,0:T(2,128)} %broadcast_in_dim.16), calls=%async_computation.2 | async-start | bytes 262144 | tf_op jit(solution)/shard_map/all_to_all | solution.py:14
  141.7 18.1 %all-to-all-done.2 = f32[128,2,128]{2,1,0:T(2,128)S(1)} async-done(((f32[128,2,128]{2,1,0:T(2,128)}), f32[128,2,128]{2,1,0:T(2,128)S(1)}, u32[]{:S(2)}, u32[]{:S(2)}) %all-to-all-start.2) | async-done | bytes 131104 | tf_op jit(solution)/shard_map/all_to_all | solution.py:14
  159.9 0.1 reshape.72
  160.1 0.1 sub.52
  160.2 1.8 fusion.18
  162.1 0.6 copy.39
  162.7 3.8 %all-to-all-start.3 = ((f32[32,2,128]{2,1,0:T(2,128)}), f32[32,2,128]{2,1,0:T(2,128)S(1)}, u32[]{:S(2)}, u32[]{:S(2)}) async-start(f32[32,2,128]{2,1,0:T(2,128)} %copy.39), calls=%async_computation.3 | async-start | bytes 65536 | tf_op jit(solution)/shard_map/all_to_all | solution.py:101
  166.5 0.1 multiply_reduce_fusion.1
  166.6 0.1 multiply_reduce_fusion
  166.8 0.3 slice_reduce_fusion
  167.1 2.9 %fusion.11 = f32[2]{0:T(128)S(1)} fusion(bf16[4,2,128,1024]{3,2,1,0:T(8,128)(2,1)S(1)} %slice_bitcast_fusion.1, f32[4,2,1024]{2,1,0:T(2,128)S(1)} %copy.42, f32[2,128]{1,0:T(2,128)S(1)} %sub.52), kind=kLoop, calls=%fused_computation.13 | loop fusion | flops 10485758 | bytes 2130952 | tf_op jit(solution)/shard_map/reduce_sum | solution.py:105
  170.0 0.0 all-gather.6.cloned.1.call-done
  170.0 5.6 %fusion.2 = f32[2,128,896]{2,1,0:T(8,128)S(1)} fusion(bf16[2,128,3584]{2,1,0:T(8,128)(2,1)} %all-gather.6.cloned.1.call-done, bf16[3584,896]{1,0:T(8,128)(2,1)} %all-gather.4.cloned.1.call-done), kind=kOutput, calls=%fused_computation.5 | convolution fusion | flops 1644167168 | bytes 9175040 | tf_op jit(solution)/shard_map/qcd,dh->qch/dot_general | solution.py:112
  175.6 0.6 convolution_multiply_fusion.1
  176.2 0.4 convolution_add_fusion
  176.5 1.4 all-to-all-done.3
  178.0 0.1 subtract_multiply_fusion
  178.1 0.1 constant_dynamic-slice_fusion.1
  178.2 0.2 convolution_bitcast_fusion.1
  178.3 0.2 dynamic_update_slice.3
  178.6 1.3 fusion.20
  179.9 0.8 copy.40
  180.7 10.2 %all-to-all-start.4 = ((f32[32,1,1024]{2,1,0:T(1,128)}), f32[32,1,1024]{2,1,0:T(1,128)S(1)}, u32[]{:S(2)}, u32[]{:S(2)}) async-start(f32[32,1,1024]{2,1,0:T(1,128)} %copy.40), calls=%async_computation.4 | async-start | bytes 262144 | tf_op jit(solution)/shard_map/all_to_all | solution.py:139
  190.9 0.9 multiply_convert_fusion.1
  191.8 15.0 %all-to-all-done.4 = f32[32,1,1024]{2,1,0:T(1,128)S(1)} async-done(((f32[32,1,1024]{2,1,0:T(1,128)}), f32[32,1,1024]{2,1,0:T(1,128)S(1)}, u32[]{:S(2)}, u32[]{:S(2)}) %all-to-all-start.4) | async-done | bytes 131104 | tf_op jit(solution)/shard_map/all_to_all | solution.py:139
  206.8 0.1 reduce_sum.154
  206.9 8.4 %psum.7 = f32[1,1024]{1,0:T(1,128)S(1)} all-reduce(f32[1,1024]{1,0:T(1,128)S(1)} %bitcast.94), channel_id=1, replica_groups=mesh['dp'=4,'cand'=32,'tensor'=4] {'dp'}, use_global_device_ids=true, to_apply=%region_15.16 | all-reduce | flops 1024 | bytes 8192 | tf_op jit(solution)/shard_map/psum | solution.py:141
  215.3 0.7 broadcast_in_dim.20
  216.0 7.1 %all-to-all-start.5 = ((f32[32,1,896]{2,1,0:T(1,128)}), f32[32,1,896]{2,1,0:T(1,128)S(1)}, u32[]{:S(2)}, u32[]{:S(2)}) async-start(f32[32,1,896]{2,1,0:T(1,128)} %broadcast_in_dim.20), calls=%async_computation.5 | async-start | bytes 229376 | tf_op jit(solution)/shard_map/all_to_all | solution.py:14
  223.1 0.9 multiply_convert_fusion.2
  224.0 0.6 fusion.40
  224.6 14.1 %all-to-all-done.5 = f32[32,1,896]{2,1,0:T(1,128)S(1)} async-done(((f32[32,1,896]{2,1,0:T(1,128)}), f32[32,1,896]{2,1,0:T(1,128)S(1)}, u32[]{:S(2)}, u32[]{:S(2)}) %all-to-all-start.5) | async-done | bytes 114720 | tf_op jit(solution)/shard_map/all_to_all | solution.py:14
  238.8 0.6 copy_bitcast_fusion
  (33 shorter events, 0.3 us)
Async XLA Ops:
  7.2 59.2 %copy-start = (bf16[16,3584]{1,0:T(8,128)(2,1)S(1)}, bf16[16,3584]{1,0:T(8,128)(2,1)}, u32[]{:S(2)}) copy-start(bf16[16,3584]{1,0:T(8,128)(2,1)} %param.14) | copy-start | bytes 344068
  7.2 85.8 %all-gather.4.cloned.1.call-start = ((), (), s32[]{:S(2)}) async-start(), calls=%async_computation.6 | async-start | bytes 6623232 | tf_op jit(solution)/shard_map/all_gather | solution.py:40
  13.0 5.2 %copy-start.3 = (bf16[2,128,896]{2,1,0:T(8,128)(2,1)S(1)}, bf16[2,128,896]{2,1,0:T(8,128)(2,1)}, u32[]{:S(2)}) copy-start(bf16[2,128,896]{2,1,0:T(8,128)(2,1)} %param.10) | copy-start | bytes 1376260
  13.0 5.2 %copy-start.6 = (bf16[896,16]{0,1:T(8,128)(2,1)S(1)}, bf16[896,16]{0,1:T(8,128)(2,1)}, u32[]{:S(2)}) copy-start(bf16[896,16]{0,1:T(8,128)(2,1)} %param.13) | copy-start | bytes 86020
  13.0 53.1 %copy-start.1 = (s32[2,128,1024]{2,1,0:T(8,128)S(1)}, s32[2,128,1024]{2,1,0:T(8,128)}, u32[]{:S(2)}) copy-start(s32[2,128,1024]{2,1,0:T(8,128)} %param.18) | copy-start | bytes 3145732
  13.0 53.4 %copy-start.5 = (bf16[2,32,3584]{2,1,0:T(8,128)(2,1)S(1)}, bf16[2,32,3584]{2,1,0:T(8,128)(2,1)}, u32[]{:S(2)}) copy-start(bf16[2,32,3584]{2,1,0:T(8,128)(2,1)} %param.11) | copy-start | bytes 1376260
  13.0 53.8 %all-to-all-start = ((bf16[4,2,2,128,1024]{4,3,2,1,0:T(8,128)(2,1)}), bf16[4,2,2,128,1024]{4,3,2,1,0:T(8,128)(2,1)}, u32[]{:S(2)}, u32[]{:S(2)}) async-start(bf16[4,2,2,128,1024]{4,3,2,1,0:T(8,128)(2,1)} %broadcast_in_dim.14), calls=%async_computation | async-start | bytes 8388608 | tf_op jit(solution)/shard_map/all_to_all | solution.py:14
  93.0 10.8 %copy-start.7 = (f32[3584]{0:T(1024)S(1)}, f32[3584]{0:T(1024)}, u32[]{:S(2)}) copy-start(f32[3584]{0:T(1024)} %param.15) | copy-start | bytes 43012
  93.0 10.8 %copy-start.8 = (f32[3584]{0:T(1024)S(1)}, f32[3584]{0:T(1024)}, u32[]{:S(2)}) copy-start(f32[3584]{0:T(1024)} %param.16) | copy-start | bytes 43012
  99.3 27.9 %all-to-all-start.1 = ((bf16[4,2,32,3584]{3,2,1,0:T(8,128)(2,1)}), bf16[4,2,32,3584]{3,2,1,0:T(8,128)(2,1)}, u32[]{:S(2)}, u32[]{:S(2)}) async-start(bf16[4,2,32,3584]{3,2,1,0:T(8,128)(2,1)} %fusion.7), calls=%async_computation.1 | async-start | bytes 3670016 | tf_op jit(solution)/shard_map/all_to_all | solution.py:70
  103.7 66.3 %all-gather.6.cloned.1.call-start = ((), (), s32[]{:S(2)}) async-start(), calls=%async_computation.7 | async-start | bytes 2293760 | tf_op jit(solution)/shard_map/all_gather | solution.py:80
  131.2 28.7 %all-to-all-start.2 = ((f32[128,2,128]{2,1,0:T(2,128)}), f32[128,2,128]{2,1,0:T(2,128)S(1)}, u32[]{:S(2)}, u32[]{:S(2)}) async-start(f32[128,2,128]{2,1,0:T(2,128)} %broadcast_in_dim.16), calls=%async_computation.2 | async-start | bytes 262144 | tf_op jit(solution)/shard_map/all_to_all | solution.py:14
  162.7 15.3 %all-to-all-start.3 = ((f32[32,2,128]{2,1,0:T(2,128)}), f32[32,2,128]{2,1,0:T(2,128)S(1)}, u32[]{:S(2)}, u32[]{:S(2)}) async-start(f32[32,2,128]{2,1,0:T(2,128)} %copy.39), calls=%async_computation.3 | async-start | bytes 65536 | tf_op jit(solution)/shard_map/all_to_all | solution.py:101
  170.0 8.0 %copy-start.9 = (f32[2]{0:T(128)S(1)}, f32[2]{0:T(128)}, u32[]{:S(2)}) copy-start(f32[2]{0:T(128)} %param.19) | copy-start | bytes 28
  170.0 8.2 %copy-start.4 = (bf16[2,128,896]{2,1,0:T(8,128)(2,1)S(1)}, bf16[2,128,896]{2,1,0:T(8,128)(2,1)}, u32[]{:S(2)}) copy-start(bf16[2,128,896]{2,1,0:T(8,128)(2,1)} %param.10) | copy-start | bytes 1376260
  170.0 5.6 %copy-start.2 = (bf16[2,128,3584]{2,1,0:T(8,128)(2,1)S(1)}, bf16[2,128,3584]{2,1,0:T(8,128)(2,1)}, u32[]{:S(2)}) copy-start(bf16[2,128,3584]{2,1,0:T(8,128)(2,1)} %all-gather.6.cloned.1.call-done) | copy-start | bytes 5505028
  180.7 26.1 %all-to-all-start.4 = ((f32[32,1,1024]{2,1,0:T(1,128)}), f32[32,1,1024]{2,1,0:T(1,128)S(1)}, u32[]{:S(2)}, u32[]{:S(2)}) async-start(f32[32,1,1024]{2,1,0:T(1,128)} %copy.40), calls=%async_computation.4 | async-start | bytes 262144 | tf_op jit(solution)/shard_map/all_to_all | solution.py:139
  216.0 22.7 %all-to-all-start.5 = ((f32[32,1,896]{2,1,0:T(1,128)}), f32[32,1,896]{2,1,0:T(1,128)S(1)}, u32[]{:S(2)}, u32[]{:S(2)}) async-start(f32[32,1,896]{2,1,0:T(1,128)} %broadcast_in_dim.20), calls=%async_computation.5 | async-start | bytes 229376 | tf_op jit(solution)/shard_map/all_to_all | solution.py:14
Sparse Core Ops, SparseCore 0:
  10.1 82.7 all-gather.3
  130.5 32.8 all-gather.5

commit v5 on v4

--- a/solution.py
+++ b/solution.py
@@ -36,6 +36,7 @@
     tensor_index = lax.axis_index("tensor")
     dp_index = lax.axis_index("dp")
     cand_index = lax.axis_index("cand")
+    dp_count = lax.axis_size("dp")
 
     full_weight = lax.all_gather(out_weight, "cand", axis=0, tiled=True)
 
@@ -131,20 +132,39 @@
         "qcr,qcd->rd", adapter_in, block, preferred_element_type=F32
     )
 
-    slots = jnp.zeros((128,), F32)
-    slots = lax.dynamic_update_slice_in_dim(slots, total, dp_index * queries, 0)
+    rank = adapter_down.shape[1]
     flat = jnp.concatenate([down_local, up_local], axis=0)
     wide = flat.shape[1]
-    flat = jnp.concatenate([flat, jnp.broadcast_to(slots, (flat.shape[0], 128))], axis=1)
-    pieces = lax.all_to_all(flat, "cand", 0, 0, tiled=True)
-    piece = jnp.sum(pieces.reshape(cand_count, -1, flat.shape[1]), axis=0)
-    piece = lax.psum(piece, "dp")
-    flat = gather_copies(piece[:, :wide], "cand").reshape(flat.shape[0], wide)
-    rank = adapter_down.shape[1]
+    segments = cand_count // near
+    members = dp_count * near
+    near_groups = [
+        [d * cand_count + a * near + b for d in range(dp_count) for b in range(near)]
+        for a in range(segments)
+    ]
+    far_groups = [[a * near + b for a in range(segments)] for b in range(near)]
+    slots = lax.dynamic_update_slice_in_dim(
+        jnp.zeros((1, 1, 128), F32), total[None, None, :], dp_index * queries, 2
+    )
+    tiles = flat.reshape(2 * rank // 8, 8, wide // 128, 128)
+    tiles = jnp.swapaxes(tiles, 1, 2).reshape(-1, 8, 128)
+    used = tiles.shape[0]
+    height = -(-(used + 1) // members)
+    slots = jnp.pad(slots, ((0, height * members - used - 1), (0, 7), (0, 0)))
+    tiles = jnp.concatenate([tiles, slots]).reshape(members, 8 * height, 128)
+    tiles = lax.all_to_all(
+        tiles, ("dp", "cand"), 0, 0, axis_index_groups=near_groups, tiled=True
+    )
+    tiles = lax.psum(jnp.sum(tiles, axis=0), "cand", axis_index_groups=far_groups)
+    tiles = jnp.broadcast_to(tiles[None], (members,) + tiles.shape)
+    tiles = lax.all_to_all(
+        tiles, ("dp", "cand"), 0, 0, axis_index_groups=near_groups, tiled=True
+    ).reshape(-1, 8, 128)
+    loss_sum = lax.dynamic_slice_in_dim(tiles[used, 0], dp_index * queries, queries, 0)
+    pair_loss = loss_sum / count
+    flat = tiles[:used].reshape(2 * rank // 8, wide // 128, 8, 128)
+    flat = jnp.swapaxes(flat, 1, 2).reshape(2 * rank, wide)
     down_grad = flat[:rank].T
     up_weight_gradient = flat[rank:]
-    loss_sum = lax.dynamic_slice_in_dim(piece[0, wide:], dp_index * queries, queries, 0)
-    pair_loss = loss_sum / count
     return (context_grad, grad_rows, down_grad, up_weight_gradient, pair_loss)
 
 

time: 247 us -> 233 us (0.943)
  waiting for transfers between devices: 93.7 us -> 80.3 us
  starting transfers between devices: 41.4 us -> 35.7 us
  blocking collectives: 56.2 us -> 61.6 us
    all_to_all x3 -> x2, waiting for transfers between devices: 32.3 us -> 18.1 us  [gather_copies(): return lax.all_to_all(copies, axis, 0, 0, tiled=True)]
    all_to_all x3 -> x2, starting transfers between devices: 22.8 us -> 15.7 us  [gather_copies(): return lax.all_to_all(copies, axis, 0, 0, tiled=True)]
    psum x1, blocking collectives: 8.41 us -> 13.8 us  [on_device(): lax.psum(jnp.sum(tiles, axis=0), 'cand', axis_index_groups=far_groups)]
    all_to_all x1 -> x2, starting transfers between devices: 10.2 us -> 11.7 us  [on_device(): lax.all_to_all(tiles, ('dp', 'cand'), 0, 0, axis_index_groups=near_groups...]
    all_to_all x1 -> x2, waiting for transfers between devices: 15 us -> 15.7 us  [on_device(): lax.all_to_all(tiles, ('dp', 'cand'), 0, 0, axis_index_groups=near_groups...]
where the time goes in v5:
time: 233 us; the launch traced here: 232 us
  waiting for transfers between devices  80.3 us (34%)
  blocking collectives  61.6 us (26%)
  starting transfers between devices  35.7 us (15%)
  other arithmetic  17.7 us (8%)
  matrix products  14.8 us (6%)
  between operations  14.3 us (6%)
  local copies, waits for them, and re-layouts  7.83 us (3%)
    all_gather x1, blocking collectives, on_device(): low_all = lax.all_gather(low_terms, 'tensor', axis=0)  47.8 us
    all_to_all x1, waiting for transfers between devices, on_device(): head_terms = lax.all_to_all(head_terms, 'tensor', 0, 0, tiled=True)  23.4 us
    all_gather x1, waiting for transfers between devices, on_device(): full_weight = lax.all_gather(out_weight, 'cand', axis=0, tiled=True)  21 us
    all_to_all x2, waiting for transfers between devices, gather_copies(): return lax.all_to_all(copies, axis, 0, 0, tiled=True)  18.1 us
    all_to_all x2, starting transfers between devices, gather_copies(): return lax.all_to_all(copies, axis, 0, 0, tiled=True)  15.7 us
    all_to_all x2, waiting for transfers between devices, on_device(): lax.all_to_all(tiles, ('dp', 'cand'), 0, 0, axis_index_groups=near_groups...  15.7 us
    psum x1, blocking collectives, on_device(): lax.psum(jnp.sum(tiles, axis=0), 'cand', axis_index_groups=far_groups)  13.8 us
    all_to_all x2, starting transfers between devices, on_device(): lax.all_to_all(tiles, ('dp', 'cand'), 0, 0, axis_index_groups=near_groups...  11.7 us
  transfers between devices with their start and end apart: 8, of which 6 were waited for; matrix products, arithmetic and copies ran while one was open for 11% of the time, Pallas kernels for 0%

profile of v5, /device:TPU:1, one launch (start us, length us, event | category | flops | bytes accessed | tf_op | source)
XLA Modules:
  0.0 232.3 jit_solution(1030955403941672378)
XLA Ops:
  7.2 0.0 copy-start
  7.2 0.0 all-gather.4.cloned.1.call-start
  7.2 0.7 all-gather.4.cloned.1.call-update
  7.9 1.3 convert_bitcast_fusion
  9.2 1.1 pad_maximum_fusion
  10.4 2.6 %broadcast_in_dim.12 = bf16[4,2,2,128,1024]{4,3,2,1,0:T(8,128)(2,1)} broadcast(bf16[2,2,128,1024]{3,2,1,0:T(8,128)(2,1)S(1)} %pad_maximum_fusion), dimensions={1,2,3,4} | broadcast | bytes 5242880 | tf_op jit(solution)/shard_map/broadcast_in_dim | solution.py:13
  13.0 5.2 %all-to-all-start = ((bf16[4,2,2,128,1024]{4,3,2,1,0:T(8,128)(2,1)}), bf16[4,2,2,128,1024]{4,3,2,1,0:T(8,128)(2,1)}, u32[]{:S(2)}, u32[]{:S(2)}) async-start(bf16[4,2,2,128,1024]{4,3,2,1,0:T(8,128)(2,1)} %broadcast_in_dim.12), calls=%async_computation | async-start | bytes 8388608 | tf_op jit(solution)/shard_map/all_to_all | solution.py:14
  18.2 0.0 copy-done.3
  18.2 0.0 copy-done.6
  18.2 0.2 convolution_convert_fusion
  18.4 47.8 %all-gather = bf16[8,128,16]{1,2,0:T(8,128)(2,1)S(1)} all-gather(bf16[2,128,16]{1,2,0:T(8,128)(2,1)S(1)} %convolution_convert_fusion), channel_id=2, replica_groups=mesh['dp'=4,'cand'=32,'tensor'=4] {'tensor'}, dimensions={0}, use_global_device_ids=true | all-gather | bytes 40960 | tf_op jit(solution)/shard_map/all_gather | solution.py:46
  66.2 0.0 copy-done.1
  66.2 0.2 convert_reduce_fusion.1
  66.4 0.0 copy-done
  66.4 0.4 fusion.10
  66.8 0.0 all-to-all-done
  66.8 3.3 %fusion.16 = (f32[4,2,1024]{2,1,0:T(2,128)S(1)}, f32[2,128]{1,0:T(2,128)S(1)}) fusion(bf16[4,2,2,128,1024]{4,3,2,1,0:T(8,128)(2,1)} %all-to-all-done), kind=kLoop, calls=%fused_computation.19 | loop fusion | flops 5234432 | bytes 4228096 | tf_op jit(solution)/shard_map/reduce_sum | solution.py:57
  70.0 1.9 slice_bitcast_fusion.1
  72.0 21.0 %all-gather.4.cloned.1.call-done = bf16[3584,896]{1,0:T(8,128)(2,1)} async-done(((bf16[112,896]{1,0:T(8,128)(2,1)}), bf16[3584,896]{1,0:T(8,128)(2,1)}) %all-gather.4.cloned.1.call-update) | async-done | bytes 6422544 | tf_op jit(solution)/shard_map/all_gather | solution.py:41
  93.0 6.3 %fusion.7 = bf16[4,2,32,3584]{3,2,1,0:T(8,128)(2,1)} fusion(bf16[3584,896]{1,0:T(8,128)(2,1)} %all-gather.4.cloned.1.call-done, bf16[2,4,32,896]{3,2,1,0:T(8,128)(2,1)} %bitcast.93), kind=kOutput, calls=%fused_computation.10 | convolution fusion | flops 1645084672 | bytes 8716288 | tf_op jit(solution)/shard_map/tqch,dh->tqcd/dot_general | solution.py:68
  99.3 4.4 %all-to-all-start.1 = ((bf16[4,2,32,3584]{3,2,1,0:T(8,128)(2,1)}), bf16[4,2,32,3584]{3,2,1,0:T(8,128)(2,1)}, u32[]{:S(2)}, u32[]{:S(2)}) async-start(bf16[4,2,32,3584]{3,2,1,0:T(8,128)(2,1)} %fusion.7), calls=%async_computation.1 | async-start | bytes 3670016 | tf_op jit(solution)/shard_map/all_to_all | solution.py:71
  103.7 0.0 all-gather.6.cloned.1.call-start
  103.7 0.0 copy-done.7
  103.7 0.0 copy-done.8
  103.8 23.4 %all-to-all-done.1 = bf16[4,2,32,3584]{3,2,1,0:T(8,128)(2,1)} async-done(((bf16[4,2,32,3584]{3,2,1,0:T(8,128)(2,1)}), bf16[4,2,32,3584]{3,2,1,0:T(8,128)(2,1)}, u32[]{:S(2)}, u32[]{:S(2)}) %all-to-all-start.1) | async-done | bytes 1835040 | tf_op jit(solution)/shard_map/all_to_all | solution.py:71
  127.1 1.9 convert_reduce_fusion
  129.0 0.3 fusion.21
  129.3 1.0 fusion.24
  130.3 0.0 all-gather.6.cloned.1.call-update
  130.3 0.1 broadcast_in_dim.13
  130.4 0.1 pad_maximum_fusion.2
  130.5 0.7 broadcast_in_dim.14
  131.2 10.5 %all-to-all-start.2 = ((f32[128,2,128]{2,1,0:T(2,128)}), f32[128,2,128]{2,1,0:T(2,128)S(1)}, u32[]{:S(2)}, u32[]{:S(2)}) async-start(f32[128,2,128]{2,1,0:T(2,128)} %broadcast_in_dim.14), calls=%async_computation.2 | async-start | bytes 262144 | tf_op jit(solution)/shard_map/all_to_all | solution.py:14
  141.7 18.1 %all-to-all-done.2 = f32[128,2,128]{2,1,0:T(2,128)S(1)} async-done(((f32[128,2,128]{2,1,0:T(2,128)}), f32[128,2,128]{2,1,0:T(2,128)S(1)}, u32[]{:S(2)}, u32[]{:S(2)}) %all-to-all-start.2) | async-done | bytes 131104 | tf_op jit(solution)/shard_map/all_to_all | solution.py:14
  159.9 0.1 reshape.78
  160.1 0.1 sub.52
  160.2 1.8 fusion.18
  162.1 0.6 copy.37
  162.7 3.8 %all-to-all-start.3 = ((f32[32,2,128]{2,1,0:T(2,128)}), f32[32,2,128]{2,1,0:T(2,128)S(1)}, u32[]{:S(2)}, u32[]{:S(2)}) async-start(f32[32,2,128]{2,1,0:T(2,128)} %copy.37), calls=%async_computation.3 | async-start | bytes 65536 | tf_op jit(solution)/shard_map/all_to_all | solution.py:102
  166.5 0.1 multiply_reduce_fusion.1
  166.6 0.1 multiply_reduce_fusion
  166.8 0.3 slice_reduce_fusion
  167.1 2.9 %fusion.11 = f32[2]{0:T(128)S(1)} fusion(bf16[4,2,128,1024]{3,2,1,0:T(8,128)(2,1)S(1)} %slice_bitcast_fusion.1, f32[4,2,1024]{2,1,0:T(2,128)S(1)} %copy.39, f32[2,128]{1,0:T(2,128)S(1)} %sub.52), kind=kLoop, calls=%fused_computation.13 | loop fusion | flops 10485758 | bytes 2130952 | tf_op jit(solution)/shard_map/reduce_sum | solution.py:106
  170.0 0.0 all-gather.6.cloned.1.call-done
  170.0 5.6 %fusion.2 = f32[2,128,896]{2,1,0:T(8,128)S(1)} fusion(bf16[2,128,3584]{2,1,0:T(8,128)(2,1)} %all-gather.6.cloned.1.call-done, bf16[3584,896]{1,0:T(8,128)(2,1)} %all-gather.4.cloned.1.call-done), kind=kOutput, calls=%fused_computation.5 | convolution fusion | flops 1644167168 | bytes 9175040 | tf_op jit(solution)/shard_map/qcd,dh->qch/dot_general | solution.py:113
  175.6 0.6 convolution_multiply_fusion.1
  176.2 0.4 convolution_add_fusion
  176.5 1.4 all-to-all-done.3
  178.0 0.1 subtract_multiply_fusion
  178.1 0.2 convolution_bitcast_fusion.1
  178.3 1.3 fusion.20
  179.6 0.1 dynamic_update_slice.3
  179.8 0.7 select_maximum_fusion
  180.4 5.8 %all-to-all-start.4 = ((f32[32,8,128]{2,1,0:T(8,128)}), f32[32,8,128]{2,1,0:T(8,128)S(1)}, u32[]{:S(2)}, u32[]{:S(2)}) async-start(f32[32,8,128]{2,1,0:T(8,128)} %select_maximum_fusion), calls=%async_computation.4 | async-start | bytes 262144 | tf_op jit(solution)/shard_map/all_to_all | solution.py:154
  186.2 0.1 constant_dynamic-slice_fusion.1
  186.3 8.6 %all-to-all-done.4 = f32[32,8,128]{2,1,0:T(8,128)S(1)} async-done(((f32[32,8,128]{2,1,0:T(8,128)}), f32[32,8,128]{2,1,0:T(8,128)S(1)}, u32[]{:S(2)}, u32[]{:S(2)}) %all-to-all-start.4) | async-done | bytes 131104 | tf_op jit(solution)/shard_map/all_to_all | solution.py:154
  195.0 13.8 %psum.7 = f32[8,128]{1,0:T(8,128)S(1)} all-reduce(f32[8,128]{1,0:T(8,128)S(1)} %reduce_sum.152), channel_id=1, replica_groups={{0,32,64,96},{4,36,68,100},{8,40,72,104},{12,44,76,108},{16,48,80,112},..., use_global_device_ids=true, to_apply=%region_15.16 | all-reduce | flops 1024 | bytes 8192 | tf_op jit(solution)/shard_map/psum | solution.py:157
  208.8 0.6 broadcast_in_dim.17
  209.4 5.9 %all-to-all-start.5 = ((f32[32,8,128]{2,1,0:T(8,128)}), f32[32,8,128]{2,1,0:T(8,128)S(1)}, u32[]{:S(2)}, u32[]{:S(2)}) async-start(f32[32,8,128]{2,1,0:T(8,128)} %broadcast_in_dim.17), calls=%async_computation.5 | async-start | bytes 262144 | tf_op jit(solution)/shard_map/all_to_all | solution.py:159
  215.4 0.9 multiply_convert_fusion.1
  216.3 0.9 multiply_convert_fusion.2
  217.1 7.0 %all-to-all-done.5 = f32[32,8,128]{2,1,0:T(8,128)S(1)} async-done(((f32[32,8,128]{2,1,0:T(8,128)}), f32[32,8,128]{2,1,0:T(8,128)S(1)}, u32[]{:S(2)}, u32[]{:S(2)}) %all-to-all-start.5) | async-done | bytes 131104 | tf_op jit(solution)/shard_map/all_to_all | solution.py:159
  224.2 0.6 fusion.40
  224.8 0.6 slice_bitcast_fusion.2
  (31 shorter events, 0.3 us)
Async XLA Ops:
  7.2 59.2 %copy-start = (bf16[16,3584]{1,0:T(8,128)(2,1)S(1)}, bf16[16,3584]{1,0:T(8,128)(2,1)}, u32[]{:S(2)}) copy-start(bf16[16,3584]{1,0:T(8,128)(2,1)} %param.14) | copy-start | bytes 344068
  7.2 85.8 %all-gather.4.cloned.1.call-start = ((), (), s32[]{:S(2)}) async-start(), calls=%async_computation.6 | async-start | bytes 6623232 | tf_op jit(solution)/shard_map/all_gather | solution.py:41
  13.0 5.2 %copy-start.3 = (bf16[2,128,896]{2,1,0:T(8,128)(2,1)S(1)}, bf16[2,128,896]{2,1,0:T(8,128)(2,1)}, u32[]{:S(2)}) copy-start(bf16[2,128,896]{2,1,0:T(8,128)(2,1)} %param.10) | copy-start | bytes 1376260
  13.0 5.2 %copy-start.6 = (bf16[896,16]{0,1:T(8,128)(2,1)S(1)}, bf16[896,16]{0,1:T(8,128)(2,1)}, u32[]{:S(2)}) copy-start(bf16[896,16]{0,1:T(8,128)(2,1)} %param.13) | copy-start | bytes 86020
  13.0 53.1 %copy-start.1 = (s32[2,128,1024]{2,1,0:T(8,128)S(1)}, s32[2,128,1024]{2,1,0:T(8,128)}, u32[]{:S(2)}) copy-start(s32[2,128,1024]{2,1,0:T(8,128)} %param.18) | copy-start | bytes 3145732
  13.0 53.4 %copy-start.5 = (bf16[2,32,3584]{2,1,0:T(8,128)(2,1)S(1)}, bf16[2,32,3584]{2,1,0:T(8,128)(2,1)}, u32[]{:S(2)}) copy-start(bf16[2,32,3584]{2,1,0:T(8,128)(2,1)} %param.11) | copy-start | bytes 1376260
  13.0 53.8 %all-to-all-start = ((bf16[4,2,2,128,1024]{4,3,2,1,0:T(8,128)(2,1)}), bf16[4,2,2,128,1024]{4,3,2,1,0:T(8,128)(2,1)}, u32[]{:S(2)}, u32[]{:S(2)}) async-start(bf16[4,2,2,128,1024]{4,3,2,1,0:T(8,128)(2,1)} %broadcast_in_dim.12), calls=%async_computation | async-start | bytes 8388608 | tf_op jit(solution)/shard_map/all_to_all | solution.py:14
  93.0 10.8 %copy-start.7 = (f32[3584]{0:T(1024)S(1)}, f32[3584]{0:T(1024)}, u32[]{:S(2)}) copy-start(f32[3584]{0:T(1024)} %param.15) | copy-start | bytes 43012
  93.0 10.8 %copy-start.8 = (f32[3584]{0:T(1024)S(1)}, f32[3584]{0:T(1024)}, u32[]{:S(2)}) copy-start(f32[3584]{0:T(1024)} %param.16) | copy-start | bytes 43012
  99.3 27.9 %all-to-all-start.1 = ((bf16[4,2,32,3584]{3,2,1,0:T(8,128)(2,1)}), bf16[4,2,32,3584]{3,2,1,0:T(8,128)(2,1)}, u32[]{:S(2)}, u32[]{:S(2)}) async-start(bf16[4,2,32,3584]{3,2,1,0:T(8,128)(2,1)} %fusion.7), calls=%async_computation.1 | async-start | bytes 3670016 | tf_op jit(solution)/shard_map/all_to_all | solution.py:71
  103.7 66.3 %all-gather.6.cloned.1.call-start = ((), (), s32[]{:S(2)}) async-start(), calls=%async_computation.7 | async-start | bytes 2293760 | tf_op jit(solution)/shard_map/all_gather | solution.py:81
  131.2 28.7 %all-to-all-start.2 = ((f32[128,2,128]{2,1,0:T(2,128)}), f32[128,2,128]{2,1,0:T(2,128)S(1)}, u32[]{:S(2)}, u32[]{:S(2)}) async-start(f32[128,2,128]{2,1,0:T(2,128)} %broadcast_in_dim.14), calls=%async_computation.2 | async-start | bytes 262144 | tf_op jit(solution)/shard_map/all_to_all | solution.py:14
  162.7 15.3 %all-to-all-start.3 = ((f32[32,2,128]{2,1,0:T(2,128)}), f32[32,2,128]{2,1,0:T(2,128)S(1)}, u32[]{:S(2)}, u32[]{:S(2)}) async-start(f32[32,2,128]{2,1,0:T(2,128)} %copy.37), calls=%async_computation.3 | async-start | bytes 65536 | tf_op jit(solution)/shard_map/all_to_all | solution.py:102
  170.0 8.0 %copy-start.9 = (f32[2]{0:T(128)S(1)}, f32[2]{0:T(128)}, u32[]{:S(2)}) copy-start(f32[2]{0:T(128)} %param.19) | copy-start | bytes 28
  170.0 8.1 %copy-start.4 = (bf16[2,128,896]{2,1,0:T(8,128)(2,1)S(1)}, bf16[2,128,896]{2,1,0:T(8,128)(2,1)}, u32[]{:S(2)}) copy-start(bf16[2,128,896]{2,1,0:T(8,128)(2,1)} %param.10) | copy-start | bytes 1376260
  170.0 5.6 %copy-start.2 = (bf16[2,128,3584]{2,1,0:T(8,128)(2,1)S(1)}, bf16[2,128,3584]{2,1,0:T(8,128)(2,1)}, u32[]{:S(2)}) copy-start(bf16[2,128,3584]{2,1,0:T(8,128)(2,1)} %all-gather.6.cloned.1.call-done) | copy-start | bytes 5505028
  180.4 14.5 %all-to-all-start.4 = ((f32[32,8,128]{2,1,0:T(8,128)}), f32[32,8,128]{2,1,0:T(8,128)S(1)}, u32[]{:S(2)}, u32[]{:S(2)}) async-start(f32[32,8,128]{2,1,0:T(8,128)} %select_maximum_fusion), calls=%async_computation.4 | async-start | bytes 262144 | tf_op jit(solution)/shard_map/all_to_all | solution.py:154
  209.4 14.7 %all-to-all-start.5 = ((f32[32,8,128]{2,1,0:T(8,128)}), f32[32,8,128]{2,1,0:T(8,128)S(1)}, u32[]{:S(2)}, u32[]{:S(2)}) async-start(f32[32,8,128]{2,1,0:T(8,128)} %broadcast_in_dim.17), calls=%async_computation.5 | async-start | bytes 262144 | tf_op jit(solution)/shard_map/all_to_all | solution.py:159
Sparse Core Ops, SparseCore 0:
  10.1 82.7 all-gather.3
  130.5 32.8 all-gather.5

commit v6 on v5

--- a/solution.py
+++ b/solution.py
@@ -65,11 +65,20 @@
     by_owner = jnp.swapaxes(
         context.reshape(queries, tensor_count, share, context.shape[2]), 0, 1
     )
-    head_terms = jnp.einsum(
-        "tqch,dh->tqcd", by_owner, full_weight, preferred_element_type=F32
+    half = width // 2
+    head_first = jnp.einsum(
+        "tqch,dh->tqcd", by_owner, full_weight[:half], preferred_element_type=F32
     ).astype(BF16)
-    head_terms = lax.all_to_all(head_terms, "tensor", 0, 0, tiled=True)
-    hidden = (base + jnp.sum(head_terms.astype(F32), axis=0)).astype(BF16).astype(F32)
+    head_first = lax.all_to_all(head_first, "tensor", 0, 0, tiled=True)
+    head_second = jnp.einsum(
+        "tqch,dh->tqcd", by_owner, full_weight[half:], preferred_element_type=F32
+    ).astype(BF16)
+    head_first, head_second = lax.optimization_barrier((head_first, head_second))
+    head_second = lax.all_to_all(head_second, "tensor", 0, 0, tiled=True)
+    head_sum = jnp.concatenate(
+        [jnp.sum(head_first.astype(F32), axis=0), jnp.sum(head_second.astype(F32), axis=0)], axis=2
+    )
+    hidden = (base + head_sum).astype(BF16).astype(F32)
     inv_rms = lax.rsqrt(jnp.mean(hidden * hidden, axis=2) + epsilon)
     gain = norm_gain * score_weight
     dot = jnp.sum(hidden * gain, axis=2)
@@ -113,8 +122,11 @@
     context_unit = jnp.einsum(
         "qcd,dh->qch", unit_all, full_weight, preferred_element_type=F32
     ) + jnp.einsum("qcr,hr->qch", adapter_unit.astype(BF16), adapter_down, preferred_element_type=F32)
-    columns, total, adapter_unit, context_unit, count = lax.optimization_barrier(
-        (columns, total, adapter_unit, context_unit, count)
+    unit_block = lax.dynamic_slice_in_dim(
+        unit_all, tensor_index * context.shape[2], context.shape[2], 2
+    )
+    columns, total, adapter_unit, context_unit, unit_block, count = lax.optimization_barrier(
+        (columns, total, adapter_unit, context_unit, unit_block, count)
     )
     score_grad = (row_sum - jnp.sum(columns, axis=0)) * (loss_scale / count)[:, None]
 
@@ -124,12 +136,9 @@
     context_grad = (score_grad[:, :, None] * context_unit).astype(BF16)
     adapter_back = (score_grad[:, :, None] * adapter_unit).astype(BF16)
     down_local = jnp.einsum("qcr,qch->rh", adapter_back, context, preferred_element_type=F32)
-    block = lax.dynamic_slice_in_dim(
-        unit_all, tensor_index * context.shape[2], context.shape[2], 2
-    )
-    block = (score_grad[:, :, None] * block.astype(F32)).astype(BF16)
+    adapter_scaled = (score_grad[:, :, None] * adapter_in.astype(F32)).astype(BF16)
     up_local = ADAPTER_SCALE * jnp.einsum(
-        "qcr,qcd->rd", adapter_in, block, preferred_element_type=F32
+        "qcr,qcd->rd", adapter_scaled, unit_block, preferred_element_type=F32
     )
 
     rank = adapter_down.shape[1]

time: 233 us -> 237 us (1.017)
  starting transfers between devices: 35.7 us -> 40.7 us
  waiting for transfers between devices: 80.3 us -> 76.5 us
    all_to_all x1 -> x2, starting transfers between devices: 4.4 us -> 8.22 us  [the longest x1 4.21 us: on_device(): head_second = lax.all_to_all(head_second, 'tensor', 0, 0, tiled=True)]
    all_to_all x1 -> x2, waiting for transfers between devices: 23.4 us -> 20.5 us  [the longest x1 11.4 us: on_device(): head_second = lax.all_to_all(head_second, 'tensor', 0, 0, tiled=True)]
    dot_general x2 -> x3, matrix products: 7.59 us -> 8.27 us  [the longest x1 4.11 us: on_device(): jnp.einsum('tqch,dh->tqcd', by_owner, full_weight[half:], preferred_eleme...]
  transfers between devices with their start and end apart: 8 -> 9, of which waited for: 6 -> 7; matrix products, arithmetic and copies ran while one was open for 11% -> 14% of each run, Pallas kernels for 0% -> 0%
where the time goes in v6:
time: 237 us
  waiting for transfers between devices  76.5 us (32%)
  blocking collectives  61.6 us (26%)
  starting transfers between devices  40.7 us (17%)
  other arithmetic  19.3 us (8%)
  matrix products  16.4 us (7%)
  between operations  14.3 us (6%)
  local copies, waits for them, and re-layouts  7.91 us (3%)
    all_gather x1, blocking collectives, on_device(): low_all = lax.all_gather(low_terms, 'tensor', axis=0)  47.8 us
    all_gather x1, waiting for transfers between devices, on_device(): full_weight = lax.all_gather(out_weight, 'cand', axis=0, tiled=True)  20.1 us
    all_to_all x2, waiting for transfers between devices, gather_copies(): return lax.all_to_all(copies, axis, 0, 0, tiled=True)  18.1 us
    all_to_all x2, starting transfers between devices, gather_copies(): return lax.all_to_all(copies, axis, 0, 0, tiled=True)  16.8 us
    all_to_all x2, waiting for transfers between devices, on_device(): lax.all_to_all(tiles, ('dp', 'cand'), 0, 0, axis_index_groups=near_groups...  15.7 us
    psum x1, blocking collectives, on_device(): lax.psum(jnp.sum(tiles, axis=0), 'cand', axis_index_groups=far_groups)  13.8 us
    all_to_all x2, starting transfers between devices, on_device(): lax.all_to_all(tiles, ('dp', 'cand'), 0, 0, axis_index_groups=near_groups...  11.8 us
    all_to_all x1, waiting for transfers between devices, on_device(): head_second = lax.all_to_all(head_second, 'tensor', 0, 0, tiled=True)  11.4 us
  transfers between devices with their start and end apart: 9, of which 7 were waited for; matrix products, arithmetic and copies ran while one was open for 14% of the time, Pallas kernels for 0%

profile of v6, /device:TPU:1, one launch (start us, length us, event | category | flops | bytes accessed | tf_op | source)
XLA Modules:
  0.0 236.7 jit_solution(17364438176664501968)
XLA Ops:
  7.2 0.0 copy-start
  7.2 0.0 all-gather.4.cloned.1.call-start
  7.2 0.7 all-gather.4.cloned.1.call-update
  7.9 1.3 convert_bitcast_fusion
  9.2 1.1 pad_maximum_fusion
  10.4 2.6 %broadcast_in_dim.12 = bf16[4,2,2,128,1024]{4,3,2,1,0:T(8,128)(2,1)} broadcast(bf16[2,2,128,1024]{3,2,1,0:T(8,128)(2,1)S(1)} %pad_maximum_fusion), dimensions={1,2,3,4} | broadcast | bytes 5242880 | tf_op jit(solution)/shard_map/broadcast_in_dim | solution.py:13
  13.0 5.2 %all-to-all-start = ((bf16[4,2,2,128,1024]{4,3,2,1,0:T(8,128)(2,1)}), bf16[4,2,2,128,1024]{4,3,2,1,0:T(8,128)(2,1)}, u32[]{:S(2)}, u32[]{:S(2)}) async-start(bf16[4,2,2,128,1024]{4,3,2,1,0:T(8,128)(2,1)} %broadcast_in_dim.12), calls=%async_computation | async-start | bytes 8388608 | tf_op jit(solution)/shard_map/all_to_all | solution.py:14
  18.2 0.0 copy-done.3
  18.2 0.2 convolution_convert_fusion
  18.4 47.8 %all-gather = bf16[8,128,16]{1,2,0:T(8,128)(2,1)S(1)} all-gather(bf16[2,128,16]{1,2,0:T(8,128)(2,1)S(1)} %convolution_convert_fusion), channel_id=2, replica_groups=mesh['dp'=4,'cand'=32,'tensor'=4] {'tensor'}, dimensions={0}, use_global_device_ids=true | all-gather | bytes 40960 | tf_op jit(solution)/shard_map/all_gather | solution.py:46
  66.2 0.2 convert_reduce_fusion.2
  66.4 1.3 fusion.2
  67.7 0.0 all-to-all-done
  67.7 3.3 %fusion.8 = (f32[4,2,1024]{2,1,0:T(2,128)S(1)}, f32[2,128]{1,0:T(2,128)S(1)}) fusion(bf16[4,2,2,128,1024]{4,3,2,1,0:T(8,128)(2,1)} %all-to-all-done), kind=kLoop, calls=%fused_computation.15 | loop fusion | flops 5234432 | bytes 4228096 | tf_op jit(solution)/shard_map/reduce_sum | solution.py:57
  71.0 1.9 slice_bitcast_fusion.1
  72.9 20.1 %all-gather.4.cloned.1.call-done = bf16[3584,896]{1,0:T(8,128)(2,1)} async-done(((bf16[112,896]{1,0:T(8,128)(2,1)}), bf16[3584,896]{1,0:T(8,128)(2,1)}) %all-gather.4.cloned.1.call-update) | async-done | bytes 6422544 | tf_op jit(solution)/shard_map/all_gather | solution.py:41
  93.0 4.0 %fusion.25 = bf16[4,2,32,1792]{3,2,1,0:T(8,128)(2,1)} fusion(bf16[3584,896]{1,0:T(8,128)(2,1)} %all-gather.4.cloned.1.call-done, bf16[2,4,32,896]{3,2,1,0:T(8,128)(2,1)S(1)} %bitcast.107), kind=kOutput, calls=%fused_computation.26 | convolution fusion | flops 822542336 | bytes 4587520 | tf_op jit(solution)/shard_map/tqch,dh->tqcd/dot_general | solution.py:69
  97.0 4.0 %all-to-all-start.1 = ((bf16[4,2,32,1792]{3,2,1,0:T(8,128)(2,1)}), bf16[4,2,32,1792]{3,2,1,0:T(8,128)(2,1)S(1)}, u32[]{:S(2)}, u32[]{:S(2)}) async-start(bf16[4,2,32,1792]{3,2,1,0:T(8,128)(2,1)} %fusion.25), calls=%async_computation.1 | async-start | bytes 1835008 | tf_op jit(solution)/shard_map/all_to_all | solution.py:72
  101.0 4.1 %fusion.22 = bf16[4,2,32,1792]{3,2,1,0:T(8,128)(2,1)} fusion(bf16[3584,896]{1,0:T(8,128)(2,1)} %all-gather.4.cloned.1.call-done, bf16[2,4,32,896]{3,2,1,0:T(8,128)(2,1)} %bitcast.106), kind=kOutput, calls=%fused_computation.25 | convolution fusion | flops 822542336 | bytes 4587520 | tf_op jit(solution)/shard_map/tqch,dh->tqcd/dot_general | solution.py:73
  105.1 9.1 %all-to-all-done.1 = bf16[4,2,32,1792]{3,2,1,0:T(8,128)(2,1)S(1)} async-done(((bf16[4,2,32,1792]{3,2,1,0:T(8,128)(2,1)}), bf16[4,2,32,1792]{3,2,1,0:T(8,128)(2,1)S(1)}, u32[]{:S(2)}, u32[]{:S(2)}) %all-to-all-start.1) | async-done | bytes 917536 | tf_op jit(solution)/shard_map/all_to_all | solution.py:72
  114.2 4.2 %all-to-all-start.2 = ((bf16[4,2,32,1792]{3,2,1,0:T(8,128)(2,1)}), bf16[4,2,32,1792]{3,2,1,0:T(8,128)(2,1)}, u32[]{:S(2)}, u32[]{:S(2)}) async-start(bf16[4,2,32,1792]{3,2,1,0:T(8,128)(2,1)} %fusion.22), calls=%async_computation.2 | async-start | bytes 1835008 | tf_op jit(solution)/shard_map/all_to_all | solution.py:77
  118.4 0.0 all-gather.6.cloned.1.call-start
  118.5 0.9 convert_reduce_fusion.1
  119.4 11.4 %all-to-all-done.2 = bf16[4,2,32,1792]{3,2,1,0:T(8,128)(2,1)} async-done(((bf16[4,2,32,1792]{3,2,1,0:T(8,128)(2,1)}), bf16[4,2,32,1792]{3,2,1,0:T(8,128)(2,1)}, u32[]{:S(2)}, u32[]{:S(2)}) %all-to-all-start.2) | async-done | bytes 917536 | tf_op jit(solution)/shard_map/all_to_all | solution.py:77
  130.8 1.4 convert_reduce_fusion
  132.2 1.6 fusion.31
  133.7 1.0 fusion.34
  134.7 0.0 all-gather.6.cloned.1.call-update
  134.7 0.1 broadcast_in_dim.13
  134.8 0.1 pad_maximum_fusion.2
  134.9 0.7 broadcast_in_dim.14
  135.6 11.6 %all-to-all-start.3 = ((f32[128,2,128]{2,1,0:T(2,128)}), f32[128,2,128]{2,1,0:T(2,128)S(1)}, u32[]{:S(2)}, u32[]{:S(2)}) async-start(f32[128,2,128]{2,1,0:T(2,128)} %broadcast_in_dim.14), calls=%async_computation.3 | async-start | bytes 262144 | tf_op jit(solution)/shard_map/all_to_all | solution.py:14
  147.3 18.1 %all-to-all-done.3 = f32[128,2,128]{2,1,0:T(2,128)S(1)} async-done(((f32[128,2,128]{2,1,0:T(2,128)}), f32[128,2,128]{2,1,0:T(2,128)S(1)}, u32[]{:S(2)}, u32[]{:S(2)}) %all-to-all-start.3) | async-done | bytes 131104 | tf_op jit(solution)/shard_map/all_to_all | solution.py:14
  165.4 0.1 reshape.79
  165.6 0.1 sub.52
  165.7 1.8 fusion.28
  167.6 0.6 copy.37
  168.2 3.8 %all-to-all-start.4 = ((f32[32,2,128]{2,1,0:T(2,128)}), f32[32,2,128]{2,1,0:T(2,128)S(1)}, u32[]{:S(2)}, u32[]{:S(2)}) async-start(f32[32,2,128]{2,1,0:T(2,128)} %copy.37), calls=%async_computation.4 | async-start | bytes 65536 | tf_op jit(solution)/shard_map/all_to_all | solution.py:111
  172.0 0.1 multiply_reduce_fusion.1
  172.1 0.1 multiply_reduce_fusion
  172.3 0.3 slice_reduce_fusion
  172.6 2.9 %fusion.3 = f32[2]{0:T(128)S(1)} fusion(bf16[4,2,128,1024]{3,2,1,0:T(8,128)(2,1)S(1)} %slice_bitcast_fusion.1, f32[4,2,1024]{2,1,0:T(2,128)S(1)} %copy.40, f32[2,128]{1,0:T(2,128)S(1)} %sub.52), kind=kLoop, calls=%fused_computation.9 | loop fusion | flops 10485758 | bytes 2130952 | tf_op jit(solution)/shard_map/reduce_sum | solution.py:115
  175.5 5.6 %fusion = f32[2,128,896]{2,1,0:T(8,128)S(1)} fusion(bf16[2,128,3584]{2,1,0:T(8,128)(2,1)} %all-gather.6.cloned.1.call-done, bf16[3584,896]{1,0:T(8,128)(2,1)} %all-gather.4.cloned.1.call-done), kind=kOutput, calls=%fused_computation.3 | convolution fusion | flops 1644167168 | bytes 9175040 | tf_op jit(solution)/shard_map/qcd,dh->qch/dot_general | solution.py:122
  181.1 0.0 copy-start.9
  181.1 0.0 copy-start.4
  181.1 0.6 convolution_multiply_fusion.1
  181.7 0.4 convolution_add_fusion
  182.1 1.4 all-to-all-done.4
  183.5 0.1 subtract_multiply_fusion
  183.6 0.2 convolution_bitcast_fusion.1
  183.8 0.2 fusion.30
  184.0 0.1 dynamic_update_slice.3
  184.1 0.7 select_maximum_fusion
  184.8 5.8 %all-to-all-start.5 = ((f32[32,8,128]{2,1,0:T(8,128)}), f32[32,8,128]{2,1,0:T(8,128)S(1)}, u32[]{:S(2)}, u32[]{:S(2)}) async-start(f32[32,8,128]{2,1,0:T(8,128)} %select_maximum_fusion), calls=%async_computation.5 | async-start | bytes 262144 | tf_op jit(solution)/shard_map/all_to_all | solution.py:163
  190.7 0.1 constant_dynamic-slice_fusion.1
  190.7 8.6 %all-to-all-done.5 = f32[32,8,128]{2,1,0:T(8,128)S(1)} async-done(((f32[32,8,128]{2,1,0:T(8,128)}), f32[32,8,128]{2,1,0:T(8,128)S(1)}, u32[]{:S(2)}, u32[]{:S(2)}) %all-to-all-start.5) | async-done | bytes 131104 | tf_op jit(solution)/shard_map/all_to_all | solution.py:163
  199.4 13.8 %psum.7 = f32[8,128]{1,0:T(8,128)S(1)} all-reduce(f32[8,128]{1,0:T(8,128)S(1)} %reduce_sum.162), channel_id=1, replica_groups={{0,32,64,96},{4,36,68,100},{8,40,72,104},{12,44,76,108},{16,48,80,112},..., use_global_device_ids=true, to_apply=%region_16.17 | all-reduce | flops 1024 | bytes 8192 | tf_op jit(solution)/shard_map/psum | solution.py:166
  213.2 0.6 broadcast_in_dim.17
  213.8 5.9 %all-to-all-start.6 = ((f32[32,8,128]{2,1,0:T(8,128)}), f32[32,8,128]{2,1,0:T(8,128)S(1)}, u32[]{:S(2)}, u32[]{:S(2)}) async-start(f32[32,8,128]{2,1,0:T(8,128)} %broadcast_in_dim.17), calls=%async_computation.6 | async-start | bytes 262144 | tf_op jit(solution)/shard_map/all_to_all | solution.py:168
  219.8 0.9 multiply_convert_fusion
  220.7 0.9 multiply_convert_fusion.1
  221.6 7.0 %all-to-all-done.6 = f32[32,8,128]{2,1,0:T(8,128)S(1)} async-done(((f32[32,8,128]{2,1,0:T(8,128)}), f32[32,8,128]{2,1,0:T(8,128)S(1)}, u32[]{:S(2)}, u32[]{:S(2)}) %all-to-all-start.6) | async-done | bytes 131104 | tf_op jit(solution)/shard_map/all_to_all | solution.py:168
  228.6 0.6 fusion.51
  229.2 0.6 slice_bitcast_fusion.2
  (36 shorter events, 0.3 us)
Async XLA Ops:
  7.2 59.2 %copy-start = (bf16[16,3584]{1,0:T(8,128)(2,1)S(1)}, bf16[16,3584]{1,0:T(8,128)(2,1)}, u32[]{:S(2)}) copy-start(bf16[16,3584]{1,0:T(8,128)(2,1)} %param.14) | copy-start | bytes 344068
  7.2 85.8 %all-gather.4.cloned.1.call-start = ((), (), s32[]{:S(2)}) async-start(), calls=%async_computation.7 | async-start | bytes 6623232 | tf_op jit(solution)/shard_map/all_gather | solution.py:41
  13.0 5.2 %copy-start.3 = (bf16[2,128,896]{2,1,0:T(8,128)(2,1)S(1)}, bf16[2,128,896]{2,1,0:T(8,128)(2,1)}, u32[]{:S(2)}) copy-start(bf16[2,128,896]{2,1,0:T(8,128)(2,1)} %param.10) | copy-start | bytes 1376260
  13.0 5.2 %copy-start.6 = (bf16[896,16]{0,1:T(8,128)(2,1)S(1)}, bf16[896,16]{0,1:T(8,128)(2,1)}, u32[]{:S(2)}) copy-start(bf16[896,16]{0,1:T(8,128)(2,1)} %param.13) | copy-start | bytes 86020
  13.0 53.1 %copy-start.1 = (s32[2,128,1024]{2,1,0:T(8,128)S(1)}, s32[2,128,1024]{2,1,0:T(8,128)}, u32[]{:S(2)}) copy-start(s32[2,128,1024]{2,1,0:T(8,128)} %param.18) | copy-start | bytes 3145732
  13.0 53.4 %copy-start.5 = (bf16[2,32,3584]{2,1,0:T(8,128)(2,1)S(1)}, bf16[2,32,3584]{2,1,0:T(8,128)(2,1)}, u32[]{:S(2)}) copy-start(bf16[2,32,3584]{2,1,0:T(8,128)(2,1)} %param.11) | copy-start | bytes 1376260
  13.0 54.7 %all-to-all-start = ((bf16[4,2,2,128,1024]{4,3,2,1,0:T(8,128)(2,1)}), bf16[4,2,2,128,1024]{4,3,2,1,0:T(8,128)(2,1)}, u32[]{:S(2)}, u32[]{:S(2)}) async-start(bf16[4,2,2,128,1024]{4,3,2,1,0:T(8,128)(2,1)} %broadcast_in_dim.12), calls=%async_computation | async-start | bytes 8388608 | tf_op jit(solution)/shard_map/all_to_all | solution.py:14
  97.0 17.3 %all-to-all-start.1 = ((bf16[4,2,32,1792]{3,2,1,0:T(8,128)(2,1)}), bf16[4,2,32,1792]{3,2,1,0:T(8,128)(2,1)S(1)}, u32[]{:S(2)}, u32[]{:S(2)}) async-start(bf16[4,2,32,1792]{3,2,1,0:T(8,128)(2,1)} %fusion.25), calls=%async_computation.1 | async-start | bytes 1835008 | tf_op jit(solution)/shard_map/all_to_all | solution.py:72
  101.0 17.5 %copy-start.7 = (f32[3584]{0:T(1024)S(1)}, f32[3584]{0:T(1024)}, u32[]{:S(2)}) copy-start(f32[3584]{0:T(1024)} %param.15) | copy-start | bytes 43012
  101.0 17.5 %copy-start.8 = (f32[3584]{0:T(1024)S(1)}, f32[3584]{0:T(1024)}, u32[]{:S(2)}) copy-start(f32[3584]{0:T(1024)} %param.16) | copy-start | bytes 43012
  114.2 16.6 %all-to-all-start.2 = ((bf16[4,2,32,1792]{3,2,1,0:T(8,128)(2,1)}), bf16[4,2,32,1792]{3,2,1,0:T(8,128)(2,1)}, u32[]{:S(2)}, u32[]{:S(2)}) async-start(bf16[4,2,32,1792]{3,2,1,0:T(8,128)(2,1)} %fusion.22), calls=%async_computation.2 | async-start | bytes 1835008 | tf_op jit(solution)/shard_map/all_to_all | solution.py:77
  118.4 57.1 %all-gather.6.cloned.1.call-start = ((), (), s32[]{:S(2)}) async-start(), calls=%async_computation.8 | async-start | bytes 2293760 | tf_op jit(solution)/shard_map/all_gather | solution.py:90
  135.6 29.8 %all-to-all-start.3 = ((f32[128,2,128]{2,1,0:T(2,128)}), f32[128,2,128]{2,1,0:T(2,128)S(1)}, u32[]{:S(2)}, u32[]{:S(2)}) async-start(f32[128,2,128]{2,1,0:T(2,128)} %broadcast_in_dim.14), calls=%async_computation.3 | async-start | bytes 262144 | tf_op jit(solution)/shard_map/all_to_all | solution.py:14
  168.2 15.3 %all-to-all-start.4 = ((f32[32,2,128]{2,1,0:T(2,128)}), f32[32,2,128]{2,1,0:T(2,128)S(1)}, u32[]{:S(2)}, u32[]{:S(2)}) async-start(f32[32,2,128]{2,1,0:T(2,128)} %copy.37), calls=%async_computation.4 | async-start | bytes 65536 | tf_op jit(solution)/shard_map/all_to_all | solution.py:111
  175.5 5.6 %copy-start.2 = (bf16[2,128,3584]{2,1,0:T(8,128)(2,1)S(1)}, bf16[2,128,3584]{2,1,0:T(8,128)(2,1)}, u32[]{:S(2)}) copy-start(bf16[2,128,3584]{2,1,0:T(8,128)(2,1)} %all-gather.6.cloned.1.call-done) | copy-start | bytes 5505028
  181.1 2.4 %copy-start.9 = (f32[2]{0:T(128)S(1)}, f32[2]{0:T(128)}, u32[]{:S(2)}) copy-start(f32[2]{0:T(128)} %param.19) | copy-start | bytes 28
  181.1 2.5 %copy-start.4 = (bf16[2,128,896]{2,1,0:T(8,128)(2,1)S(1)}, bf16[2,128,896]{2,1,0:T(8,128)(2,1)}, u32[]{:S(2)}) copy-start(bf16[2,128,896]{2,1,0:T(8,128)(2,1)} %param.10) | copy-start | bytes 1376260
  184.8 14.6 %all-to-all-start.5 = ((f32[32,8,128]{2,1,0:T(8,128)}), f32[32,8,128]{2,1,0:T(8,128)S(1)}, u32[]{:S(2)}, u32[]{:S(2)}) async-start(f32[32,8,128]{2,1,0:T(8,128)} %select_maximum_fusion), calls=%async_computation.5 | async-start | bytes 262144 | tf_op jit(solution)/shard_map/all_to_all | solution.py:163
  213.8 14.8 %all-to-all-start.6 = ((f32[32,8,128]{2,1,0:T(8,128)}), f32[32,8,128]{2,1,0:T(8,128)S(1)}, u32[]{:S(2)}, u32[]{:S(2)}) async-start(f32[32,8,128]{2,1,0:T(8,128)} %broadcast_in_dim.17), calls=%async_computation.6 | async-start | bytes 262144 | tf_op jit(solution)/shard_map/all_to_all | solution.py:168
Sparse Core Ops, SparseCore 0:
  10.1 82.7 all-gather.3
  134.9 33.9 all-gather.5

commit v7 on v5

--- a/solution.py
+++ b/solution.py
@@ -69,7 +69,8 @@
         "tqch,dh->tqcd", by_owner, full_weight, preferred_element_type=F32
     ).astype(BF16)
     head_terms = lax.all_to_all(head_terms, "tensor", 0, 0, tiled=True)
-    hidden = (base + jnp.sum(head_terms.astype(F32), axis=0)).astype(BF16).astype(F32)
+    head_sum = jnp.sum(head_terms.astype(F32), axis=0)
+    hidden = (base + head_sum).astype(BF16).astype(F32)
     inv_rms = lax.rsqrt(jnp.mean(hidden * hidden, axis=2) + epsilon)
     gain = norm_gain * score_weight
     dot = jnp.sum(hidden * gain, axis=2)
@@ -77,18 +78,19 @@
     slant = inv_rms * inv_rms * dot / width
     unit = inv_rms[:, :, None] * (gain - hidden * slant[:, :, None])
 
-    unit_sent, unit, scores = lax.optimization_barrier((unit.astype(BF16), unit, scores))
-    unit_all = lax.all_gather(unit_sent, "tensor", axis=1, tiled=True)
     message = jnp.concatenate(
         [scores, jnp.broadcast_to(mask_count[:, None], (queries, 128 - share))], axis=1
     )
-    message = gather_copies(message, ("cand", "tensor"))
+    message = gather_copies(message, "tensor")
     count = jnp.sum(message[:, :, share], axis=0)
-    message = message[:, :, :share].reshape(cand_count, tensor_count, queries, share)
-    own_scores = lax.dynamic_index_in_dim(message, cand_index, 0, keepdims=False)
-    own_scores = jnp.swapaxes(own_scores, 0, 1).reshape(queries, cand_rows)
-    message = message.reshape(tensor_count, near, tensor_count, queries, share)
-    col_scores = jnp.moveaxis(message, 3, 1).reshape(tensor_count, queries, cols)
+    own_scores = jnp.swapaxes(message[:, :, :share], 0, 1).reshape(queries, cand_rows)
+    own_scores, count, unit_sent = lax.optimization_barrier((own_scores, count, unit.astype(BF16)))
+    unit_all = lax.all_gather(unit_sent, "tensor", axis=1, tiled=True)
+    counts = jnp.pad(count[None], ((0, 0), (0, cand_rows - queries)))
+    message = gather_copies(jnp.concatenate([own_scores, counts], axis=0), "cand")
+    count = jnp.sum(message[:, queries, :queries], axis=0)
+    message = message[:, :queries].reshape(tensor_count, near, queries, cand_rows)
+    col_scores = jnp.swapaxes(message, 1, 2).reshape(tensor_count, queries, cols)
 
     margin = own_scores[None, :, :, None] - col_scores[:, :, None, :]
     chance = valid.astype(F32) * jax.nn.sigmoid(margin)
@@ -113,8 +115,11 @@
     context_unit = jnp.einsum(
         "qcd,dh->qch", unit_all, full_weight, preferred_element_type=F32
     ) + jnp.einsum("qcr,hr->qch", adapter_unit.astype(BF16), adapter_down, preferred_element_type=F32)
-    columns, total, adapter_unit, context_unit, count = lax.optimization_barrier(
-        (columns, total, adapter_unit, context_unit, count)
+    unit_block = lax.dynamic_slice_in_dim(
+        unit_all, tensor_index * context.shape[2], context.shape[2], 2
+    )
+    columns, total, adapter_unit, unit_block = lax.optimization_barrier(
+        (columns, total, adapter_unit, unit_block)
     )
     score_grad = (row_sum - jnp.sum(columns, axis=0)) * (loss_scale / count)[:, None]
 
@@ -124,12 +129,9 @@
     context_grad = (score_grad[:, :, None] * context_unit).astype(BF16)
     adapter_back = (score_grad[:, :, None] * adapter_unit).astype(BF16)
     down_local = jnp.einsum("qcr,qch->rh", adapter_back, context, preferred_element_type=F32)
-    block = lax.dynamic_slice_in_dim(
-        unit_all, tensor_index * context.shape[2], context.shape[2], 2
-    )
-    block = (score_grad[:, :, None] * block.astype(F32)).astype(BF16)
+    adapter_scaled = (score_grad[:, :, None] * adapter_in.astype(F32)).astype(BF16)
     up_local = ADAPTER_SCALE * jnp.einsum(
-        "qcr,qcd->rd", adapter_in, block, preferred_element_type=F32
+        "qcr,qcd->rd", adapter_scaled, unit_block, preferred_element_type=F32
     )
 
     rank = adapter_down.shape[1]

time: 233 us -> 234 us (level)
  waiting for transfers between devices: 80.3 us -> 76.6 us
  starting transfers between devices: 35.7 us -> 39.4 us
  blocking collectives: 61.6 us -> 58.7 us
    all_to_all x2, waiting for transfers between devices: 15.7 us -> 10.5 us  [on_device(): lax.all_to_all(tiles, ('dp', 'cand'), 0, 0, axis_index_groups=near_groups...]
    all_to_all x1, waiting for transfers between devices: 1.42 us -> 5.78 us  [on_device(): columns = lax.all_to_all(columns, 'cand', 0, 0, tiled=True)]
    psum x1, blocking collectives: 13.8 us -> 11 us  [on_device(): lax.psum(jnp.sum(tiles, axis=0), 'cand', axis_index_groups=far_groups)]
    all_to_all x2 -> x3, starting transfers between devices: 15.7 us -> 18.3 us  [gather_copies(): return lax.all_to_all(copies, axis, 0, 0, tiled=True)]
    all_to_all x2 -> x3, waiting for transfers between devices: 18.1 us -> 16.2 us  [gather_copies(): return lax.all_to_all(copies, axis, 0, 0, tiled=True)]
  transfers between devices with their start and end apart: 8 -> 9, of which waited for: 6 -> 7; matrix products, arithmetic and copies ran while one was open for 11% -> 13% of each run, Pallas kernels for 0% -> 0%
where the time goes in v7:
time: 234 us; the launch traced here: 233 us
  waiting for transfers between devices  76.6 us (33%)
  blocking collectives  58.7 us (25%)
  starting transfers between devices  39.4 us (17%)
  other arithmetic  18 us (8%)
  matrix products  16.3 us (7%)
  between operations  14.3 us (6%)
  local copies, waits for them, and re-layouts  9.41 us (4%)
    all_gather x1, blocking collectives, on_device(): low_all = lax.all_gather(low_terms, 'tensor', axis=0)  47.8 us
    all_to_all x1, waiting for transfers between devices, on_device(): head_terms = lax.all_to_all(head_terms, 'tensor', 0, 0, tiled=True)  23.4 us
    all_gather x1, waiting for transfers between devices, on_device(): full_weight = lax.all_gather(out_weight, 'cand', axis=0, tiled=True)  20.1 us
    all_to_all x3, starting transfers between devices, gather_copies(): return lax.all_to_all(copies, axis, 0, 0, tiled=True)  18.3 us
    all_to_all x3, waiting for transfers between devices, gather_copies(): return lax.all_to_all(copies, axis, 0, 0, tiled=True)  16.2 us
    all_to_all x2, starting transfers between devices, on_device(): lax.all_to_all(tiles, ('dp', 'cand'), 0, 0, axis_index_groups=near_groups...  11.5 us
    psum x1, blocking collectives, on_device(): lax.psum(jnp.sum(tiles, axis=0), 'cand', axis_index_groups=far_groups)  11 us
    all_to_all x2, waiting for transfers between devices, on_device(): lax.all_to_all(tiles, ('dp', 'cand'), 0, 0, axis_index_groups=near_groups...  10.5 us
  transfers between devices with their start and end apart: 9, of which 7 were waited for; matrix products, arithmetic and copies ran while one was open for 13% of the time, Pallas kernels for 0%

profile of v7, /device:TPU:1, one launch (start us, length us, event | category | flops | bytes accessed | tf_op | source)
XLA Modules:
  0.0 232.8 jit_solution(4905823786561994282)
XLA Ops:
  7.2 0.0 copy-start
  7.2 0.0 all-gather.4.cloned.1.call-start
  7.2 0.7 all-gather.4.cloned.1.call-update
  7.9 1.3 convert_bitcast_fusion
  9.2 1.1 pad_maximum_fusion
  10.4 2.6 %broadcast_in_dim.16 = bf16[4,2,2,128,1024]{4,3,2,1,0:T(8,128)(2,1)} broadcast(bf16[2,2,128,1024]{3,2,1,0:T(8,128)(2,1)S(1)} %pad_maximum_fusion), dimensions={1,2,3,4} | broadcast | bytes 5242880 | tf_op jit(solution)/shard_map/broadcast_in_dim | solution.py:13
  13.0 5.2 %all-to-all-start = ((bf16[4,2,2,128,1024]{4,3,2,1,0:T(8,128)(2,1)}), bf16[4,2,2,128,1024]{4,3,2,1,0:T(8,128)(2,1)}, u32[]{:S(2)}, u32[]{:S(2)}) async-start(bf16[4,2,2,128,1024]{4,3,2,1,0:T(8,128)(2,1)} %broadcast_in_dim.16), calls=%async_computation | async-start | bytes 8388608 | tf_op jit(solution)/shard_map/all_to_all | solution.py:14
  18.2 0.0 copy-done.3
  18.2 0.2 convolution_convert_fusion
  18.4 47.8 %all-gather = bf16[8,128,16]{1,2,0:T(8,128)(2,1)S(1)} all-gather(bf16[2,128,16]{1,2,0:T(8,128)(2,1)S(1)} %convolution_convert_fusion), channel_id=2, replica_groups=mesh['dp'=4,'cand'=32,'tensor'=4] {'tensor'}, dimensions={0}, use_global_device_ids=true | all-gather | bytes 40960 | tf_op jit(solution)/shard_map/all_gather | solution.py:46
  66.2 0.2 convert_reduce_fusion.1
  66.4 1.3 fusion.10
  67.7 0.0 all-to-all-done
  67.7 3.3 %fusion.16 = (f32[4,2,1024]{2,1,0:T(2,128)S(1)}, f32[2,128]{1,0:T(2,128)S(1)}) fusion(bf16[4,2,2,128,1024]{4,3,2,1,0:T(8,128)(2,1)} %all-to-all-done), kind=kLoop, calls=%fused_computation.19 | loop fusion | flops 5234432 | bytes 4228096 | tf_op jit(solution)/shard_map/reduce_sum | solution.py:57
  71.0 1.9 slice_bitcast_fusion.1
  72.9 20.1 %all-gather.4.cloned.1.call-done = bf16[3584,896]{1,0:T(8,128)(2,1)} async-done(((bf16[112,896]{1,0:T(8,128)(2,1)}), bf16[3584,896]{1,0:T(8,128)(2,1)}) %all-gather.4.cloned.1.call-update) | async-done | bytes 6422544 | tf_op jit(solution)/shard_map/all_gather | solution.py:41
  93.0 6.3 %fusion.7 = bf16[4,2,32,3584]{3,2,1,0:T(8,128)(2,1)} fusion(bf16[3584,896]{1,0:T(8,128)(2,1)} %all-gather.4.cloned.1.call-done, bf16[2,4,32,896]{3,2,1,0:T(8,128)(2,1)S(1)} %bitcast.94), kind=kOutput, calls=%fused_computation.10 | convolution fusion | flops 1645084672 | bytes 8716288 | tf_op jit(solution)/shard_map/tqch,dh->tqcd/dot_general | solution.py:68
  99.2 4.4 %all-to-all-start.1 = ((bf16[4,2,32,3584]{3,2,1,0:T(8,128)(2,1)}), bf16[4,2,32,3584]{3,2,1,0:T(8,128)(2,1)}, u32[]{:S(2)}, u32[]{:S(2)}) async-start(bf16[4,2,32,3584]{3,2,1,0:T(8,128)(2,1)} %fusion.7), calls=%async_computation.1 | async-start | bytes 3670016 | tf_op jit(solution)/shard_map/all_to_all | solution.py:71
  103.6 0.0 copy-done.6
  103.7 0.0 copy-done.7
  103.7 0.0 copy-start.8
  103.7 23.4 %all-to-all-done.1 = bf16[4,2,32,3584]{3,2,1,0:T(8,128)(2,1)} async-done(((bf16[4,2,32,3584]{3,2,1,0:T(8,128)(2,1)}), bf16[4,2,32,3584]{3,2,1,0:T(8,128)(2,1)}, u32[]{:S(2)}, u32[]{:S(2)}) %all-to-all-start.1) | async-done | bytes 1835040 | tf_op jit(solution)/shard_map/all_to_all | solution.py:71
  127.1 1.9 convert_reduce_fusion
  129.0 1.5 fusion.24
  130.5 0.1 broadcast_in_dim.17
  130.6 0.1 pad_maximum_fusion.2
  130.6 0.6 broadcast_in_dim.18
  131.2 3.2 %all-to-all-start.2 = ((f32[4,2,128]{2,1,0:T(2,128)}), f32[4,2,128]{2,1,0:T(2,128)S(1)}, u32[]{:S(2)}, u32[]{:S(2)}) async-start(f32[4,2,128]{2,1,0:T(2,128)} %broadcast_in_dim.18), calls=%async_computation.2 | async-start | bytes 8192 | tf_op jit(solution)/shard_map/all_to_all | solution.py:14
  134.5 0.0 all-gather.6.cloned.1.call-start
  134.5 1.0 fusion.28
  135.5 3.1 %all-to-all-done.2 = f32[4,2,128]{2,1,0:T(2,128)S(1)} async-done(((f32[4,2,128]{2,1,0:T(2,128)}), f32[4,2,128]{2,1,0:T(2,128)S(1)}, u32[]{:S(2)}, u32[]{:S(2)}) %all-to-all-start.2) | async-done | bytes 4128 | tf_op jit(solution)/shard_map/all_to_all | solution.py:14
  138.6 0.1 reshape.67
  138.7 0.2 slice_reduce_fusion.1
  138.9 0.0 all-gather.6.cloned.1.call-update
  138.9 0.6 broadcast_in_dim.20
  139.6 9.9 %all-to-all-start.3 = ((f32[32,3,128]{2,1,0:T(4,128)}), f32[32,3,128]{2,1,0:T(4,128)S(1)}, u32[]{:S(2)}, u32[]{:S(2)}) async-start(f32[32,3,128]{2,1,0:T(4,128)} %broadcast_in_dim.20), calls=%async_computation.3 | async-start | bytes 131072 | tf_op jit(solution)/shard_map/all_to_all | solution.py:14
  149.5 13.1 %all-to-all-done.3 = f32[32,3,128]{2,1,0:T(4,128)S(1)} async-done(((f32[32,3,128]{2,1,0:T(4,128)}), f32[32,3,128]{2,1,0:T(4,128)S(1)}, u32[]{:S(2)}, u32[]{:S(2)}) %all-to-all-start.3) | async-done | bytes 49184 | tf_op jit(solution)/shard_map/all_to_all | solution.py:14
  162.6 1.8 fusion.18
  164.5 0.6 copy.46
  165.2 5.1 %all-to-all-start.4 = ((f32[32,2,128]{2,1,0:T(2,128)}), f32[32,2,128]{2,1,0:T(2,128)S(1)}, u32[]{:S(2)}, u32[]{:S(2)}) async-start(f32[32,2,128]{2,1,0:T(2,128)} %copy.46), calls=%async_computation.4 | async-start | bytes 65536 | tf_op jit(solution)/shard_map/all_to_all | solution.py:104
  170.3 0.1 slice_reduce_fusion
  170.3 0.1 multiply_reduce_fusion.1
  170.4 0.1 multiply_reduce_fusion
  170.6 2.9 %fusion.11 = f32[2]{0:T(128)S(1)} fusion(bf16[4,2,128,1024]{3,2,1,0:T(8,128)(2,1)S(1)} %slice_bitcast_fusion.1, f32[4,2,1024]{2,1,0:T(2,128)S(1)} %copy.48, f32[2,128]{1,0:T(2,128)S(1)} %reshape.67), kind=kLoop, calls=%fused_computation.13 | loop fusion | flops 10485758 | bytes 2130952 | tf_op jit(solution)/shard_map/reduce_sum | solution.py:108
  173.5 2.2 convolution_multiply_fusion.1
  175.7 1.1 constant_dynamic-slice_fusion.2
  176.8 5.8 %all-to-all-done.4 = f32[32,2,128]{2,1,0:T(2,128)S(1)} async-done(((f32[32,2,128]{2,1,0:T(2,128)}), f32[32,2,128]{2,1,0:T(2,128)S(1)}, u32[]{:S(2)}, u32[]{:S(2)}) %all-to-all-start.4) | async-done | bytes 32800 | tf_op jit(solution)/shard_map/all_to_all | solution.py:104
  182.6 0.1 subtract_multiply_fusion
  182.6 0.1 constant_dynamic-slice_fusion.1
  182.7 0.2 convolution_bitcast_fusion.1
  182.9 0.2 fusion.22
  183.1 0.1 dynamic_update_slice.3
  183.3 0.7 select_maximum_fusion
  183.9 5.6 %all-to-all-start.5 = ((f32[32,8,128]{2,1,0:T(8,128)}), f32[32,8,128]{2,1,0:T(8,128)S(1)}, u32[]{:S(2)}, u32[]{:S(2)}) async-start(f32[32,8,128]{2,1,0:T(8,128)} %select_maximum_fusion), calls=%async_computation.5 | async-start | bytes 262144 | tf_op jit(solution)/shard_map/all_to_all | solution.py:156
  189.5 1.0 fusion.29
  190.5 7.7 %all-to-all-done.5 = f32[32,8,128]{2,1,0:T(8,128)S(1)} async-done(((f32[32,8,128]{2,1,0:T(8,128)}), f32[32,8,128]{2,1,0:T(8,128)S(1)}, u32[]{:S(2)}, u32[]{:S(2)}) %all-to-all-start.5) | async-done | bytes 131104 | tf_op jit(solution)/shard_map/all_to_all | solution.py:156
  198.3 11.0 %psum.7 = f32[8,128]{1,0:T(8,128)S(1)} all-reduce(f32[8,128]{1,0:T(8,128)S(1)} %reduce_sum.162), channel_id=1, replica_groups={{0,32,64,96},{4,36,68,100},{8,40,72,104},{12,44,76,108},{16,48,80,112},..., use_global_device_ids=true, to_apply=%region_16.17 | all-reduce | flops 1024 | bytes 8192 | tf_op jit(solution)/shard_map/psum | solution.py:159
  209.2 0.7 broadcast_in_dim.23
  209.9 5.9 %all-to-all-start.6 = ((f32[32,8,128]{2,1,0:T(8,128)}), f32[32,8,128]{2,1,0:T(8,128)S(1)}, u32[]{:S(2)}, u32[]{:S(2)}) async-start(f32[32,8,128]{2,1,0:T(8,128)} %broadcast_in_dim.23), calls=%async_computation.6 | async-start | bytes 262144 | tf_op jit(solution)/shard_map/all_to_all | solution.py:161
  215.9 4.9 %fusion.2 = f32[2,128,896]{2,1,0:T(8,128)S(1)} fusion(bf16[2,128,3584]{2,1,0:T(8,128)(2,1)S(1)} %copy-done.2, bf16[3584,896]{1,0:T(8,128)(2,1)} %all-gather.4.cloned.1.call-done), kind=kOutput, calls=%fused_computation.5 | convolution fusion | flops 1644167168 | bytes 9175040 | tf_op jit(solution)/shard_map/qcd,dh->qch/dot_general | solution.py:115
  220.7 1.1 fusion.21
  221.9 2.8 %all-to-all-done.6 = f32[32,8,128]{2,1,0:T(8,128)S(1)} async-done(((f32[32,8,128]{2,1,0:T(8,128)}), f32[32,8,128]{2,1,0:T(8,128)S(1)}, u32[]{:S(2)}, u32[]{:S(2)}) %all-to-all-start.6) | async-done | bytes 131104 | tf_op jit(solution)/shard_map/all_to_all | solution.py:161
  224.7 0.6 fusion.42
  225.3 0.6 slice_bitcast_fusion.2
  (36 shorter events, 0.3 us)
Async XLA Ops:
  7.2 59.2 %copy-start = (bf16[16,3584]{1,0:T(8,128)(2,1)S(1)}, bf16[16,3584]{1,0:T(8,128)(2,1)}, u32[]{:S(2)}) copy-start(bf16[16,3584]{1,0:T(8,128)(2,1)} %param.14) | copy-start | bytes 344068
  7.2 85.8 %all-gather.4.cloned.1.call-start = ((), (), s32[]{:S(2)}) async-start(), calls=%async_computation.7 | async-start | bytes 6623232 | tf_op jit(solution)/shard_map/all_gather | solution.py:41
  13.0 5.2 %copy-start.3 = (bf16[2,128,896]{2,1,0:T(8,128)(2,1)S(1)}, bf16[2,128,896]{2,1,0:T(8,128)(2,1)}, u32[]{:S(2)}) copy-start(bf16[2,128,896]{2,1,0:T(8,128)(2,1)} %param.10) | copy-start | bytes 1376260
  13.0 5.2 %copy-start.5 = (bf16[896,16]{0,1:T(8,128)(2,1)S(1)}, bf16[896,16]{0,1:T(8,128)(2,1)}, u32[]{:S(2)}) copy-start(bf16[896,16]{0,1:T(8,128)(2,1)} %param.13) | copy-start | bytes 86020
  13.0 53.1 %copy-start.1 = (s32[2,128,1024]{2,1,0:T(8,128)S(1)}, s32[2,128,1024]{2,1,0:T(8,128)}, u32[]{:S(2)}) copy-start(s32[2,128,1024]{2,1,0:T(8,128)} %param.18) | copy-start | bytes 3145732
  13.0 53.4 %copy-start.4 = (bf16[2,32,3584]{2,1,0:T(8,128)(2,1)S(1)}, bf16[2,32,3584]{2,1,0:T(8,128)(2,1)}, u32[]{:S(2)}) copy-start(bf16[2,32,3584]{2,1,0:T(8,128)(2,1)} %param.11) | copy-start | bytes 1376260
  13.0 54.7 %all-to-all-start = ((bf16[4,2,2,128,1024]{4,3,2,1,0:T(8,128)(2,1)}), bf16[4,2,2,128,1024]{4,3,2,1,0:T(8,128)(2,1)}, u32[]{:S(2)}, u32[]{:S(2)}) async-start(bf16[4,2,2,128,1024]{4,3,2,1,0:T(8,128)(2,1)} %broadcast_in_dim.16), calls=%async_computation | async-start | bytes 8388608 | tf_op jit(solution)/shard_map/all_to_all | solution.py:14
  93.0 10.7 %copy-start.6 = (f32[3584]{0:T(1024)S(1)}, f32[3584]{0:T(1024)}, u32[]{:S(2)}) copy-start(f32[3584]{0:T(1024)} %param.15) | copy-start | bytes 43012
  93.0 10.7 %copy-start.7 = (f32[3584]{0:T(1024)S(1)}, f32[3584]{0:T(1024)}, u32[]{:S(2)}) copy-start(f32[3584]{0:T(1024)} %param.16) | copy-start | bytes 43012
  99.2 27.9 %all-to-all-start.1 = ((bf16[4,2,32,3584]{3,2,1,0:T(8,128)(2,1)}), bf16[4,2,32,3584]{3,2,1,0:T(8,128)(2,1)}, u32[]{:S(2)}, u32[]{:S(2)}) async-start(bf16[4,2,32,3584]{3,2,1,0:T(8,128)(2,1)} %fusion.7), calls=%async_computation.1 | async-start | bytes 3670016 | tf_op jit(solution)/shard_map/all_to_all | solution.py:71
  103.7 66.6 %copy-start.8 = (f32[2]{0:T(128)S(1)}, f32[2]{0:T(128)}, u32[]{:S(2)}) copy-start(f32[2]{0:T(128)} %param.19) | copy-start | bytes 28
  131.2 7.4 %all-to-all-start.2 = ((f32[4,2,128]{2,1,0:T(2,128)}), f32[4,2,128]{2,1,0:T(2,128)S(1)}, u32[]{:S(2)}, u32[]{:S(2)}) async-start(f32[4,2,128]{2,1,0:T(2,128)} %broadcast_in_dim.18), calls=%async_computation.2 | async-start | bytes 8192 | tf_op jit(solution)/shard_map/all_to_all | solution.py:14
  134.5 39.0 %all-gather.6.cloned.1.call-start = ((), (), s32[]{:S(2)}) async-start(), calls=%async_computation.8 | async-start | bytes 2293760 | tf_op jit(solution)/shard_map/all_gather | solution.py:88
  139.6 23.0 %all-to-all-start.3 = ((f32[32,3,128]{2,1,0:T(4,128)}), f32[32,3,128]{2,1,0:T(4,128)S(1)}, u32[]{:S(2)}, u32[]{:S(2)}) async-start(f32[32,3,128]{2,1,0:T(4,128)} %broadcast_in_dim.20), calls=%async_computation.3 | async-start | bytes 131072 | tf_op jit(solution)/shard_map/all_to_all | solution.py:14
  165.2 17.4 %all-to-all-start.4 = ((f32[32,2,128]{2,1,0:T(2,128)}), f32[32,2,128]{2,1,0:T(2,128)S(1)}, u32[]{:S(2)}, u32[]{:S(2)}) async-start(f32[32,2,128]{2,1,0:T(2,128)} %copy.46), calls=%async_computation.4 | async-start | bytes 65536 | tf_op jit(solution)/shard_map/all_to_all | solution.py:104
  173.5 42.4 %copy-start.2 = (bf16[2,128,3584]{2,1,0:T(8,128)(2,1)S(1)}, bf16[2,128,3584]{2,1,0:T(8,128)(2,1)}, u32[]{:S(2)}) copy-start(bf16[2,128,3584]{2,1,0:T(8,128)(2,1)} %all-gather.6.cloned.1.call-done) | copy-start | bytes 5505028
  183.9 14.3 %all-to-all-start.5 = ((f32[32,8,128]{2,1,0:T(8,128)}), f32[32,8,128]{2,1,0:T(8,128)S(1)}, u32[]{:S(2)}, u32[]{:S(2)}) async-start(f32[32,8,128]{2,1,0:T(8,128)} %select_maximum_fusion), calls=%async_computation.5 | async-start | bytes 262144 | tf_op jit(solution)/shard_map/all_to_all | solution.py:156
  209.9 14.7 %all-to-all-start.6 = ((f32[32,8,128]{2,1,0:T(8,128)}), f32[32,8,128]{2,1,0:T(8,128)S(1)}, u32[]{:S(2)}, u32[]{:S(2)}) async-start(f32[32,8,128]{2,1,0:T(8,128)} %broadcast_in_dim.23), calls=%async_computation.6 | async-start | bytes 262144 | tf_op jit(solution)/shard_map/all_to_all | solution.py:161
Sparse Core Ops, SparseCore 0:
  10.1 82.7 all-gather.3
  139.0 32.8 all-gather.5

commit v8 on v5

--- a/solution.py
+++ b/solution.py
@@ -51,16 +51,16 @@
 
     mask_count = jnp.sum(pair_mask.astype(F32), axis=(1, 2))
     pairs = gather_copies(jnp.stack([pair_mask.astype(BF16), teacher]), "tensor")
-    valid = pairs[:, 0]
-    known = valid.astype(F32) * pairs[:, 1].astype(F32)
+    known = pairs[:, 0].astype(F32) * pairs[:, 1].astype(F32)
     row_known = jnp.sum(known, axis=(0, 3))
     col_known = jnp.sum(known, axis=2)
 
-    full_weight, adapter_in, base, mask_count, valid, row_known, col_known = (
+    full_weight, adapter_in, base, mask_count, pairs, row_known, col_known = (
         lax.optimization_barrier(
-            (full_weight, adapter_in, base, mask_count, valid, row_known, col_known)
+            (full_weight, adapter_in, base, mask_count, pairs, row_known, col_known)
         )
     )
+    valid = pairs[:, 0]
 
     by_owner = jnp.swapaxes(
         context.reshape(queries, tensor_count, share, context.shape[2]), 0, 1
@@ -113,8 +113,11 @@
     context_unit = jnp.einsum(
         "qcd,dh->qch", unit_all, full_weight, preferred_element_type=F32
     ) + jnp.einsum("qcr,hr->qch", adapter_unit.astype(BF16), adapter_down, preferred_element_type=F32)
-    columns, total, adapter_unit, context_unit, count = lax.optimization_barrier(
-        (columns, total, adapter_unit, context_unit, count)
+    unit_block = lax.dynamic_slice_in_dim(
+        unit_all, tensor_index * context.shape[2], context.shape[2], 2
+    )
+    columns, total, adapter_unit, context_unit, unit_block, count = lax.optimization_barrier(
+        (columns, total, adapter_unit, context_unit, unit_block, count)
     )
     score_grad = (row_sum - jnp.sum(columns, axis=0)) * (loss_scale / count)[:, None]
 
@@ -124,12 +127,9 @@
     context_grad = (score_grad[:, :, None] * context_unit).astype(BF16)
     adapter_back = (score_grad[:, :, None] * adapter_unit).astype(BF16)
     down_local = jnp.einsum("qcr,qch->rh", adapter_back, context, preferred_element_type=F32)
-    block = lax.dynamic_slice_in_dim(
-        unit_all, tensor_index * context.shape[2], context.shape[2], 2
-    )
-    block = (score_grad[:, :, None] * block.astype(F32)).astype(BF16)
+    adapter_scaled = (score_grad[:, :, None] * adapter_in.astype(F32)).astype(BF16)
     up_local = ADAPTER_SCALE * jnp.einsum(
-        "qcr,qcd->rd", adapter_in, block, preferred_element_type=F32
+        "qcr,qcd->rd", adapter_scaled, unit_block, preferred_element_type=F32
     )
 
     rank = adapter_down.shape[1]

time: 233 us -> 233 us (level)
  transfers between devices with their start and end apart: 8 -> 8, of which waited for: 6 -> 5; matrix products, arithmetic and copies ran while one was open for 11% -> 12% of each run, Pallas kernels for 0% -> 0%
where the time goes in v8:
time: 233 us; the launch traced here: 232 us
  waiting for transfers between devices  80.5 us (35%)
  blocking collectives  61.6 us (26%)
  starting transfers between devices  36.9 us (16%)
  other arithmetic  19.3 us (8%)
  between operations  14.3 us (6%)
  matrix products  13.6 us (6%)
  local copies, waits for them, and re-layouts  5.97 us (3%)
    all_gather x1, blocking collectives, on_device(): low_all = lax.all_gather(low_terms, 'tensor', axis=0)  47.8 us
    all_to_all x1, waiting for transfers between devices, on_device(): head_terms = lax.all_to_all(head_terms, 'tensor', 0, 0, tiled=True)  23.1 us
    all_gather x1, waiting for transfers between devices, on_device(): full_weight = lax.all_gather(out_weight, 'cand', axis=0, tiled=True)  22.9 us
    all_to_all x2, waiting for transfers between devices, gather_copies(): return lax.all_to_all(copies, axis, 0, 0, tiled=True)  18.1 us
    all_to_all x2, starting transfers between devices, gather_copies(): return lax.all_to_all(copies, axis, 0, 0, tiled=True)  15.8 us
    all_to_all x2, waiting for transfers between devices, on_device(): lax.all_to_all(tiles, ('dp', 'cand'), 0, 0, axis_index_groups=near_groups...  15.7 us
    psum x1, blocking collectives, on_device(): lax.psum(jnp.sum(tiles, axis=0), 'cand', axis_index_groups=far_groups)  13.8 us
    all_to_all x2, starting transfers between devices, on_device(): lax.all_to_all(tiles, ('dp', 'cand'), 0, 0, axis_index_groups=near_groups...  13.2 us
  transfers between devices with their start and end apart: 8, of which 5 were waited for; matrix products, arithmetic and copies ran while one was open for 12% of the time, Pallas kernels for 0%

profile of v8, /device:TPU:1, one launch (start us, length us, event | category | flops | bytes accessed | tf_op | source)
XLA Modules:
  0.0 232.1 jit_solution(9265086626323393322)
XLA Ops:
  7.2 0.0 copy-start
  7.2 0.0 all-gather.4.cloned.1.call-start
  7.2 0.7 all-gather.4.cloned.1.call-update
  7.9 1.3 convert_bitcast_fusion
  9.2 1.1 pad_maximum_fusion
  10.4 2.6 %broadcast_in_dim.12 = bf16[4,2,2,128,1024]{4,3,2,1,0:T(8,128)(2,1)} broadcast(bf16[2,2,128,1024]{3,2,1,0:T(8,128)(2,1)S(1)} %pad_maximum_fusion), dimensions={1,2,3,4} | broadcast | bytes 5242880 | tf_op jit(solution)/shard_map/broadcast_in_dim | solution.py:13
  13.0 5.2 %all-to-all-start = ((bf16[4,2,2,128,1024]{4,3,2,1,0:T(8,128)(2,1)}), bf16[4,2,2,128,1024]{4,3,2,1,0:T(8,128)(2,1)}, u32[]{:S(2)}, u32[]{:S(2)}) async-start(bf16[4,2,2,128,1024]{4,3,2,1,0:T(8,128)(2,1)} %broadcast_in_dim.12), calls=%async_computation | async-start | bytes 8388608 | tf_op jit(solution)/shard_map/all_to_all | solution.py:14
  18.2 0.0 copy-done.3
  18.2 0.0 copy-done.5
  18.2 0.2 convolution_convert_fusion
  18.4 47.8 %all-gather = bf16[8,128,16]{1,2,0:T(8,128)(2,1)S(1)} all-gather(bf16[2,128,16]{1,2,0:T(8,128)(2,1)S(1)} %convolution_convert_fusion), channel_id=2, replica_groups=mesh['dp'=4,'cand'=32,'tensor'=4] {'tensor'}, dimensions={0}, use_global_device_ids=true | all-gather | bytes 40960 | tf_op jit(solution)/shard_map/all_gather | solution.py:46
  66.1 0.0 copy-done.1
  66.2 0.2 convert_reduce_fusion.1
  66.4 0.0 copy-done
  66.4 0.0 copy-done.4
  66.4 0.4 fusion.10
  66.8 0.0 all-to-all-done
  66.8 3.3 %fusion.16 = (f32[4,2,1024]{2,1,0:T(2,128)S(1)}, f32[2,128]{1,0:T(2,128)S(1)}) fusion(bf16[4,2,2,128,1024]{4,3,2,1,0:T(8,128)(2,1)} %all-to-all-done), kind=kLoop, calls=%fused_computation.19 | loop fusion | flops 5234432 | bytes 4228096 | tf_op jit(solution)/shard_map/reduce_sum | solution.py:56
  70.0 22.9 %all-gather.4.cloned.1.call-done = bf16[3584,896]{1,0:T(8,128)(2,1)} async-done(((bf16[112,896]{1,0:T(8,128)(2,1)}), bf16[3584,896]{1,0:T(8,128)(2,1)}) %all-gather.4.cloned.1.call-update) | async-done | bytes 6422544 | tf_op jit(solution)/shard_map/all_gather | solution.py:41
  93.0 6.2 %fusion.7 = bf16[4,2,32,3584]{3,2,1,0:T(8,128)(2,1)} fusion(bf16[3584,896]{1,0:T(8,128)(2,1)} %all-gather.4.cloned.1.call-done, bf16[2,4,32,896]{3,2,1,0:T(8,128)(2,1)S(1)} %bitcast.86), kind=kOutput, calls=%fused_computation.10 | convolution fusion | flops 1645084672 | bytes 8716288 | tf_op jit(solution)/shard_map/tqch,dh->tqcd/dot_general | solution.py:68
  99.1 4.1 %all-to-all-start.1 = ((bf16[4,2,32,3584]{3,2,1,0:T(8,128)(2,1)}), bf16[4,2,32,3584]{3,2,1,0:T(8,128)(2,1)S(1)}, u32[]{:S(2)}, u32[]{:S(2)}) async-start(bf16[4,2,32,3584]{3,2,1,0:T(8,128)(2,1)} %fusion.7), calls=%async_computation.1 | async-start | bytes 3670016 | tf_op jit(solution)/shard_map/all_to_all | solution.py:71
  103.2 0.0 all-gather.6.cloned.1.call-start
  103.2 0.0 copy-done.6
  103.2 0.0 copy-done.7
  103.2 23.1 %all-to-all-done.1 = bf16[4,2,32,3584]{3,2,1,0:T(8,128)(2,1)S(1)} async-done(((bf16[4,2,32,3584]{3,2,1,0:T(8,128)(2,1)}), bf16[4,2,32,3584]{3,2,1,0:T(8,128)(2,1)S(1)}, u32[]{:S(2)}, u32[]{:S(2)}) %all-to-all-start.1) | async-done | bytes 1835040 | tf_op jit(solution)/shard_map/all_to_all | solution.py:71
  126.3 0.3 convert_reduce_fusion
  126.6 0.3 fusion.21
  126.9 1.0 fusion.24
  127.9 0.0 all-gather.6.cloned.1.call-update
  127.9 0.1 broadcast_in_dim.13
  128.0 0.1 pad_maximum_fusion.2
  128.0 0.7 broadcast_in_dim.14
  128.7 10.6 %all-to-all-start.2 = ((f32[128,2,128]{2,1,0:T(2,128)}), f32[128,2,128]{2,1,0:T(2,128)S(1)}, u32[]{:S(2)}, u32[]{:S(2)}) async-start(f32[128,2,128]{2,1,0:T(2,128)} %broadcast_in_dim.14), calls=%async_computation.2 | async-start | bytes 262144 | tf_op jit(solution)/shard_map/all_to_all | solution.py:14
  139.4 18.1 %all-to-all-done.2 = f32[128,2,128]{2,1,0:T(2,128)S(1)} async-done(((f32[128,2,128]{2,1,0:T(2,128)}), f32[128,2,128]{2,1,0:T(2,128)S(1)}, u32[]{:S(2)}, u32[]{:S(2)}) %all-to-all-start.2) | async-done | bytes 131104 | tf_op jit(solution)/shard_map/all_to_all | solution.py:14
  157.5 0.1 reshape.81
  157.7 0.1 sub.52
  157.8 3.4 %fusion.18 = (f32[2,128]{1,0:T(2,128)S(1)}, f32[4,2,1024]{2,1,0:T(2,128)S(1)}) fusion(f32[4,2,1024]{2,1,0:T(2,128)S(1)} %copy.37, f32[2,128]{1,0:T(2,128)S(1)} %sub.52, bf16[4,2,2,128,1024]{4,3,2,1,0:T(8,128)(2,1)} %all-to-all-done), kind=kLoop, calls=%fused_computation.26 | loop fusion | flops 8380160 | bytes 2164736 | tf_op jit(solution)/shard_map/reduce_sum | solution.py:95
  161.3 0.6 copy.35
  162.0 3.8 %all-to-all-start.3 = ((f32[32,2,128]{2,1,0:T(2,128)}), f32[32,2,128]{2,1,0:T(2,128)S(1)}, u32[]{:S(2)}, u32[]{:S(2)}) async-start(f32[32,2,128]{2,1,0:T(2,128)} %copy.35), calls=%async_computation.3 | async-start | bytes 65536 | tf_op jit(solution)/shard_map/all_to_all | solution.py:102
  165.8 0.1 multiply_reduce_fusion.1
  165.9 0.1 multiply_reduce_fusion
  166.1 0.3 slice_reduce_fusion
  166.4 4.5 %fusion.11 = f32[2]{0:T(128)S(1)} fusion(f32[4,2,1024]{2,1,0:T(2,128)S(1)} %copy.37, f32[2,128]{1,0:T(2,128)S(1)} %sub.52, bf16[4,2,2,128,1024]{4,3,2,1,0:T(8,128)(2,1)} %all-to-all-done), kind=kLoop, calls=%fused_computation.13 | loop fusion | flops 10485758 | bytes 2130952 | tf_op jit(solution)/shard_map/reduce_sum | solution.py:106
  170.8 5.6 %fusion.2 = f32[2,128,896]{2,1,0:T(8,128)S(1)} fusion(bf16[2,128,3584]{2,1,0:T(8,128)(2,1)} %all-gather.6.cloned.1.call-done, bf16[3584,896]{1,0:T(8,128)(2,1)} %all-gather.4.cloned.1.call-done), kind=kOutput, calls=%fused_computation.5 | convolution fusion | flops 1644167168 | bytes 9175040 | tf_op jit(solution)/shard_map/qcd,dh->qch/dot_general | solution.py:113
  176.4 0.0 copy-start.8
  176.5 0.6 convolution_multiply_fusion.1
  177.0 0.4 convolution_add_fusion
  177.4 0.0 all-to-all-done.3
  177.5 0.1 subtract_multiply_fusion
  177.6 0.2 convolution_bitcast_fusion.1
  177.7 0.2 fusion.20
  178.0 0.1 dynamic_update_slice.3
  178.1 0.7 select_maximum_fusion
  178.8 7.2 %all-to-all-start.4 = ((f32[32,8,128]{2,1,0:T(8,128)}), f32[32,8,128]{2,1,0:T(8,128)S(1)}, u32[]{:S(2)}, u32[]{:S(2)}) async-start(f32[32,8,128]{2,1,0:T(8,128)} %select_maximum_fusion), calls=%async_computation.4 | async-start | bytes 262144 | tf_op jit(solution)/shard_map/all_to_all | solution.py:154
  186.0 0.1 constant_dynamic-slice_fusion.1
  186.1 8.6 %all-to-all-done.4 = f32[32,8,128]{2,1,0:T(8,128)S(1)} async-done(((f32[32,8,128]{2,1,0:T(8,128)}), f32[32,8,128]{2,1,0:T(8,128)S(1)}, u32[]{:S(2)}, u32[]{:S(2)}) %all-to-all-start.4) | async-done | bytes 131104 | tf_op jit(solution)/shard_map/all_to_all | solution.py:154
  194.8 13.8 %psum.7 = f32[8,128]{1,0:T(8,128)S(1)} all-reduce(f32[8,128]{1,0:T(8,128)S(1)} %reduce_sum.152), channel_id=1, replica_groups={{0,32,64,96},{4,36,68,100},{8,40,72,104},{12,44,76,108},{16,48,80,112},..., use_global_device_ids=true, to_apply=%region_15.16 | all-reduce | flops 1024 | bytes 8192 | tf_op jit(solution)/shard_map/psum | solution.py:157
  208.6 0.6 broadcast_in_dim.17
  209.2 5.9 %all-to-all-start.5 = ((f32[32,8,128]{2,1,0:T(8,128)}), f32[32,8,128]{2,1,0:T(8,128)S(1)}, u32[]{:S(2)}, u32[]{:S(2)}) async-start(f32[32,8,128]{2,1,0:T(8,128)} %broadcast_in_dim.17), calls=%async_computation.5 | async-start | bytes 262144 | tf_op jit(solution)/shard_map/all_to_all | solution.py:159
  215.2 0.9 multiply_convert_fusion
  216.0 0.9 multiply_convert_fusion.1
  216.9 7.0 %all-to-all-done.5 = f32[32,8,128]{2,1,0:T(8,128)S(1)} async-done(((f32[32,8,128]{2,1,0:T(8,128)}), f32[32,8,128]{2,1,0:T(8,128)S(1)}, u32[]{:S(2)}, u32[]{:S(2)}) %all-to-all-start.5) | async-done | bytes 131104 | tf_op jit(solution)/shard_map/all_to_all | solution.py:159
  224.0 0.6 fusion.38
  224.6 0.6 slice_bitcast_fusion
  (29 shorter events, 0.3 us)
Async XLA Ops:
  7.2 59.2 %copy-start = (bf16[16,3584]{1,0:T(8,128)(2,1)S(1)}, bf16[16,3584]{1,0:T(8,128)(2,1)}, u32[]{:S(2)}) copy-start(bf16[16,3584]{1,0:T(8,128)(2,1)} %param.14) | copy-start | bytes 344068
  7.2 85.8 %all-gather.4.cloned.1.call-start = ((), (), s32[]{:S(2)}) async-start(), calls=%async_computation.6 | async-start | bytes 6623232 | tf_op jit(solution)/shard_map/all_gather | solution.py:41
  13.0 5.2 %copy-start.3 = (bf16[2,128,896]{2,1,0:T(8,128)(2,1)S(1)}, bf16[2,128,896]{2,1,0:T(8,128)(2,1)}, u32[]{:S(2)}) copy-start(bf16[2,128,896]{2,1,0:T(8,128)(2,1)} %param.10) | copy-start | bytes 1376260
  13.0 5.2 %copy-start.5 = (bf16[896,16]{0,1:T(8,128)(2,1)S(1)}, bf16[896,16]{0,1:T(8,128)(2,1)}, u32[]{:S(2)}) copy-start(bf16[896,16]{0,1:T(8,128)(2,1)} %param.13) | copy-start | bytes 86020
  13.0 53.1 %copy-start.1 = (s32[2,128,1024]{2,1,0:T(8,128)S(1)}, s32[2,128,1024]{2,1,0:T(8,128)}, u32[]{:S(2)}) copy-start(s32[2,128,1024]{2,1,0:T(8,128)} %param.18) | copy-start | bytes 3145732
  13.0 53.4 %copy-start.4 = (bf16[2,32,3584]{2,1,0:T(8,128)(2,1)S(1)}, bf16[2,32,3584]{2,1,0:T(8,128)(2,1)}, u32[]{:S(2)}) copy-start(bf16[2,32,3584]{2,1,0:T(8,128)(2,1)} %param.11) | copy-start | bytes 1376260
  13.0 53.8 %all-to-all-start = ((bf16[4,2,2,128,1024]{4,3,2,1,0:T(8,128)(2,1)}), bf16[4,2,2,128,1024]{4,3,2,1,0:T(8,128)(2,1)}, u32[]{:S(2)}, u32[]{:S(2)}) async-start(bf16[4,2,2,128,1024]{4,3,2,1,0:T(8,128)(2,1)} %broadcast_in_dim.12), calls=%async_computation | async-start | bytes 8388608 | tf_op jit(solution)/shard_map/all_to_all | solution.py:14
  93.0 10.2 %copy-start.6 = (f32[3584]{0:T(1024)S(1)}, f32[3584]{0:T(1024)}, u32[]{:S(2)}) copy-start(f32[3584]{0:T(1024)} %param.15) | copy-start | bytes 43012
  93.0 10.2 %copy-start.7 = (f32[3584]{0:T(1024)S(1)}, f32[3584]{0:T(1024)}, u32[]{:S(2)}) copy-start(f32[3584]{0:T(1024)} %param.16) | copy-start | bytes 43012
  99.1 27.1 %all-to-all-start.1 = ((bf16[4,2,32,3584]{3,2,1,0:T(8,128)(2,1)}), bf16[4,2,32,3584]{3,2,1,0:T(8,128)(2,1)S(1)}, u32[]{:S(2)}, u32[]{:S(2)}) async-start(bf16[4,2,32,3584]{3,2,1,0:T(8,128)(2,1)} %fusion.7), calls=%async_computation.1 | async-start | bytes 3670016 | tf_op jit(solution)/shard_map/all_to_all | solution.py:71
  103.2 67.6 %all-gather.6.cloned.1.call-start = ((), (), s32[]{:S(2)}) async-start(), calls=%async_computation.7 | async-start | bytes 2293760 | tf_op jit(solution)/shard_map/all_gather | solution.py:81
  128.7 28.8 %all-to-all-start.2 = ((f32[128,2,128]{2,1,0:T(2,128)}), f32[128,2,128]{2,1,0:T(2,128)S(1)}, u32[]{:S(2)}, u32[]{:S(2)}) async-start(f32[128,2,128]{2,1,0:T(2,128)} %broadcast_in_dim.14), calls=%async_computation.2 | async-start | bytes 262144 | tf_op jit(solution)/shard_map/all_to_all | solution.py:14
  162.0 15.5 %all-to-all-start.3 = ((f32[32,2,128]{2,1,0:T(2,128)}), f32[32,2,128]{2,1,0:T(2,128)S(1)}, u32[]{:S(2)}, u32[]{:S(2)}) async-start(f32[32,2,128]{2,1,0:T(2,128)} %copy.35), calls=%async_computation.3 | async-start | bytes 65536 | tf_op jit(solution)/shard_map/all_to_all | solution.py:102
  170.8 5.6 %copy-start.2 = (bf16[2,128,3584]{2,1,0:T(8,128)(2,1)S(1)}, bf16[2,128,3584]{2,1,0:T(8,128)(2,1)}, u32[]{:S(2)}) copy-start(bf16[2,128,3584]{2,1,0:T(8,128)(2,1)} %all-gather.6.cloned.1.call-done) | copy-start | bytes 5505028
  176.4 1.0 copy-start.8
  178.8 16.0 %all-to-all-start.4 = ((f32[32,8,128]{2,1,0:T(8,128)}), f32[32,8,128]{2,1,0:T(8,128)S(1)}, u32[]{:S(2)}, u32[]{:S(2)}) async-start(f32[32,8,128]{2,1,0:T(8,128)} %select_maximum_fusion), calls=%async_computation.4 | async-start | bytes 262144 | tf_op jit(solution)/shard_map/all_to_all | solution.py:154
  209.2 14.8 %all-to-all-start.5 = ((f32[32,8,128]{2,1,0:T(8,128)}), f32[32,8,128]{2,1,0:T(8,128)S(1)}, u32[]{:S(2)}, u32[]{:S(2)}) async-start(f32[32,8,128]{2,1,0:T(8,128)} %broadcast_in_dim.17), calls=%async_computation.5 | async-start | bytes 262144 | tf_op jit(solution)/shard_map/all_to_all | solution.py:159
Sparse Core Ops, SparseCore 0:
  10.1 82.7 all-gather.3
  128.0 32.9 all-gather.5

commit v9 on v8

--- a/solution.py
+++ b/solution.py
@@ -60,7 +60,6 @@
             (full_weight, adapter_in, base, mask_count, pairs, row_known, col_known)
         )
     )
-    valid = pairs[:, 0]
 
     by_owner = jnp.swapaxes(
         context.reshape(queries, tensor_count, share, context.shape[2]), 0, 1
@@ -76,6 +75,9 @@
     scores = dot * inv_rms
     slant = inv_rms * inv_rms * dot / width
     unit = inv_rms[:, :, None] * (gain - hidden * slant[:, :, None])
+
+    pairs, scores = lax.optimization_barrier((pairs, scores))
+    valid = lax.optimization_barrier(pairs[:, 0])
 
     unit_sent, unit, scores = lax.optimization_barrier((unit.astype(BF16), unit, scores))
     unit_all = lax.all_gather(unit_sent, "tensor", axis=1, tiled=True)

time: 233 us -> 229 us (0.983)
  other arithmetic: 19.3 us -> 16.1 us
  transfers between devices with their start and end apart: 8 -> 8, of which waited for: 5 -> 6; matrix products, arithmetic and copies ran while one was open for 12% -> 12% of each run, Pallas kernels for 0% -> 0%
where the time goes in v9:
time: 229 us
  waiting for transfers between devices  79.9 us (35%)
  blocking collectives  61.5 us (27%)
  starting transfers between devices  35.5 us (16%)
  other arithmetic  16.1 us (7%)
  between operations  14.3 us (6%)
  matrix products  13.6 us (6%)
  local copies, waits for them, and re-layouts  7.95 us (3%)
    all_gather x1, blocking collectives, on_device(): low_all = lax.all_gather(low_terms, 'tensor', axis=0)  47.8 us
    all_to_all x1, waiting for transfers between devices, on_device(): head_terms = lax.all_to_all(head_terms, 'tensor', 0, 0, tiled=True)  23.1 us
    all_gather x1, waiting for transfers between devices, on_device(): full_weight = lax.all_gather(out_weight, 'cand', axis=0, tiled=True)  22.9 us
    all_to_all x2, waiting for transfers between devices, gather_copies(): return lax.all_to_all(copies, axis, 0, 0, tiled=True)  16.1 us
    all_to_all x2, starting transfers between devices, gather_copies(): return lax.all_to_all(copies, axis, 0, 0, tiled=True)  15.8 us
    all_to_all x2, waiting for transfers between devices, on_device(): lax.all_to_all(tiles, ('dp', 'cand'), 0, 0, axis_index_groups=near_groups...  15.7 us
    psum x1, blocking collectives, on_device(): lax.psum(jnp.sum(tiles, axis=0), 'cand', axis_index_groups=far_groups)  13.8 us
    all_to_all x2, starting transfers between devices, on_device(): lax.all_to_all(tiles, ('dp', 'cand'), 0, 0, axis_index_groups=near_groups...  11.8 us
  transfers between devices with their start and end apart: 8, of which 6 were waited for; matrix products, arithmetic and copies ran while one was open for 12% of the time, Pallas kernels for 0%

profile of v9, /device:TPU:1, one launch (start us, length us, event | category | flops | bytes accessed | tf_op | source)
XLA Modules:
  0.0 228.8 jit_solution(7035708157234387548)
XLA Ops:
  7.2 0.0 copy-start
  7.2 0.0 all-gather.4.cloned.1.call-start
  7.2 0.7 all-gather.4.cloned.1.call-update
  7.9 1.3 convert_bitcast_fusion
  9.2 1.1 pad_maximum_fusion
  10.4 2.6 %broadcast_in_dim.12 = bf16[4,2,2,128,1024]{4,3,2,1,0:T(8,128)(2,1)} broadcast(bf16[2,2,128,1024]{3,2,1,0:T(8,128)(2,1)S(1)} %pad_maximum_fusion), dimensions={1,2,3,4} | broadcast | bytes 5242880 | tf_op jit(solution)/shard_map/broadcast_in_dim | solution.py:13
  13.0 5.2 %all-to-all-start = ((bf16[4,2,2,128,1024]{4,3,2,1,0:T(8,128)(2,1)}), bf16[4,2,2,128,1024]{4,3,2,1,0:T(8,128)(2,1)}, u32[]{:S(2)}, u32[]{:S(2)}) async-start(bf16[4,2,2,128,1024]{4,3,2,1,0:T(8,128)(2,1)} %broadcast_in_dim.12), calls=%async_computation | async-start | bytes 8388608 | tf_op jit(solution)/shard_map/all_to_all | solution.py:14
  18.2 0.0 copy-done.3
  18.2 0.0 copy-done.6
  18.2 0.2 convolution_convert_fusion
  18.4 47.8 %all-gather = bf16[8,128,16]{1,2,0:T(8,128)(2,1)S(1)} all-gather(bf16[2,128,16]{1,2,0:T(8,128)(2,1)S(1)} %convolution_convert_fusion), channel_id=2, replica_groups=mesh['dp'=4,'cand'=32,'tensor'=4] {'tensor'}, dimensions={0}, use_global_device_ids=true | all-gather | bytes 40960 | tf_op jit(solution)/shard_map/all_gather | solution.py:46
  66.2 0.0 copy-done.1
  66.2 0.2 convert_reduce_fusion.1
  66.4 0.0 copy-done
  66.4 0.0 copy-done.5
  66.4 0.4 fusion.10
  66.8 0.0 all-to-all-done
  66.8 3.3 %fusion.16 = (f32[4,2,1024]{2,1,0:T(2,128)S(1)}, f32[2,128]{1,0:T(2,128)S(1)}) fusion(bf16[4,2,2,128,1024]{4,3,2,1,0:T(8,128)(2,1)} %all-to-all-done), kind=kLoop, calls=%fused_computation.19 | loop fusion | flops 5234432 | bytes 4228096 | tf_op jit(solution)/shard_map/reduce_sum | solution.py:56
  70.0 22.9 %all-gather.4.cloned.1.call-done = bf16[3584,896]{1,0:T(8,128)(2,1)} async-done(((bf16[112,896]{1,0:T(8,128)(2,1)}), bf16[3584,896]{1,0:T(8,128)(2,1)}) %all-gather.4.cloned.1.call-update) | async-done | bytes 6422544 | tf_op jit(solution)/shard_map/all_gather | solution.py:41
  93.0 6.2 %fusion.7 = bf16[4,2,32,3584]{3,2,1,0:T(8,128)(2,1)} fusion(bf16[3584,896]{1,0:T(8,128)(2,1)} %all-gather.4.cloned.1.call-done, bf16[2,4,32,896]{3,2,1,0:T(8,128)(2,1)S(1)} %bitcast.80), kind=kOutput, calls=%fused_computation.10 | convolution fusion | flops 1645084672 | bytes 8716288 | tf_op jit(solution)/shard_map/tqch,dh->tqcd/dot_general | solution.py:67
  99.1 4.1 %all-to-all-start.1 = ((bf16[4,2,32,3584]{3,2,1,0:T(8,128)(2,1)}), bf16[4,2,32,3584]{3,2,1,0:T(8,128)(2,1)S(1)}, u32[]{:S(2)}, u32[]{:S(2)}) async-start(bf16[4,2,32,3584]{3,2,1,0:T(8,128)(2,1)} %fusion.7), calls=%async_computation.1 | async-start | bytes 3670016 | tf_op jit(solution)/shard_map/all_to_all | solution.py:70
  103.2 0.0 all-gather.6.cloned.1.call-start
  103.2 23.1 %all-to-all-done.1 = bf16[4,2,32,3584]{3,2,1,0:T(8,128)(2,1)S(1)} async-done(((bf16[4,2,32,3584]{3,2,1,0:T(8,128)(2,1)}), bf16[4,2,32,3584]{3,2,1,0:T(8,128)(2,1)S(1)}, u32[]{:S(2)}, u32[]{:S(2)}) %all-to-all-start.1) | async-done | bytes 1835040 | tf_op jit(solution)/shard_map/all_to_all | solution.py:70
  126.3 0.3 convert_reduce_fusion
  126.6 0.3 fusion.22
  126.9 1.0 fusion.24
  127.9 0.0 all-gather.6.cloned.1.call-update
  127.9 0.1 broadcast_in_dim.13
  128.0 0.1 pad_maximum_fusion.2
  128.0 0.7 broadcast_in_dim.14
  128.7 10.7 %all-to-all-start.2 = ((f32[128,2,128]{2,1,0:T(2,128)}), f32[128,2,128]{2,1,0:T(2,128)S(1)}, u32[]{:S(2)}, u32[]{:S(2)}) async-start(f32[128,2,128]{2,1,0:T(2,128)} %broadcast_in_dim.14), calls=%async_computation.2 | async-start | bytes 262144 | tf_op jit(solution)/shard_map/all_to_all | solution.py:14
  139.4 2.0 slice_bitcast_fusion
  141.4 16.1 %all-to-all-done.2 = f32[128,2,128]{2,1,0:T(2,128)S(1)} async-done(((f32[128,2,128]{2,1,0:T(2,128)}), f32[128,2,128]{2,1,0:T(2,128)S(1)}, u32[]{:S(2)}, u32[]{:S(2)}) %all-to-all-start.2) | async-done | bytes 131104 | tf_op jit(solution)/shard_map/all_to_all | solution.py:14
  157.5 0.1 reshape.78
  157.7 0.1 sub.49
  157.8 1.8 fusion.18
  159.7 0.6 copy.35
  160.3 3.8 %all-to-all-start.3 = ((f32[32,2,128]{2,1,0:T(2,128)}), f32[32,2,128]{2,1,0:T(2,128)S(1)}, u32[]{:S(2)}, u32[]{:S(2)}) async-start(f32[32,2,128]{2,1,0:T(2,128)} %copy.35), calls=%async_computation.3 | async-start | bytes 65536 | tf_op jit(solution)/shard_map/all_to_all | solution.py:104
  164.2 0.1 multiply_reduce_fusion.1
  164.3 0.1 multiply_reduce_fusion
  164.4 0.3 slice_reduce_fusion
  164.8 2.9 %fusion.11 = f32[2]{0:T(128)S(1)} fusion(bf16[4,2,128,1024]{3,2,1,0:T(8,128)(2,1)S(1)} %slice_bitcast_fusion, f32[4,2,1024]{2,1,0:T(2,128)S(1)} %copy.37, f32[2,128]{1,0:T(2,128)S(1)} %sub.49), kind=kLoop, calls=%fused_computation.13 | loop fusion | flops 10485758 | bytes 2130952 | tf_op jit(solution)/shard_map/reduce_sum | solution.py:108
  167.6 5.6 %fusion.2 = f32[2,128,896]{2,1,0:T(8,128)S(1)} fusion(bf16[2,128,3584]{2,1,0:T(8,128)(2,1)} %all-gather.6.cloned.1.call-done, bf16[3584,896]{1,0:T(8,128)(2,1)} %all-gather.4.cloned.1.call-done), kind=kOutput, calls=%fused_computation.5 | convolution fusion | flops 1644167168 | bytes 9175040 | tf_op jit(solution)/shard_map/qcd,dh->qch/dot_general | solution.py:115
  173.2 0.0 copy-start.9
  173.2 0.0 copy-start.4
  173.3 0.6 convolution_multiply_fusion.1
  173.8 0.4 convolution_add_fusion
  174.2 1.4 all-to-all-done.3
  175.7 0.1 subtract_multiply_fusion
  175.7 0.2 convolution_bitcast_fusion.1
  175.9 0.2 fusion.20
  176.1 0.1 dynamic_update_slice.3
  176.3 0.7 select_maximum_fusion
  177.0 5.9 %all-to-all-start.4 = ((f32[32,8,128]{2,1,0:T(8,128)}), f32[32,8,128]{2,1,0:T(8,128)S(1)}, u32[]{:S(2)}, u32[]{:S(2)}) async-start(f32[32,8,128]{2,1,0:T(8,128)} %select_maximum_fusion), calls=%async_computation.4 | async-start | bytes 262144 | tf_op jit(solution)/shard_map/all_to_all | solution.py:156
  182.8 0.1 constant_dynamic-slice_fusion.1
  182.9 8.6 %all-to-all-done.4 = f32[32,8,128]{2,1,0:T(8,128)S(1)} async-done(((f32[32,8,128]{2,1,0:T(8,128)}), f32[32,8,128]{2,1,0:T(8,128)S(1)}, u32[]{:S(2)}, u32[]{:S(2)}) %all-to-all-start.4) | async-done | bytes 131104 | tf_op jit(solution)/shard_map/all_to_all | solution.py:156
  191.6 13.8 %psum.7 = f32[8,128]{1,0:T(8,128)S(1)} all-reduce(f32[8,128]{1,0:T(8,128)S(1)} %reduce_sum.152), channel_id=1, replica_groups={{0,32,64,96},{4,36,68,100},{8,40,72,104},{12,44,76,108},{16,48,80,112},..., use_global_device_ids=true, to_apply=%region_15.16 | all-reduce | flops 1024 | bytes 8192 | tf_op jit(solution)/shard_map/psum | solution.py:159
  205.3 0.6 broadcast_in_dim.17
  206.0 5.9 %all-to-all-start.5 = ((f32[32,8,128]{2,1,0:T(8,128)}), f32[32,8,128]{2,1,0:T(8,128)S(1)}, u32[]{:S(2)}, u32[]{:S(2)}) async-start(f32[32,8,128]{2,1,0:T(8,128)} %broadcast_in_dim.17), calls=%async_computation.5 | async-start | bytes 262144 | tf_op jit(solution)/shard_map/all_to_all | solution.py:161
  211.9 0.9 multiply_convert_fusion
  212.8 0.9 multiply_convert_fusion.1
  213.7 7.0 %all-to-all-done.5 = f32[32,8,128]{2,1,0:T(8,128)S(1)} async-done(((f32[32,8,128]{2,1,0:T(8,128)}), f32[32,8,128]{2,1,0:T(8,128)S(1)}, u32[]{:S(2)}, u32[]{:S(2)}) %all-to-all-start.5) | async-done | bytes 131104 | tf_op jit(solution)/shard_map/all_to_all | solution.py:161
  220.8 0.6 fusion.38
  221.3 0.6 slice_bitcast_fusion.1
  (32 shorter events, 0.3 us)
Async XLA Ops:
  7.2 59.2 %copy-start = (bf16[16,3584]{1,0:T(8,128)(2,1)S(1)}, bf16[16,3584]{1,0:T(8,128)(2,1)}, u32[]{:S(2)}) copy-start(bf16[16,3584]{1,0:T(8,128)(2,1)} %param.14) | copy-start | bytes 344068
  7.2 85.8 %all-gather.4.cloned.1.call-start = ((), (), s32[]{:S(2)}) async-start(), calls=%async_computation.6 | async-start | bytes 6623232 | tf_op jit(solution)/shard_map/all_gather | solution.py:41
  13.0 5.2 %copy-start.3 = (bf16[2,128,896]{2,1,0:T(8,128)(2,1)S(1)}, bf16[2,128,896]{2,1,0:T(8,128)(2,1)}, u32[]{:S(2)}) copy-start(bf16[2,128,896]{2,1,0:T(8,128)(2,1)} %param.10) | copy-start | bytes 1376260
  13.0 5.2 %copy-start.6 = (bf16[896,16]{0,1:T(8,128)(2,1)S(1)}, bf16[896,16]{0,1:T(8,128)(2,1)}, u32[]{:S(2)}) copy-start(bf16[896,16]{0,1:T(8,128)(2,1)} %param.13) | copy-start | bytes 86020
  13.0 53.1 %copy-start.1 = (s32[2,128,1024]{2,1,0:T(8,128)S(1)}, s32[2,128,1024]{2,1,0:T(8,128)}, u32[]{:S(2)}) copy-start(s32[2,128,1024]{2,1,0:T(8,128)} %param.18) | copy-start | bytes 3145732
  13.0 53.4 %copy-start.5 = (bf16[2,32,3584]{2,1,0:T(8,128)(2,1)S(1)}, bf16[2,32,3584]{2,1,0:T(8,128)(2,1)}, u32[]{:S(2)}) copy-start(bf16[2,32,3584]{2,1,0:T(8,128)(2,1)} %param.11) | copy-start | bytes 1376260
  13.0 53.8 %all-to-all-start = ((bf16[4,2,2,128,1024]{4,3,2,1,0:T(8,128)(2,1)}), bf16[4,2,2,128,1024]{4,3,2,1,0:T(8,128)(2,1)}, u32[]{:S(2)}, u32[]{:S(2)}) async-start(bf16[4,2,2,128,1024]{4,3,2,1,0:T(8,128)(2,1)} %broadcast_in_dim.12), calls=%async_computation | async-start | bytes 8388608 | tf_op jit(solution)/shard_map/all_to_all | solution.py:14
  93.0 10.2 %copy-start.7 = (f32[3584]{0:T(1024)S(1)}, f32[3584]{0:T(1024)}, u32[]{:S(2)}) copy-start(f32[3584]{0:T(1024)} %param.15) | copy-start | bytes 43012
  93.0 10.2 %copy-start.8 = (f32[3584]{0:T(1024)S(1)}, f32[3584]{0:T(1024)}, u32[]{:S(2)}) copy-start(f32[3584]{0:T(1024)} %param.16) | copy-start | bytes 43012
  99.1 27.1 %all-to-all-start.1 = ((bf16[4,2,32,3584]{3,2,1,0:T(8,128)(2,1)}), bf16[4,2,32,3584]{3,2,1,0:T(8,128)(2,1)S(1)}, u32[]{:S(2)}, u32[]{:S(2)}) async-start(bf16[4,2,32,3584]{3,2,1,0:T(8,128)(2,1)} %fusion.7), calls=%async_computation.1 | async-start | bytes 3670016 | tf_op jit(solution)/shard_map/all_to_all | solution.py:70
  103.2 64.4 %all-gather.6.cloned.1.call-start = ((), (), s32[]{:S(2)}) async-start(), calls=%async_computation.7 | async-start | bytes 2293760 | tf_op jit(solution)/shard_map/all_gather | solution.py:83
  128.7 28.8 %all-to-all-start.2 = ((f32[128,2,128]{2,1,0:T(2,128)}), f32[128,2,128]{2,1,0:T(2,128)S(1)}, u32[]{:S(2)}, u32[]{:S(2)}) async-start(f32[128,2,128]{2,1,0:T(2,128)} %broadcast_in_dim.14), calls=%async_computation.2 | async-start | bytes 262144 | tf_op jit(solution)/shard_map/all_to_all | solution.py:14
  160.3 15.3 %all-to-all-start.3 = ((f32[32,2,128]{2,1,0:T(2,128)}), f32[32,2,128]{2,1,0:T(2,128)S(1)}, u32[]{:S(2)}, u32[]{:S(2)}) async-start(f32[32,2,128]{2,1,0:T(2,128)} %copy.35), calls=%async_computation.3 | async-start | bytes 65536 | tf_op jit(solution)/shard_map/all_to_all | solution.py:104
  167.6 5.6 %copy-start.2 = (bf16[2,128,3584]{2,1,0:T(8,128)(2,1)S(1)}, bf16[2,128,3584]{2,1,0:T(8,128)(2,1)}, u32[]{:S(2)}) copy-start(bf16[2,128,3584]{2,1,0:T(8,128)(2,1)} %all-gather.6.cloned.1.call-done) | copy-start | bytes 5505028
  173.2 2.4 %copy-start.9 = (f32[2]{0:T(128)S(1)}, f32[2]{0:T(128)}, u32[]{:S(2)}) copy-start(f32[2]{0:T(128)} %param.19) | copy-start | bytes 28
  173.2 2.5 %copy-start.4 = (bf16[2,128,896]{2,1,0:T(8,128)(2,1)S(1)}, bf16[2,128,896]{2,1,0:T(8,128)(2,1)}, u32[]{:S(2)}) copy-start(bf16[2,128,896]{2,1,0:T(8,128)(2,1)} %param.10) | copy-start | bytes 1376260
  177.0 14.6 %all-to-all-start.4 = ((f32[32,8,128]{2,1,0:T(8,128)}), f32[32,8,128]{2,1,0:T(8,128)S(1)}, u32[]{:S(2)}, u32[]{:S(2)}) async-start(f32[32,8,128]{2,1,0:T(8,128)} %select_maximum_fusion), calls=%async_computation.4 | async-start | bytes 262144 | tf_op jit(solution)/shard_map/all_to_all | solution.py:156
  206.0 14.8 %all-to-all-start.5 = ((f32[32,8,128]{2,1,0:T(8,128)}), f32[32,8,128]{2,1,0:T(8,128)S(1)}, u32[]{:S(2)}, u32[]{:S(2)}) async-start(f32[32,8,128]{2,1,0:T(8,128)} %broadcast_in_dim.17), calls=%async_computation.5 | async-start | bytes 262144 | tf_op jit(solution)/shard_map/all_to_all | solution.py:161
Sparse Core Ops, SparseCore 0:
  10.1 82.7 all-gather.3
  128.0 32.9 all-gather.5
